TPU v7x, 32 devices: a whole 2x2x4 slice. The times are simulated.
32 devices in a mesh: dp: 8 (over z, x), fsdp: 4 (over y, core).
Axes of the slice: x: 2, y: 2, z: 4, core: 2. Of those that a mesh axis runs over, the one named last changes fastest.
Arguments:
- patches: bfloat16 [25088, 768], P(('dp', 'fsdp')), may hold values from -6 to 6
- lengths: int32 [32, 4], P(('dp', 'fsdp')), may hold values from 0 to 784, as said below
- cotangent: bfloat16 [25088, 768], P(('dp', 'fsdp')), may hold values from -6 to 6
- owners: int32 [432], replicated, may hold values from 0 to 447, as said below
- master: float32 [448, 128, 128], P(('dp', 'fsdp')), as said below
- first_moment: float32 [448, 128, 128], P(('dp', 'fsdp')), may hold values from -3 to 3
- second_moment: float32 [448, 128, 128], P(('dp', 'fsdp')), may hold values from 0.25 to 1
- left_basis: float32 [448, 128, 128], P(('dp', 'fsdp')), as said below
- right_basis: float32 [448, 128, 128], P(('dp', 'fsdp')), as said below
- vectors: float32 [12, 768], replicated, as said below
- vector_first: float32 [12, 768], replicated, may hold values from -3 to 3
- vector_second: float32 [12, 768], replicated, may hold values from 0.25 to 1
Outputs:
- result: bfloat16 [25088, 768], P(('dp', 'fsdp'))
- grad_input: bfloat16 [25088, 768], P(('dp', 'fsdp'))
- clip_norm: float32 [], replicated
- new_master: float32 [448, 128, 128], P(('dp', 'fsdp'))
- new_first: float32 [448, 128, 128], P(('dp', 'fsdp'))
- new_second: float32 [448, 128, 128], P(('dp', 'fsdp'))
- new_vectors: float32 [12, 768], replicated
- new_vector_first: float32 [12, 768], replicated
- new_vector_second: float32 [12, 768], replicated
Inputs may be any that keep to these rules, and one draw needn't show every extreme that they name: `lengths`: row d lists the patch counts of device d's images (devices in the order of dp+fsdp): each count is 0, 196 or 784, nonzero counts come first, and their sum lies between half of 784 and 784. Distinct slot numbers: block b of the stacked weight blocks lives in slot owners[b]; slot s belongs to device s // 14 in the order of dp+fsdp; other slots hold no weight. `master`: slots named in owners hold the layer's weight blocks. `left_basis`: each slot's matrix is orthogonal. `right_basis`: each slot's matrix is orthogonal. `vectors`: rows in the order of the steps: the two norms' gains near one, the rest biases.
All inputs are finite; a program needn't handle non-finite values.
Results may differ from a plain program's by a relative error of at most 0.012.
Values may be sent and summed in bfloat16 or wider, within the bound.
No kernel may reach another device: no remote copies, remote signals or barrier semaphores. Data moves between devices by JAX's collectives and lax.ppermute only.
A program may use at most 256 MiB of HBM per device.

v0:
```python
from functools import partial
import math

import jax
import jax.numpy as jnp
from jax import lax
from jax.sharding import PartitionSpec as P

HEADS = 12
P_LARGE = 784
STEP = 2


masked_value = -1000000000.0
norm_eps = 1e-06
adam_eps = 1e-08
beta = 0.5
rate_matrix = 0.03
rate_vector = 0.05
decay_weight = 0.01
highest = lax.Precision.HIGHEST


def layout(counts, rows):
    ends = jnp.cumsum(counts)
    places = jnp.arange(rows, dtype=jnp.int32)
    image = jnp.sum((places[:, None] >= ends[None, :]).astype(jnp.int32), axis=1)
    within = places < ends[-1]
    image = jnp.where(within, image, -1)
    return (image, within.astype(jnp.float32)[:, None])


def to_blocks(matrix, size):
    height, breadth = matrix.shape
    return (
        matrix.reshape(height // size, size, breadth // size, size)
        .transpose(0, 2, 1, 3)
        .reshape(-1, size, size)
    )


def from_blocks(blocks, height, breadth, size):
    return (
        blocks.reshape(height // size, breadth // size, size, size)
        .transpose(0, 2, 1, 3)
        .reshape(height, breadth)
    )


def split_blocks(blocks, width, hidden, size):
    side = width // size
    counts = [3 * side * side, side * side, side * (hidden // size), side * (hidden // size)]
    shapes = [(width, 3 * width), (width, width), (width, hidden), (hidden, width)]
    matrices = []
    begin = 0
    for count, shape in zip(counts, shapes):
        matrices.append(from_blocks(blocks[begin : begin + count], shape[0], shape[1], size))
        begin += count
    return matrices


def norm_parts(values, gain, shift):
    center = values - jnp.mean(values, axis=-1, keepdims=True)
    factor = lax.rsqrt(jnp.mean(center * center, axis=-1, keepdims=True) + norm_eps)
    normal = center * factor
    return (normal * gain + shift, normal, factor)


def norm_back(grad, normal, factor, gain):
    inner = grad * gain
    return factor * (
        inner
        - jnp.mean(inner, axis=-1, keepdims=True)
        - normal * jnp.mean(inner * normal, axis=-1, keepdims=True)
    )


def masked_scores(query, keys, image_query, image_keys, scale):
    scores = jnp.einsum("qhd,khd->hqk", query, keys, preferred_element_type=jnp.float32) * scale
    same = image_query[:, None] == image_keys[None, :]
    return jnp.where(same[None], scores, masked_value)


def attend_forward(query, keys, values, image_query, image_keys, scale):
    scores = masked_scores(query, keys, image_query, image_keys, scale)
    peak = jnp.max(scores, axis=-1, keepdims=True)
    expd = jnp.exp(scores - peak)
    total = jnp.sum(expd, axis=-1, keepdims=True)
    probs = (expd / total).astype(jnp.bfloat16)
    mixed = jnp.einsum("hqk,khd->qhd", probs, values, preferred_element_type=jnp.float32)
    return (mixed, peak + jnp.log(total))


def attend_back(query, keys, values, image_query, image_keys, scale, logsum, grad_mixed):
    scores = masked_scores(query, keys, image_query, image_keys, scale)
    probs = jnp.exp(scores - logsum)
    probs_low = probs.astype(jnp.bfloat16)
    grad_values = jnp.einsum(
        "hqk,qhd->khd", probs_low, grad_mixed, preferred_element_type=jnp.float32
    )
    grad_probs = jnp.einsum("qhd,khd->hqk", grad_mixed, values, preferred_element_type=jnp.float32)
    grad_scores = probs * (grad_probs - jnp.sum(probs * grad_probs, axis=-1, keepdims=True))
    grad_low = grad_scores.astype(jnp.bfloat16)
    grad_query = (
        jnp.einsum("hqk,khd->qhd", grad_low, keys, preferred_element_type=jnp.float32) * scale
    )
    grad_keys = (
        jnp.einsum("hqk,qhd->khd", grad_low, query, preferred_element_type=jnp.float32) * scale
    )
    return (grad_query, grad_keys, grad_values)


def rotate(left, middle, right):
    turned = jnp.einsum("sji,sjk->sik", left, middle, precision=highest)
    return jnp.einsum("sik,skl->sil", turned, right, precision=highest)


def shards(
    patches,
    lengths,
    cotangent,
    owners,
    master,
    first_moment,
    second_moment,
    left_basis,
    right_basis,
    vectors,
    vector_first,
    vector_second,
):
    rows, width = patches.shape
    size = master.shape[1]
    hidden = 4 * width
    heads = HEADS
    depth = width // heads
    scale = depth ** (-0.5)
    image, inside = layout(lengths[0], rows)
    whole = lax.all_gather(master.astype(jnp.bfloat16), ("dp", "fsdp"), axis=0, tiled=True)
    chosen = jnp.take(whole, owners, axis=0)
    w_attn, w_out, w_up, w_down = split_blocks(chosen, width, hidden, size)
    inputs = patches.astype(jnp.float32)
    normed, normal_one, factor_one = norm_parts(inputs, vectors[0], vectors[1])
    normed_low = normed.astype(jnp.bfloat16)
    bias_attn = jnp.concatenate([vectors[2], jnp.zeros_like(vectors[2]), vectors[3]])
    project = (jnp.dot(normed_low, w_attn, preferred_element_type=jnp.float32) + bias_attn).astype(
        jnp.bfloat16
    )
    query = project[:, :width].reshape(rows, heads, depth)
    keys = project[:, width : 2 * width].reshape(rows, heads, depth)
    values = project[:, 2 * width :].reshape(rows, heads, depth)
    block = P_LARGE // 2
    number = rows // block
    query_blocks = query.reshape(number, block, heads, depth)
    image_blocks = image.reshape(number, block)

    def forward_block(item):
        return attend_forward(item[0], keys, values, item[1], image, scale)

    mixed, logsum = lax.map(forward_block, (query_blocks, image_blocks))
    mixed_low = mixed.reshape(rows, width).astype(jnp.bfloat16)
    branch = jnp.dot(mixed_low, w_out, preferred_element_type=jnp.float32) + vectors[4]
    middle = inputs + inside * branch
    second, normal_two, factor_two = norm_parts(middle, vectors[5], vectors[6])
    second_low = second.astype(jnp.bfloat16)
    pre = jnp.dot(second_low, w_up, preferred_element_type=jnp.float32) + vectors[7:11].reshape(-1)
    active, gelu_pull = jax.vjp(partial(jax.nn.gelu, approximate=False), pre)
    active_low = active.astype(jnp.bfloat16)
    output = jnp.dot(active_low, w_down, preferred_element_type=jnp.float32) + vectors[11]
    result = (middle + inside * output).astype(jnp.bfloat16)
    grad_out = cotangent.astype(jnp.float32)
    grad_two = (inside * grad_out).astype(jnp.bfloat16)
    bias_down = jnp.sum(grad_two, axis=0, dtype=jnp.float32)
    grad_down = jnp.dot(active_low.T, grad_two, preferred_element_type=jnp.float32)
    grad_active = jnp.dot(grad_two, w_down.T, preferred_element_type=jnp.float32)
    grad_pre = gelu_pull(grad_active)[0].astype(jnp.bfloat16)
    bias_up = jnp.sum(grad_pre, axis=0, dtype=jnp.float32)
    grad_up = jnp.dot(second_low.T, grad_pre, preferred_element_type=jnp.float32)
    grad_second = jnp.dot(grad_pre, w_up.T, preferred_element_type=jnp.float32)
    gain_two = jnp.sum(grad_second * normal_two, axis=0)
    shift_two = jnp.sum(grad_second, axis=0)
    grad_middle = grad_out + norm_back(grad_second, normal_two, factor_two, vectors[5])
    grad_one = (inside * grad_middle).astype(jnp.bfloat16)
    bias_out = jnp.sum(grad_one, axis=0, dtype=jnp.float32)
    grad_wout = jnp.dot(mixed_low.T, grad_one, preferred_element_type=jnp.float32)
    grad_mixed = jnp.dot(grad_one, w_out.T, preferred_element_type=jnp.float32).astype(jnp.bfloat16)
    grad_mixed = grad_mixed.reshape(number, block, heads, depth)

    def backward_block(carry, item):
        query_part, image_part, logsum_part, grad_part = item
        grad_query, grad_keys, grad_values = attend_back(
            query_part, keys, values, image_part, image, scale, logsum_part, grad_part
        )
        return ((carry[0] + grad_keys, carry[1] + grad_values), grad_query)

    empty = jnp.zeros((rows, heads, depth), jnp.float32)
    (grad_keys, grad_values), grad_query = lax.scan(
        backward_block, (empty, empty), (query_blocks, image_blocks, logsum, grad_mixed)
    )
    grad_project = jnp.concatenate(
        [
            grad_query.reshape(rows, width),
            grad_keys.reshape(rows, width),
            grad_values.reshape(rows, width),
        ],
        axis=1,
    ).astype(jnp.bfloat16)
    bias_query = jnp.sum(grad_project[:, :width], axis=0, dtype=jnp.float32)
    bias_value = jnp.sum(grad_project[:, 2 * width :], axis=0, dtype=jnp.float32)
    grad_attn = jnp.dot(normed_low.T, grad_project, preferred_element_type=jnp.float32)
    grad_normed = jnp.dot(grad_project, w_attn.T, preferred_element_type=jnp.float32)
    gain_one = jnp.sum(grad_normed * normal_one, axis=0)
    shift_one = jnp.sum(grad_normed, axis=0)
    grad_input = (grad_middle + norm_back(grad_normed, normal_one, factor_one, vectors[0])).astype(
        jnp.bfloat16
    )
    vector_grad = jnp.concatenate(
        [
            jnp.stack([gain_one, shift_one, bias_query, bias_value, bias_out, gain_two, shift_two]),
            bias_up.reshape(4, width),
            bias_down[None, :],
        ],
        axis=0,
    )
    grad_blocks = jnp.concatenate(
        [
            to_blocks(grad_attn, size),
            to_blocks(grad_wout, size),
            to_blocks(grad_up, size),
            to_blocks(grad_down, size),
        ]
    )
    slots = master.shape[0] * lax.axis_size(("dp", "fsdp"))
    buffer = jnp.zeros((slots, size, size), jnp.float32).at[owners].set(grad_blocks)
    owned = lax.psum_scatter(buffer, ("dp", "fsdp"), scatter_dimension=0, tiled=True)
    total_blocks, vector_sum = lax.psum((jnp.sum(owned * owned), vector_grad), ("dp", "fsdp"))
    clip_norm = jnp.sqrt(total_blocks + jnp.sum(vector_sum * vector_sum))
    count = owners.shape[0] * size * size + vectors.shape[0] * width
    factor = jnp.minimum(1.0, 0.5 * math.sqrt(count) / clip_norm)
    rotated = rotate(left_basis, factor * owned, right_basis)
    new_first = beta * first_moment + (1.0 - beta) * rotated
    new_second = beta * second_moment + (1.0 - beta) * rotated * rotated
    correction = 1.0 - beta**STEP
    direction = new_first / correction / (jnp.sqrt(new_second / correction) + adam_eps)
    back_turn = jnp.einsum("sij,sjk->sik", left_basis, direction, precision=highest)
    update = jnp.einsum("sik,slk->sil", back_turn, right_basis, precision=highest)
    new_master = master - rate_matrix * (update + decay_weight * master)
    vector_clip = factor * vector_sum
    new_vector_first = beta * vector_first + (1.0 - beta) * vector_clip
    new_vector_second = beta * vector_second + (1.0 - beta) * vector_clip * vector_clip
    vector_step = (
        new_vector_first / correction / (jnp.sqrt(new_vector_second / correction) + adam_eps)
    )
    new_vectors = vectors - rate_vector * vector_step
    return (
        result,
        grad_input,
        clip_norm,
        new_master,
        new_first,
        new_second,
        new_vectors,
        new_vector_first,
        new_vector_second,
    )


def solution(mesh):
    return jax.shard_map(
        shards,
        mesh=mesh,
        in_specs=(
            P(("dp", "fsdp"), None),
            P(("dp", "fsdp"), None),
            P(("dp", "fsdp"), None),
            P(),
            P(("dp", "fsdp"), None, None),
            P(("dp", "fsdp"), None, None),
            P(("dp", "fsdp"), None, None),
            P(("dp", "fsdp"), None, None),
            P(("dp", "fsdp"), None, None),
            P(),
            P(),
            P(),
        ),
        out_specs=(
            P(("dp", "fsdp"), None),
            P(("dp", "fsdp"), None),
            P(),
            P(("dp", "fsdp"), None, None),
            P(("dp", "fsdp"), None, None),
            P(("dp", "fsdp"), None, None),
            P(),
            P(),
            P(),
        ),
        check_vma=False,
    )
```

profile of v0, /device:TPU:0, one launch (start us, length us, event | category | flops | bytes accessed | tf_op | source)
XLA Modules:
  0.0 998.5 jit_solution(3734922240223502791)
XLA Ops:
  19.6 99.3 %all-gather.2.cloned.1.call-done = bf16[448,128,128]{2,1,0:T(8,128)(2,1)} async-done(((bf16[14,128,128]{2,1,0:T(8,128)(2,1)}), bf16[448,128,128]{2,1,0:T(8,128)(2,1)}) %all-gather.2.cloned.1.call-update) | async-done | bytes 14680080 | tf_op jit(solution)/shard_map/all_gather | solution.py:139
  118.9 18.4 %gather_fusion = bf16[432,128,128]{2,1,0:T(8,128)(2,1)} fusion(bf16[448,128,128]{2,1,0:T(8,128)(2,1)} %all-gather.2.cloned.1.call-done, s32[1024]{0:T(1024)S(1)} %pad_clamp_fusion), kind=kCustom, calls=%fused_computation | custom fusion | bytes 28313280 | tf_op jit(solution)/shard_map/jit(_take)/gather | solution.py:140
  137.3 7.9 broadcast_select_fusion
  150.2 11.7 %fusion.101 = (bf16[144,128,128]{2,1,0:T(8,128)(2,1)}, bf16[144,128,128]{2,1,0:T(8,128)(2,1)}) fusion(bf16[432,128,128]{2,1,0:T(8,128)(2,1)} %copy-done.5), kind=kLoop, calls=%fused_computation.176 | loop fusion | bytes 18874368 | tf_op jit(solution)/shard_map/slice | solution.py:57
  163.9 7.2 copy.104
  171.1 7.7 copy.103
  200.9 33.8 %while.27 = (s32[]{:T(128)}, bf16[2,392,12,64]{1,3,2,0:T(8,128)(2,1)}, f32[2,12,392,1]{2,1,3,0:T(8,128)}, s32[2,392]{1,0:T(2,128)S(1)}, s32[784]{0:T(1024)S(1)},...) while((s32[]{:T(128)}, ...), condition=%wide.region_7.8_spmd, body=%wide.region_4.7_spmd.sunk | while | flops 988669440 | bytes 62213196 | solution.py:160
  248.4 29.8 %multiply_convert_fusion.1 = (bf16[784,3072]{1,0:T(8,128)(2,1)}, f32[784,3072]{1,0:T(8,128)}, f32[784,3072]{1,0:T(8,128)}) fusion(f32[3072]{0:T(1024)S(1)} %copy-done.46, bf16[96,8,24,128]{3,2,1,0:T(8,128)(2,1)} %bitcast.211, f32[784,768]{1,0:T(8,128)S(1)} %get-tuple-element.326, f32[768]{0:T(1024)S(1)} %copy-done.29, f32[768]{0:T(1024)S(1)} %copy-done.28, ...), kind=kOutput, calls=%fused_computation.48 | convolution fusion | flops 3861344256 | bytes 31236224 | tf_op jit(solution)/shard_map/dot_general | solution.py:166
  278.2 11.7 %convert_reduce_fusion = (f32[3072]{0:T(1024)}, bf16[784,3072]{1,0:T(8,128)(2,1)S(1)}) fusion(f32[784,3072]{1,0:T(8,128)} %get-tuple-element.312, bf16[96,8,24,128]{3,2,1,0:T(8,128)(2,1)S(1)} %bitcast.210, bf16[784,768]{1,0:T(8,128)(2,1)S(1)} %copy-done.21, f32[784]{0:T(1024)S(1)} %copy-done.41, f32[784,3072]{1,0:T(8,128)} %get-tuple-element.327, ...), kind=kOutput, calls=%fused_computation.46 | convolution fusion | flops 3742123008 | bytes 30035008 | tf_op jit(solution)/shard_map/dot_general | solution.py:175
  289.9 7.5 multiply_reduce_fusion.1
  297.3 8.3 convolution_bitcast_fusion.1
  319.8 119.3 %while.28 = (s32[]{:T(128)}, f32[784,12,64]{0,2,1:T(8,128)}, f32[784,12,64]{0,2,1:T(8,128)}, bf16[2,392,12,64]{1,3,2,0:T(8,128)(2,1)}, bf16[2,392,12,64]{1,3,2,0...) while((s32[]{:T(128)}, f32[784,12,64]{0,2,1:T(8,128)}, ...), condition=%wide.region_14.15_spmd.clone, body=%wide.region_12.14_spmd.clone.sunk | while | flops 2397084672 | bytes 238127184 | solution.py:197
  321.3 9.8 fusion.153
  331.1 13.0 %multiply_reduce_fusion.9 = (f32[12,392]{1,0:T(8,128)S(1)}, f32[12,392,784]{2,1,0:T(8,128)}) fusion(f32[12,392,784]{2,1,0:T(8,128)} %fusion.153, f32[12,392]{1,0:T(8,128)S(1)} %dynamic-slice_bitcast_fusion.2, bf16[784,12,64]{0,2,1:T(8,128)(2,1)} %get-tuple-element.518, bf16[2,392,12,64]{1,3,2,0:T(8,128)(2,1)} %get-tuple-element.515, s32[]{:T(128)S(6)} %copy.202, ...), kind=kOutput, calls=%fused_computation.19.clone.1 | convolution fusion | flops 490490784 | bytes 34118532 | tf_op jit(solution)/shard_map/while/body/eval_jaxpr/qhd,khd->hqk/dot_general | solution.py:79
  344.1 15.1 %multiply_convert_fusion.5 = bf16[12,392,784]{2,1,0:T(8,128)(2,1)} fusion(f32[12,392,784]{2,1,0:T(8,128)} %get-tuple-element.456, f32[12,392,784]{2,1,0:T(8,128)} %fusion.153, f32[12,392]{1,0:T(8,128)S(1)} %get-tuple-element.457), kind=kLoop, calls=%fused_computation.18.clone.1 | loop fusion | flops 11063808 | bytes 36898176 | tf_op jit(solution)/shard_map/while/body/eval_jaxpr/convert_element_type | solution.py:103
  366.3 7.6 bitcast_dynamic-update-slice_fusion.8
  379.7 9.8 fusion.153
  389.5 13.0 %multiply_reduce_fusion.9 = (f32[12,392]{1,0:T(8,128)S(1)}, f32[12,392,784]{2,1,0:T(8,128)}) fusion(f32[12,392,784]{2,1,0:T(8,128)} %fusion.153, f32[12,392]{1,0:T(8,128)S(1)} %dynamic-slice_bitcast_fusion.2, bf16[784,12,64]{0,2,1:T(8,128)(2,1)} %get-tuple-element.518, bf16[2,392,12,64]{1,3,2,0:T(8,128)(2,1)} %get-tuple-element.515, s32[]{:T(128)S(6)} %copy.202, ...), kind=kOutput, calls=%fused_computation.19.clone.1 | convolution fusion | flops 490490784 | bytes 34118532 | tf_op jit(solution)/shard_map/while/body/eval_jaxpr/qhd,khd->hqk/dot_general | solution.py:79
  402.5 15.1 %multiply_convert_fusion.5 = bf16[12,392,784]{2,1,0:T(8,128)(2,1)} fusion(f32[12,392,784]{2,1,0:T(8,128)} %get-tuple-element.456, f32[12,392,784]{2,1,0:T(8,128)} %fusion.153, f32[12,392]{1,0:T(8,128)S(1)} %get-tuple-element.457), kind=kLoop, calls=%fused_computation.18.clone.1 | loop fusion | flops 11063808 | bytes 36898176 | tf_op jit(solution)/shard_map/while/body/eval_jaxpr/convert_element_type | solution.py:103
  426.7 7.6 bitcast_dynamic-update-slice_fusion.8
  458.8 7.2 fusion.67
  466.0 9.1 reshape.256
  475.2 7.8 copy.109
  483.0 7.4 convolution_bitcast_fusion
  496.2 9.7 copy.115
  509.1 19.5 %pad_maximum_fusion = f32[432,128,128]{2,1,0:T(8,128)} fusion(f32[144,128,128]{2,1,0:T(8,128)} %bitcast.199, f32[144,128,128]{2,1,0:T(8,128)} %bitcast.198, f32[36,128,128]{2,1,0:T(8,128)S(1)} %bitcast.215, f32[108,128,128]{2,1,0:T(8,128)} %bitcast.203), kind=kLoop, calls=%fused_computation.42 | loop fusion | flops 21233664 | bytes 56623104 | tf_op jit(solution)/shard_map/concatenate | solution.py:225
  528.6 13.4 %broadcast_in_dim.92 = f32[448,128,128]{2,1,0:T(8,128)} broadcast(f32[]{:T(128)} %constant.72.clone.1), dimensions={} | broadcast | bytes 29360132 | tf_op jit(solution)/shard_map/broadcast_in_dim | solution.py:234
  542.0 78.6 %scatter_fusion = f32[448,128,128]{2,1,0:T(8,128)} fusion(f32[448,128,128]{2,1,0:T(8,128)} %broadcast_in_dim.92, s32[432]{0:T(512)S(1)} %copy-done.36, f32[432,128,128]{2,1,0:T(8,128)} %pad_maximum_fusion), kind=kCustom, calls=%fused_computation.1 | custom fusion | bytes 84936384 | tf_op jit(solution)/shard_map/scatter | solution.py:234
  621.8 9.9 fusion.64
  631.9 8.9 add_convert_fusion.2
  640.8 290.0 %reduce-scatter.2.cloned.1.call-done = f32[14,128,128]{2,1,0:T(8,128)} async-done(((f32[448,128,128]{2,1,0:T(8,128)}), f32[14,128,128]{2,1,0:T(8,128)}) %reduce-scatter.2.cloned.1.call-update) | async-done | bytes 917520 | tf_op jit(solution)/shard_map/reduce_scatter | solution.py:235
  937.0 42.9 %all-reduce = (f32[]{:T(128)}, f32[12,768]{1,0:T(8,128)S(1)}) all-reduce(f32[]{:T(128)} %multiply_reduce_fusion.6, f32[12,768]{1,0:T(8,128)S(1)} %concatenate.16), channel_id=1, replica_groups=mesh['dp'=8,'fsdp'=4] {'dp','fsdp'}, use_global_device_ids=true, to_apply=%region_20.21 | all-reduce | flops 9217 | bytes 73736 | tf_op jit(solution)/shard_map/psum | solution.py:236
  (241 shorter events, 174.7 us)
Async XLA Ops:
  7.2 976.4 %copy-start = (f32[14,128,128]{2,1,0:T(8,128)S(1)}, f32[14,128,128]{2,1,0:T(8,128)}, u32[]{:S(2)}) copy-start(f32[14,128,128]{2,1,0:T(8,128)} %param.24) | copy-start | bytes 2752516
  7.2 11.0 %copy-start.47 = (s32[432]{0:T(512)S(1)}, s32[432]{0:T(512)}, u32[]{:S(2)}) copy-start(s32[432]{0:T(512)} %param.19) | copy-start | bytes 5188
  7.2 10.5 %copy-start.9 = (bf16[784,768]{1,0:T(8,128)(2,1)S(1)}, bf16[784,768]{1,0:T(8,128)(2,1)}, u32[]{:S(2)}) copy-start(bf16[784,768]{1,0:T(8,128)(2,1)} %param.16) | copy-start | bytes 3612676
  7.2 111.7 %all-gather.2.cloned.1.call-start = ((), (), s32[]{:S(2)}) async-start(), calls=%async_computation.1 | async-start | bytes 15138816 | tf_op jit(solution)/shard_map/all_gather | solution.py:139
  9.5 921.3 %reduce-scatter.2.cloned.1.call-start = ((), (), s32[]{:S(2)}) async-start(), calls=%async_computation.2 | async-start | bytes 30277632 | tf_op jit(solution)/shard_map/reduce_scatter | solution.py:235
  16.1 165.1 %copy-start.37 = (f32[768]{0:T(1024)}, f32[768]{0:T(1024)S(1)}, u32[]{:S(2)}) copy-start(f32[768]{0:T(1024)S(1)} %get-tuple-element.262) | copy-start | bytes 9220
  16.1 165.1 %copy-start.49 = (f32[768]{0:T(1024)}, f32[768]{0:T(1024)S(1)}, u32[]{:S(2)}) copy-start(f32[768]{0:T(1024)S(1)} %get-tuple-element.261) | copy-start | bytes 9220
  17.7 163.6 %copy-start.33 = (f32[784]{0:T(1024)}, f32[784]{0:T(1024)S(1)}, u32[]{:S(2)}) copy-start(f32[784]{0:T(1024)S(1)} %broadcast_multiply_fusion.5) | copy-start | bytes 9412
  19.6 161.7 %copy-start.43 = (f32[784]{0:T(1024)}, f32[784]{0:T(1024)S(1)}, u32[]{:S(2)}) copy-start(f32[784]{0:T(1024)S(1)} %add_rsqrt_fusion.1) | copy-start | bytes 9412
  150.2 11.7 %slice-start.3 = ((bf16[432,128,128]{2,1,0:T(8,128)(2,1)}), bf16[36,128,128]{2,1,0:T(8,128)(2,1)S(1)}, s32[]{:S(2)}) async-start(bf16[432,128,128]{2,1,0:T(8,128)(2,1)} %copy-done.5), calls=%async_computation.6 | async-start | bytes 2359296 | tf_op jit(solution)/shard_map/slice | solution.py:57
  234.7 13.1 %copy-start.6 = (bf16[784,12,64]{0,2,1:T(8,128)(2,1)}, bf16[784,12,64]{0,2,1:T(8,128)(2,1)S(1)}, u32[]{:S(2)}) copy-start(bf16[784,12,64]{0,2,1:T(8,128)(2,1)S(1)} %get-tuple-element.528) | copy-start | bytes 3612676
  234.7 9.7 copy-start.10
  234.7 9.7 copy-start.41
  234.7 9.7 copy-start.51
  244.4 33.7 %slice-start.5 = ((s8[4718592]{0:T(1024)(128)(4,1)}), s8[4194304]{0:T(1024)(128)(4,1)S(1)}, s32[]{:S(2)}) async-start(s8[4718592]{0:T(1024)(128)(4,1)} %bitcast.208), calls=%async_computation.8 | async-start | bytes 8388608
  247.8 57.8 %copy-start.7 = (f32[784,768]{1,0:T(8,128)}, f32[784,768]{1,0:T(8,128)S(1)}, u32[]{:S(2)}) copy-start(f32[784,768]{1,0:T(8,128)S(1)} %get-tuple-element.326) | copy-start | bytes 7225348
  248.3 29.8 %slice-start.6 = ((s8[4718592]{0:T(1024)(128)(4,1)}), s8[524288]{0:T(1024)(128)(4,1)S(1)}, s32[]{:S(2)}) async-start(s8[4718592]{0:T(1024)(128)(4,1)} %bitcast.208), calls=%async_computation.9 | async-start | bytes 1048576
  248.4 29.8 %copy-start.21 = (bf16[784,768]{1,0:T(8,128)(2,1)S(1)}, bf16[784,768]{1,0:T(8,128)(2,1)}, u32[]{:S(2)}) copy-start(bf16[784,768]{1,0:T(8,128)(2,1)} %param.18) | copy-start | bytes 3612676
  344.1 18.5 %copy-start.1 = (f32[12,392,784]{2,1,0:T(8,128)S(1)}, f32[12,392,784]{2,1,0:T(8,128)}, u32[]{:S(2)}) copy-start(f32[12,392,784]{2,1,0:T(8,128)} %get-tuple-element.456) | copy-start | bytes 44255236 | tf_op jit(solution)/shard_map/while
  362.6 11.3 %slice-start = ((s8[8429568]{0:T(1024)(128)(4,1)}), s8[40960]{0:T(1024)(128)(4,1)S(1)}, s32[]{:S(2)}) async-start(s8[8429568]{0:T(1024)(128)(4,1)} %bitcast.193), calls=%async_computation.3 | async-start | bytes 81920 | tf_op jit(solution)/shard_map/while
  362.6 11.3 %slice-start.1 = ((s8[8429568]{0:T(1024)(128)(4,1)}), s8[4194304]{0:T(1024)(128)(4,1)S(1)}, s32[]{:S(2)}) async-start(s8[8429568]{0:T(1024)(128)(4,1)} %bitcast.193), calls=%async_computation.4 | async-start | bytes 8388608 | tf_op jit(solution)/shard_map/while
  402.5 18.5 %copy-start.1 = (f32[12,392,784]{2,1,0:T(8,128)S(1)}, f32[12,392,784]{2,1,0:T(8,128)}, u32[]{:S(2)}) copy-start(f32[12,392,784]{2,1,0:T(8,128)} %get-tuple-element.456) | copy-start | bytes 44255236 | tf_op jit(solution)/shard_map/while
  421.0 13.2 %slice-start = ((s8[8429568]{0:T(1024)(128)(4,1)}), s8[40960]{0:T(1024)(128)(4,1)S(1)}, s32[]{:S(2)}) async-start(s8[8429568]{0:T(1024)(128)(4,1)} %bitcast.193), calls=%async_computation.3 | async-start | bytes 81920 | tf_op jit(solution)/shard_map/while
  421.0 13.2 %slice-start.1 = ((s8[8429568]{0:T(1024)(128)(4,1)}), s8[4194304]{0:T(1024)(128)(4,1)S(1)}, s32[]{:S(2)}) async-start(s8[8429568]{0:T(1024)(128)(4,1)} %bitcast.193), calls=%async_computation.4 | async-start | bytes 8388608 | tf_op jit(solution)/shard_map/while
  446.4 12.4 %copy-start.20 = (bf16[784,12,64]{0,2,1:T(8,128)(2,1)}, bf16[784,12,64]{0,2,1:T(8,128)(2,1)S(1)}, u32[]{:S(2)}) copy-start(bf16[784,12,64]{0,2,1:T(8,128)(2,1)S(1)} %convert.13) | copy-start | bytes 3612676
  447.1 11.7 %copy-start.19 = (bf16[784,12,64]{0,2,1:T(8,128)(2,1)}, bf16[784,12,64]{0,2,1:T(8,128)(2,1)S(1)}, u32[]{:S(2)}) copy-start(bf16[784,12,64]{0,2,1:T(8,128)(2,1)S(1)} %get-tuple-element.310) | copy-start | bytes 3612676
  475.2 7.8 copy-start.22
  528.6 13.4 %copy-start.36 = (s32[432]{0:T(512)S(1)}, s32[432]{0:T(512)}, u32[]{:S(2)}) copy-start(s32[432]{0:T(512)} %copy-done.35) | copy-start | bytes 5188
  621.7 10.1 %copy-start.8 = (f32[784,768]{1,0:T(8,128)S(1)}, f32[784,768]{1,0:T(8,128)}, u32[]{:S(2)}) copy-start(f32[784,768]{1,0:T(8,128)} %copy-done.7) | copy-start | bytes 7225348
  621.8 10.1 %copy-start.48 = (f32[768]{0:T(1024)S(1)}, f32[768]{0:T(1024)}, u32[]{:S(2)}) copy-start(f32[768]{0:T(1024)} %get-tuple-element.255) | copy-start | bytes 9220
  932.8 49.1 %copy-start.17 = (f32[14,128,128]{2,1,0:T(8,128)S(1)}, f32[14,128,128]{2,1,0:T(8,128)}, u32[]{:S(2)}) copy-start(f32[14,128,128]{2,1,0:T(8,128)} %reduce-scatter.2.cloned.1.call-done) | copy-start | bytes 2752516
  932.8 49.1 %copy-start.23 = (f32[14,128,128]{2,1,0:T(8,128)S(1)}, f32[14,128,128]{2,1,0:T(8,128)}, u32[]{:S(2)}) copy-start(f32[14,128,128]{2,1,0:T(8,128)} %param.23) | copy-start | bytes 2752516
  (39 other events, 153.4 us)
Sparse Core Ops, SparseCore 0:
  11.4 107.4 all-gather.1
  620.9 309.8 reduce-scatter.1
where the time goes:
time: 1010 us; the launch traced here: 999 us
  waiting for transfers between devices  389 us (39%)
  local copies, waits for them, and re-layouts  249 us (25%)
  matrix products  206 us (20%)
  other arithmetic  91.5 us (9%)
  blocking collectives  42.9 us (4%)
  between operations  17.6 us (2%)
    reduce_scatter x1, waiting for transfers between devices, shards(): lax.psum_scatter(buffer, ('dp', 'fsdp'), scatter_dimension=0, tiled=True)  290 us
    all_gather x1, waiting for transfers between devices, shards(): lax.all_gather(master.astype(jnp.bfloat16), ('dp', 'fsdp'), axis=0, tiled...  99.3 us
    scatter x1, local copies, waits for them, and re-layouts, shards(): jnp.zeros((slots, size, size), jnp.float32).at[owners].set(grad_blocks)  78.6 us
    psum x1, blocking collectives, shards(): lax.psum((jnp.sum(owned * owned), vector_grad), ('dp', 'fsdp'))  42.9 us
    dot_general x4, matrix products, masked_scores(): jnp.einsum('qhd,khd->hqk', query, keys, preferred_element_type=jnp.float32)  35.6 us
    convert_element_type x2, other arithmetic, attend_back(): grad_low = grad_scores.astype(jnp.bfloat16)  30.2 us
    dot_general x1, matrix products, shards(): jnp.dot(second_low, w_up, preferred_element_type=jnp.float32)  29.8 us
    unnamed x105, local copies, waits for them, and re-layouts  22.7 us
  transfers between devices with their start and end apart: 2, of which 2 were waited for; matrix products, arithmetic and copies ran while one was open for 3% of the time, Pallas kernels for 0%

commit v1 on v0

v1 whole, which is shorter than its diff:
```python
import functools
import math

import jax
import jax.numpy as jnp
from jax import lax
from jax.experimental import pallas as pl
from jax.experimental.pallas import tpu as pltpu
from jax.sharding import PartitionSpec as P

HEADS = 12
STEP = 2
AXES = ("dp", "fsdp")

norm_eps = 1e-06
adam_eps = 1e-08
beta = 0.5
rate_matrix = 0.03
rate_vector = 0.05
decay_weight = 0.01
highest = lax.Precision.HIGHEST
far = 2.0**30
low = jnp.bfloat16
wide = jnp.float32

CHUNK = 512


def ring_order(dp, fsdp):
    if (dp, fsdp) != (8, 4):
        return None
    order = []
    for turn, (x, y) in enumerate(((0, 0), (1, 0), (1, 1), (0, 1))):
        places = range(4) if turn % 2 == 0 else range(3, -1, -1)
        for z in places:
            order += [(z * 2 + x) * 4 + y * 2 + core for core in (0, 1)]
    return order


def mm(a, b, ca, cb):
    return lax.dot_general(a, b, (((ca,), (cb,)), ((), ())), preferred_element_type=wide)


def normal_parts(values):
    center = values - jnp.mean(values, axis=-1, keepdims=True)
    factor = lax.rsqrt(jnp.mean(center * center, axis=-1, keepdims=True) + norm_eps)
    return center * factor, factor


def norm_back(grad, normal, factor, gain):
    inner = grad * gain
    return factor * (
        inner
        - jnp.mean(inner, axis=-1, keepdims=True)
        - normal * jnp.mean(inner * normal, axis=-1, keepdims=True)
    )


def start_blocks(place, whole, target, sem, first, across, row0, col0, height, breadth):
    def one(index, carry):
        r = index // breadth
        c = index % breadth
        slot = place[first + (row0 + r) * across + col0 + c]
        pltpu.make_async_copy(
            whole.at[slot],
            target.at[pl.ds(pl.multiple_of(r * 128, 128), 128), pl.ds(pl.multiple_of(c * 128, 128), 128)],
            sem,
        ).start()
        return carry

    lax.fori_loop(0, height * breadth, one, 0)


def store_blocks(place, source, buffer, sem, first, across, row0, col0, height, breadth):
    def one(index, carry):
        r = index // breadth
        c = index % breadth
        slot = place[first + (row0 + r) * across + col0 + c]
        pltpu.make_async_copy(
            source.at[pl.ds(pl.multiple_of(r * 128, 128), 128), pl.ds(pl.multiple_of(c * 128, 128), 128)],
            buffer.at[slot],
            sem,
        ).start()
        return carry

    lax.fori_loop(0, height * breadth, one, 0)


def await_bytes(ref, sem):
    pltpu.make_async_copy(ref, ref, sem).wait()


TILE = 112


def tiles(rows):
    return rows // TILE


def rows_of(t):
    return pl.ds(pl.multiple_of(t * TILE, 16), TILE)


def qkv_kernel(place, whole, patches, vectors, project, weight, normed, sems):
    rows, width = patches.shape
    side = width // 128
    for part in range(3):
        start_blocks(
            place, whole, weight.at[part], sems.at[part], 0, 3 * side, 0, part * side, side, side
        )

    def norm(t, carry):
        at = rows_of(t)
        normal, _ = normal_parts(patches[at, :].astype(wide))
        normed[at, :] = (normal * vectors[0:1, :] + vectors[1:2, :]).astype(low)
        return carry

    lax.fori_loop(0, tiles(rows), norm, 0)
    for part in range(3):
        await_bytes(weight.at[part], sems.at[part])
        out = mm(normed[...], weight[part], 1, 0)
        if part == 0:
            out = out + vectors[2:3, :]
        if part == 2:
            out = out + vectors[3:4, :]
        project[:, part * width : (part + 1) * width] = out.astype(low)


def attend_kernel(query, keys, values, image_query, image_keys, mixed, probs, scores):
    rows = query.shape[0]
    lane = lax.broadcasted_iota(jnp.int32, (rows, 128), 1)
    wide_keys = jnp.concatenate([keys[...], image_keys[...]], axis=1)
    scaled = query[...] * jnp.asarray(0.125, low)
    outs = []
    for h in range(2):
        part = jnp.where(lane // 64 == h, scaled, jnp.zeros_like(scaled))
        scores[h] = mm(jnp.concatenate([part, image_query[...]], axis=1), wide_keys, 1, 1)
    for h in range(2):
        for t in range(tiles(rows)):
            at = slice(t * TILE, (t + 1) * TILE)
            s = scores[h, at, :]
            e = jnp.exp(s - jnp.max(s, axis=-1, keepdims=True))
            total = jnp.sum(e, axis=-1, keepdims=True)
            probs[h, at, :] = (e * (1.0 / total)).astype(low)
        outs.append(mm(probs[h], values[...], 1, 0))
    mixed[...] = jnp.where(lane < 64, outs[0], outs[1]).astype(low)


def feed_kernel(
    place,
    whole,
    patches,
    cotangent,
    mixed,
    inside,
    vectors,
    bias_up,
    result,
    grad_middle,
    grad_mixed,
    sums,
    sums_up,
    buffer,
    w_out,
    w_up,
    w_down,
    middle,
    normal,
    factor,
    second,
    second_t,
    grad_two,
    out_sum,
    back_sum,
    stage_up,
    stage_down,
    stage_out,
    active,
    grad_pre,
    sems,
    out_sems,
):
    step = pl.program_id(0)
    steps = pl.num_programs(0)
    rows, width = patches.shape
    side = width // 128
    hidden = 4 * width
    high = hidden // 128
    per = CHUNK // 128
    first_out = 3 * side * side
    first_up = 4 * side * side
    first_down = first_up + side * high

    def fetch(index, slot):
        start_blocks(
            place, whole, w_up.at[slot], sems.at[slot], first_up, high, 0, index * per, side, per
        )
        start_blocks(
            place, whole, w_down.at[slot], sems.at[2 + slot], first_down, side, index * per, 0, per, side
        )

    @pl.when(step == 0)
    def _():
        start_blocks(place, whole, w_out, sems.at[4], first_out, side, 0, 0, side, side)
        fetch(0, 0)
        fetch(1, 1)
        await_bytes(w_out, sems.at[4])
        out_sum[...] = mm(mixed[...], w_out[...], 1, 0)

        def norm(t, total):
            at = rows_of(t)
            keep = inside[at, :]
            mid = patches[at, :].astype(wide) + keep * (out_sum[at, :] + vectors[4:5, :])
            middle[at, :] = mid
            scaled, q = normal_parts(mid)
            normal[at, :] = scaled
            factor[at, :] = q
            second[at, :] = (scaled * vectors[5:6, :] + vectors[6:7, :]).astype(low)
            two = (keep * cotangent[at, :].astype(wide)).astype(low)
            grad_two[at, :] = two
            return total + jnp.sum(two.astype(wide), axis=0, keepdims=True)

        sums[3:4, :] = lax.fori_loop(0, tiles(rows), norm, jnp.zeros((1, width), wide))
        second_t[...] = second[...].T

    slot = lax.rem(step, 2)
    await_bytes(w_up.at[slot], sems.at[slot])
    await_bytes(w_down.at[slot], sems.at[2 + slot])
    up = w_up[slot]
    down = w_down[slot]
    pre = mm(second[...], up, 1, 0) + bias_up[0]
    grad_active = mm(grad_two[...], down, 1, 1)
    half = 0.5 * (1.0 + lax.erf(pre * math.sqrt(0.5)))
    active[...] = (pre * half).astype(low)
    slope = half + pre * (jnp.exp(-0.5 * pre * pre) * (1.0 / math.sqrt(2.0 * math.pi)))
    back = (grad_active * slope).astype(low)
    grad_pre[...] = back
    sums_up[0] = jnp.sum(back.astype(wide), axis=0, keepdims=True)
    gone = mm(active[...], down, 1, 0)
    came = mm(grad_pre[...], up, 1, 1)

    @pl.when(step == 0)
    def _():
        out_sum[...] = gone
        back_sum[...] = came

    @pl.when(step > 0)
    def _():
        out_sum[...] += gone
        back_sum[...] += came

    @pl.when(step >= 2)
    def _():
        await_bytes(stage_up.at[slot], out_sems.at[slot])
        await_bytes(stage_down.at[slot], out_sems.at[2 + slot])

    stage_up[slot] = mm(second_t[...], grad_pre[...], 1, 0).astype(low)
    stage_down[slot] = mm(active[...], grad_two[...], 0, 0).astype(low)
    store_blocks(
        place, stage_up.at[slot], buffer, out_sems.at[slot], first_up, high, 0, step * per, side, per
    )
    store_blocks(
        place, stage_down.at[slot], buffer, out_sems.at[2 + slot], first_down, side, step * per, 0, per, side
    )

    @pl.when(step + 2 < steps)
    def _():
        fetch(step + 2, slot)

    @pl.when(step == steps - 1)
    def _():
        def finish(t, total):
            at = rows_of(t)
            keep = inside[at, :]
            result[at, :] = (middle[at, :] + keep * (out_sum[at, :] + vectors[11:12, :])).astype(low)
            grad = back_sum[at, :]
            scaled = normal[at, :]
            mid = cotangent[at, :].astype(wide) + norm_back(
                grad, scaled, factor[at, :], vectors[5:6, :]
            )
            grad_middle[at, :] = mid
            one = (keep * mid).astype(low)
            second[at, :] = one
            gain, shift, bias = total
            return (
                gain + jnp.sum(grad * scaled, axis=0, keepdims=True),
                shift + jnp.sum(grad, axis=0, keepdims=True),
                bias + jnp.sum(one.astype(wide), axis=0, keepdims=True),
            )

        empty = jnp.zeros((1, width), wide)
        gain, shift, bias = lax.fori_loop(0, tiles(rows), finish, (empty, empty, empty))
        sums[0:1, :] = bias
        sums[1:2, :] = gain
        sums[2:3, :] = shift
        sums[4:8, :] = jnp.zeros((4, width), wide)
        stage_out[...] = mm(mixed[...], second[...], 0, 0).astype(low)
        store_blocks(place, stage_out, buffer, out_sems.at[4], first_out, side, 0, 0, side, side)
        grad_mixed[...] = mm(second[...], w_out[...], 1, 1).astype(low)
        for other in range(2):
            await_bytes(stage_up.at[other], out_sems.at[other])
            await_bytes(stage_down.at[other], out_sems.at[2 + other])
        await_bytes(stage_out, out_sems.at[4])


def back_kernel(
    place,
    whole,
    held,
    query,
    keys,
    values,
    probs,
    grad_mixed,
    mixed,
    patches,
    grad_middle,
    vectors,
    grad_input,
    sums,
    buffer,
    weight,
    grad_project,
    grad_low,
    normed,
    grad_sum,
    stage,
    sems,
    out_sems,
):
    del held
    step = pl.program_id(0)
    steps = pl.num_programs(0)
    rows, width = patches.shape
    side = width // 128
    scale = 0.125

    @pl.when(step == 0)
    def _():
        for part in range(3):
            start_blocks(
                place, whole, weight.at[part], sems.at[part], 0, 3 * side, 0, part * side, side, side
            )

        def norm(t, carry):
            at = rows_of(t)
            normal, _ = normal_parts(patches[at, :].astype(wide))
            normed[at, :] = (normal * vectors[0:1, :] + vectors[1:2, :]).astype(low)
            return carry

        lax.fori_loop(0, tiles(rows), norm, 0)

    lane = lax.broadcasted_iota(jnp.int32, (rows, 128), 1)
    grad = grad_mixed[...]
    grad_t = grad.T
    query_t = query[...].T
    outer = grad.astype(wide) * mixed[...].astype(wide)
    turned_query = []
    turned_keys = []
    turned_values = []
    for h in range(2):
        mine = lane // 64 == h
        delta = jnp.sum(jnp.where(mine, outer, 0.0), axis=-1, keepdims=True)
        part = jnp.where(mine, grad, jnp.zeros_like(grad))
        grad_probs = mm(part, values[...], 1, 1)
        grad_low[h] = (probs[h].astype(wide) * (grad_probs - delta)).astype(low)
        turned_query.append(mm(grad_low[h], keys[...], 1, 0))
        turned_keys.append(mm(query_t[h * 64 : (h + 1) * 64, :], grad_low[h], 1, 0))
        turned_values.append(mm(grad_t[h * 64 : (h + 1) * 64, :], probs[h], 1, 0))
    grad_query = jnp.where(lane < 64, turned_query[0], turned_query[1]) * scale
    grad_keys = (jnp.concatenate(turned_keys, axis=0) * scale).T
    grad_values = jnp.concatenate(turned_values, axis=0).T
    at = pl.multiple_of(step * 128, 128)
    for part, value in enumerate((grad_query, grad_keys, grad_values)):
        grad_project[part, :, pl.ds(at, 128)] = value.astype(low)

    @pl.when(step == steps - 1)
    def _():
        for part in range(3):
            if part == 2:
                await_bytes(stage.at[0], out_sems.at[0])
            stage[part % 2] = mm(normed[...], grad_project[part], 0, 0).astype(low)
            store_blocks(
                place, stage.at[part % 2], buffer, out_sems.at[part % 2], 0, 3 * side, 0, part * side, side, side
            )
        for part in range(3):
            await_bytes(weight.at[part], sems.at[part])
        total = mm(grad_project[0], weight[0], 1, 1)
        total = total + mm(grad_project[1], weight[1], 1, 1)
        grad_sum[...] = total + mm(grad_project[2], weight[2], 1, 1)

        def finish(t, carry):
            at = rows_of(t)
            grad = grad_sum[at, :]
            normal, factor = normal_parts(patches[at, :].astype(wide))
            back = norm_back(grad, normal, factor, vectors[0:1, :])
            grad_input[at, :] = (grad_middle[at, :] + back).astype(low)
            gain, shift, bias_query, bias_value = carry
            return (
                gain + jnp.sum(grad * normal, axis=0, keepdims=True),
                shift + jnp.sum(grad, axis=0, keepdims=True),
                bias_query + jnp.sum(grad_project[0, at, :].astype(wide), axis=0, keepdims=True),
                bias_value + jnp.sum(grad_project[2, at, :].astype(wide), axis=0, keepdims=True),
            )

        empty = jnp.zeros((1, width), wide)
        found = lax.fori_loop(0, tiles(rows), finish, (empty, empty, empty, empty))
        for row in range(4):
            sums[row : row + 1, :] = found[row]
        sums[4:8, :] = jnp.zeros((4, width), wide)
        await_bytes(stage.at[1], out_sems.at[1])
        await_bytes(stage.at[0], out_sems.at[0])


VMEM_LIMIT = 60 * 1024 * 1024


def params(count=1):
    return pltpu.CompilerParams(
        dimension_semantics=("arbitrary",) * count, vmem_limit_bytes=VMEM_LIMIT
    )


def whole_spec():
    return pl.BlockSpec(memory_space=pl.ANY)


def full(shape):
    return pl.BlockSpec(shape, lambda *_: (0,) * len(shape))


def layer(whole, place, patches, cotangent, counts, vectors, slots):
    rows, width = patches.shape
    hidden = 4 * width
    side = width // 128
    pairs = width // 128
    shape = jax.ShapeDtypeStruct
    ends = jnp.cumsum(counts)
    places = jnp.arange(rows, dtype=jnp.int32)[:, None]
    image = jnp.sum((places >= ends[None, :]).astype(jnp.int32), axis=1, keepdims=True)
    within = places < ends[-1]
    image = jnp.where(within, image, 4)
    inside = within.astype(wide)
    lanes = jnp.arange(128, dtype=jnp.int32)[None, :]
    image_keys = (lanes == image).astype(low)
    image_query = jnp.where((lanes != image) & (lanes < 5), -far, 0.0).astype(low)

    project = pl.pallas_call(
        qkv_kernel,
        grid_spec=pltpu.PrefetchScalarGridSpec(
            num_scalar_prefetch=1,
            grid=(1,),
            in_specs=[whole_spec(), full((rows, width)), full((12, width))],
            out_specs=full((rows, 3 * width)),
            scratch_shapes=[
                pltpu.VMEM((3, width, width), low),
                pltpu.VMEM((rows, width), low),
                pltpu.SemaphoreType.DMA((3,)),
            ],
        ),
        out_shape=shape((rows, 3 * width), low),
        compiler_params=params(),
        name="qkv",
    )(place, whole, patches, vectors)

    def column(offset):
        return pl.BlockSpec((rows, 128), lambda j, *_: (0, j + offset))

    mixed, probs = pl.pallas_call(
        attend_kernel,
        grid=(pairs,),
        in_specs=[
            column(0),
            column(pairs),
            column(2 * pairs),
            full((rows, 128)),
            full((rows, 128)),
        ],
        out_specs=[column(0), pl.BlockSpec((2, rows, rows), lambda j: (j, 0, 0))],
        out_shape=[shape((rows, width), low), shape((HEADS, rows, rows), low)],
        scratch_shapes=[pltpu.VMEM((2, rows, rows), wide)],
        compiler_params=params(),
        name="attend",
    )(project, project, project, image_query, image_keys)

    steps = hidden // CHUNK
    result, grad_middle, grad_mixed, sums_two, sums_up, buffer = pl.pallas_call(
        feed_kernel,
        grid_spec=pltpu.PrefetchScalarGridSpec(
            num_scalar_prefetch=1,
            grid=(steps,),
            in_specs=[
                whole_spec(),
                full((rows, width)),
                full((rows, width)),
                full((rows, width)),
                full((rows, 1)),
                full((12, width)),
                pl.BlockSpec((1, 1, CHUNK), lambda c, *_: (c, 0, 0)),
            ],
            out_specs=[
                full((rows, width)),
                full((rows, width)),
                full((rows, width)),
                full((8, width)),
                pl.BlockSpec((1, 1, CHUNK), lambda c, *_: (c, 0, 0)),
                whole_spec(),
            ],
            scratch_shapes=[
                pltpu.VMEM((width, width), low),
                pltpu.VMEM((2, width, CHUNK), low),
                pltpu.VMEM((2, CHUNK, width), low),
                pltpu.VMEM((rows, width), wide),
                pltpu.VMEM((rows, width), wide),
                pltpu.VMEM((rows, 1), wide),
                pltpu.VMEM((rows, width), low),
                pltpu.VMEM((width, rows), low),
                pltpu.VMEM((rows, width), low),
                pltpu.VMEM((rows, width), wide),
                pltpu.VMEM((rows, width), wide),
                pltpu.VMEM((2, width, CHUNK), low),
                pltpu.VMEM((2, CHUNK, width), low),
                pltpu.VMEM((width, width), low),
                pltpu.VMEM((rows, CHUNK), low),
                pltpu.VMEM((rows, CHUNK), low),
                pltpu.SemaphoreType.DMA((5,)),
                pltpu.SemaphoreType.DMA((5,)),
            ],
        ),
        out_shape=[
            shape((rows, width), low),
            shape((rows, width), wide),
            shape((rows, width), low),
            shape((8, width), wide),
            shape((steps, 1, CHUNK), wide),
            shape((slots, 128, 128), low),
        ],
        compiler_params=params(),
        name="feed",
    )(
        place,
        whole,
        patches,
        cotangent,
        mixed,
        inside,
        vectors,
        vectors[7:11].reshape(steps, 1, CHUNK),
    )

    grad_input, sums_one, buffer = pl.pallas_call(
        back_kernel,
        grid_spec=pltpu.PrefetchScalarGridSpec(
            num_scalar_prefetch=1,
            grid=(pairs,),
            in_specs=[
                whole_spec(),
                whole_spec(),
                column(0),
                column(pairs),
                column(2 * pairs),
                pl.BlockSpec((2, rows, rows), lambda j, *_: (j, 0, 0)),
                column(0),
                column(0),
                full((rows, width)),
                full((rows, width)),
                full((12, width)),
            ],
            out_specs=[full((rows, width)), full((8, width)), whole_spec()],
            scratch_shapes=[
                pltpu.VMEM((3, width, width), low),
                pltpu.VMEM((3, rows, width), low),
                pltpu.VMEM((2, rows, rows), low),
                pltpu.VMEM((rows, width), low),
                pltpu.VMEM((rows, width), wide),
                pltpu.VMEM((2, width, width), low),
                pltpu.SemaphoreType.DMA((3,)),
                pltpu.SemaphoreType.DMA((2,)),
            ],
        ),
        out_shape=[
            shape((rows, width), low),
            shape((8, width), wide),
            shape((slots, 128, 128), low),
        ],
        input_output_aliases={2: 2},
        compiler_params=params(),
        name="back",
    )(
        place,
        whole,
        buffer,
        project,
        project,
        project,
        probs,
        grad_mixed,
        mixed,
        patches,
        grad_middle,
        vectors,
    )
    del side
    vector_grad = jnp.concatenate(
        [sums_one[0:4], sums_two[0:3], sums_up.reshape(4, width), sums_two[3:4]], axis=0
    )
    return result, grad_input, vector_grad, buffer


def shards(
    sizes,
    patches,
    lengths,
    cotangent,
    owners,
    master,
    first_moment,
    second_moment,
    left_basis,
    right_basis,
    vectors,
    vector_first,
    vector_second,
):
    dp, fsdp = sizes
    devices = dp * fsdp
    width = patches.shape[1]
    held, size = master.shape[0], master.shape[1]
    slots = held * devices
    order = ring_order(dp, fsdp)
    me = lax.axis_index(AXES)
    if order is None:
        groups = None
        place = owners
    else:
        groups = [order]
        rank = [0] * devices
        for spot, device in enumerate(order):
            rank[device] = spot
        device = owners // held
        spot = jnp.sum(
            jnp.where(
                device[:, None] == jnp.arange(devices, dtype=jnp.int32)[None, :],
                jnp.array(rank, jnp.int32)[None, :],
                0,
            ),
            axis=1,
        )
        place = spot * held + owners % held
    mine = me * held + jnp.arange(held, dtype=jnp.int32)
    named = jnp.any(mine[:, None] == owners[None, :], axis=1)

    whole = lax.all_gather(
        master.astype(low), AXES, axis=0, tiled=True, axis_index_groups=groups
    )
    result, grad_input, vector_grad, buffer = layer(
        whole, place, patches, cotangent, lengths[0], vectors, slots
    )

    def everywhere(value):
        step = 1
        while step < devices:
            value = value + lax.ppermute(value, AXES, [(d, d ^ step) for d in range(devices)])
            step *= 2
        return value

    vector_sum = everywhere(vector_grad)
    owned = lax.psum_scatter(
        buffer, AXES, scatter_dimension=0, tiled=True, axis_index_groups=groups
    )
    owned = jnp.where(named[:, None, None], owned.astype(wide), 0.0)
    total_blocks = everywhere(jnp.broadcast_to(jnp.sum(owned * owned), (8, 128)))[0, 0]
    clip_norm = jnp.sqrt(total_blocks + jnp.sum(vector_sum * vector_sum))
    count = owners.shape[0] * size * size + vectors.shape[0] * width
    factor = jnp.minimum(1.0, 0.5 * math.sqrt(count) / clip_norm)
    turned = jnp.einsum("sji,sjk->sik", left_basis, owned, precision=highest)
    rotated = factor * jnp.einsum("sik,skl->sil", turned, right_basis, precision=highest)
    new_first = beta * first_moment + (1.0 - beta) * rotated
    new_second = beta * second_moment + (1.0 - beta) * rotated * rotated
    correction = 1.0 - beta**STEP
    direction = new_first / correction / (jnp.sqrt(new_second / correction) + adam_eps)
    back_turn = jnp.einsum("sij,sjk->sik", left_basis, direction, precision=highest)
    update = jnp.einsum("sik,slk->sil", back_turn, right_basis, precision=highest)
    new_master = master - rate_matrix * (update + decay_weight * master)
    vector_clip = factor * vector_sum
    new_vector_first = beta * vector_first + (1.0 - beta) * vector_clip
    new_vector_second = beta * vector_second + (1.0 - beta) * vector_clip * vector_clip
    vector_step = (
        new_vector_first / correction / (jnp.sqrt(new_vector_second / correction) + adam_eps)
    )
    new_vectors = vectors - rate_vector * vector_step
    return (
        result,
        grad_input,
        clip_norm,
        new_master,
        new_first,
        new_second,
        new_vectors,
        new_vector_first,
        new_vector_second,
    )


def solution(mesh):
    sizes = (mesh.shape["dp"], mesh.shape["fsdp"])
    rows = P(AXES, None)
    blocks = P(AXES, None, None)
    return jax.shard_map(
        functools.partial(shards, sizes),
        mesh=mesh,
        in_specs=(rows, rows, rows, P(), blocks, blocks, blocks, blocks, blocks, P(), P(), P()),
        out_specs=(rows, rows, P(), blocks, blocks, blocks, P(), P(), P()),
        check_vma=False,
    )
```

time: 1010 us -> 374 us (0.37); the launches traced: 999 us -> 373 us
  local copies, waits for them, and re-layouts: 249 us -> 4.27 us
  waiting for transfers between devices: 389 us -> 185 us
  matrix products: 206 us -> 9.77 us
  Pallas kernels: 0 us -> 130 us
  other arithmetic: 91.5 us -> 14.3 us
  blocking collectives: 42.9 us -> 0 us
  starting transfers between devices: 0.08 us -> 13 us
    dot_general x28 -> x2, matrix products: 202 us -> 5.35 us  [the longest x1 2.69 us: shards(): jnp.einsum('sik,skl->sil', turned, right_basis, precision=highest)]
    reduce_scatter x1, waiting for transfers between devices: 290 us -> 98.6 us  [shards(): lax.psum_scatter(buffer, AXES, scatter_dimension=0, tiled=True, axis_inde...]
    pallas_call x0 -> x4, Pallas kernels: none -> 130 us  [the longest x1 58.3 us: layer(): pl.pallas_call(feed_kernel, grid_spec=pltpu.PrefetchScalarGridSpec(num_sc...]
    scatter x1 -> x0, local copies, waits for them, and re-layouts: 78.6 us -> none  [shards(): jnp.zeros((slots, size, size), jnp.float32).at[owners].set(grad_blocks)]
    psum x1 -> x0, blocking collectives: 42.9 us -> none  [shards(): lax.psum((jnp.sum(owned * owned), vector_grad), ('dp', 'fsdp'))]
    reshape x9 -> x2, local copies, waits for them, and re-layouts: 38.9 us -> 0.63 us  [the longest x1 0.62 us: layer(): vectors[7:11].reshape(steps, 1, CHUNK)]
    convert_element_type x5 -> x4, other arithmetic: 37.8 us -> 5.24 us  [the longest x1 2.1 us: shards(): master.astype(low)]
    unnamed x105 -> x24, local copies, waits for them, and re-layouts: 22.7 us -> 1.08 us
  transfers between devices with their start and end apart: 2 -> 12, of which waited for: 2 -> 8; matrix products, arithmetic and copies ran while one was open for 3% -> 5% of each run, Pallas kernels for 0% -> 0%
where the time goes in v1:
time: 374 us; the launch traced here: 373 us
  waiting for transfers between devices  185 us (49%)
  Pallas kernels  130 us (35%)
  between operations  16.8 us (4%)
  other arithmetic  14.3 us (4%)
  starting transfers between devices  13 us (3%)
  matrix products  9.77 us (3%)
  local copies, waits for them, and re-layouts  4.27 us (1%)
    reduce_scatter x1, waiting for transfers between devices, shards(): lax.psum_scatter(buffer, AXES, scatter_dimension=0, tiled=True, axis_inde...  98.6 us
    all_gather x1, waiting for transfers between devices, shards(): lax.all_gather(master.astype(low), AXES, axis=0, tiled=True, axis_index_g...  78.1 us
    pallas_call x1, Pallas kernels, layer(): pl.pallas_call(feed_kernel, grid_spec=pltpu.PrefetchScalarGridSpec(num_sc...  58.3 us
    pallas_call x1, Pallas kernels, layer(): pl.pallas_call(back_kernel, grid_spec=pltpu.PrefetchScalarGridSpec(num_sc...  41.6 us
    pallas_call x1, Pallas kernels, layer(): pl.pallas_call(attend_kernel, grid=(pairs,), in_specs=[column(0), column(...  18.8 us
    ppermute x10, starting transfers between devices, everywhere(): lax.ppermute(value, AXES, [(d, d ^ step) for d in range(devices)])  12.9 us
    pallas_call x1, Pallas kernels, layer(): pl.pallas_call(qkv_kernel, grid_spec=pltpu.PrefetchScalarGridSpec(num_sca...  10.9 us
    ppermute x10, waiting for transfers between devices, everywhere(): lax.ppermute(value, AXES, [(d, d ^ step) for d in range(devices)])  8.79 us
  transfers between devices with their start and end apart: 12, of which 8 were waited for; matrix products, arithmetic and copies ran while one was open for 5% of the time, Pallas kernels for 0%

profile of v1, /device:TPU:0, one launch (start us, length us, event | category | flops | bytes accessed | tf_op | source)
XLA Modules:
  0.0 373.3 jit_solution(16457412600278131350)
XLA Ops:
  7.2 2.1 convert_element_type.18
  9.4 0.8 reduce-window.4
  10.8 0.8 slice.20
  12.3 0.7 add_select_fusion.1
  13.0 0.7 select_reduce_fusion
  13.8 1.4 fusion.16.inside
  15.2 1.3 fusion.19.place
  17.2 0.9 fusion.15.image_keys
  18.0 0.9 select_convert_fusion.image_query
  18.9 78.1 %all-gather.2.cloned.1.call-done.whole = bf16[448,128,128]{2,1,0:T(8,128)(2,1)} async-done(((bf16[14,128,128]{2,1,0:T(8,128)(2,1)}), bf16[448,128,128]{2,1,0:T(8,128)(2,1)}) %all-gather.2.cloned.1.call-update) | async-done | bytes 14680080 | tf_op jit(solution)/shard_map/all_gather | solution.py:653
  96.9 10.9 %qkv.1.query.keys.values = bf16[784,2304]{1,0:T(8,128)(2,1)} custom-call(s32[432]{0:T(512)} %fusion.19.place, bf16[448,128,128]{2,1,0:T(8,128)(2,1)} %all-gather.2.cloned.1.call-done.whole, bf16[784,768]{1,0:T(8,128)(2,1)} %patches.5, f32[12,768]{1,0:T(8,128)} %vectors.5), custom_call_target="tpu_custom_call" | custom-call | tf_op jit(solution)/shard_map/qkv/pallas_call | solution.py:448
  107.8 18.8 %attend.1 = (bf16[784,768]{1,0:T(8,128)(2,1)}, bf16[12,784,784]{2,1,0:T(8,128)(2,1)}) custom-call(bf16[784,2304]{1,0:T(8,128)(2,1)} %qkv.1.query.keys.values, bf16[784,2304]{1,0:T(8,128)(2,1)} %qkv.1.query.keys.values, bf16[784,2304]{1,0:T(8,128)(2,1)} %qkv.1.query.keys.values, bf16[784,128]{1,0:T(8,128)(2,1)} %select_convert_fusion.image_query, ...), custom_call_target="tpu_custom_call" | custom-call | tf_op jit(solution)/shard_map/attend/pallas_call | solution.py:469
  126.6 58.3 %feed.1 = (bf16[784,768]{1,0:T(8,128)(2,1)}, f32[784,768]{1,0:T(8,128)}, bf16[784,768]{1,0:T(8,128)(2,1)}, f32[8,768]{1,0:T(8,128)}, f32[6,1,512]{2,1,0:T(1,128)}, /*index=5*/bf16[448,128,128]{2,1,0:T(8,128)(2,1)}) custom-call(s32[432]{0:T(512)} %fusion.19.place, bf16[448,128,128]{2,1,0:T(8,128)(2,1)} %all-gather.2.cloned.1.call-done.whole, ...), custom_call_target="tpu_custom_call" | custom-call | tf_op jit(solution)/shard_map/feed/pallas_call | solution.py:487
  184.9 41.6 %back.1 = (bf16[784,768]{1,0:T(8,128)(2,1)}, f32[8,768]{1,0:T(8,128)}, bf16[448,128,128]{2,1,0:T(8,128)(2,1)}) custom-call(s32[432]{0:T(512)} %fusion.19.place, bf16[448,128,128]{2,1,0:T(8,128)(2,1)} %all-gather.2.cloned.1.call-done.whole, bf16[448,128,128]{2,1,0:T(8,128)(2,1)} %get-tuple-element.22.held, ...), custom_call_target="tpu_custom_call", output_to_operand_aliasing={{2}: (2, {})} | custom-call | tf_op jit(solution)/shard_map/back/pallas_call | solution.py:551
  227.7 1.0 collective-permute-done.5
  228.7 1.5 collective-permute-start.6
  230.4 2.5 collective-permute-done.6
  232.9 1.4 collective-permute-start.7
  234.3 98.6 %reduce-scatter.2.cloned.1.call-done = bf16[14,128,128]{2,1,0:T(8,128)(2,1)} async-done(((bf16[448,128,128]{2,1,0:T(8,128)(2,1)}), bf16[14,128,128]{2,1,0:T(8,128)(2,1)}) %reduce-scatter.2.cloned.1.call-update) | async-done | bytes 458768 | tf_op jit(solution)/shard_map/reduce_scatter | solution.py:668
  332.9 1.9 multiply_reduce_fusion
  335.9 1.5 collective-permute-start.8
  338.0 1.4 collective-permute-start.1
  340.1 2.7 collective-permute-start.9
  343.4 0.7 collective-permute-start.2
  344.1 2.9 collective-permute-done.2
  347.1 1.5 collective-permute-start.3
  349.2 1.5 collective-permute-done.3
  350.7 1.7 collective-permute-start.4
  352.3 2.7 fusion.9
  357.1 2.7 multiply_add_fusion
  359.8 1.5 fusion.3
  361.7 3.0 fusion.1
  (62 shorter events, 8.7 us)
Async XLA Ops:
  7.2 349.9 %copy-start = (f32[14,128,128]{2,1,0:T(8,128)S(1)}, f32[14,128,128]{2,1,0:T(8,128)}, u32[]{:S(2)}) copy-start(f32[14,128,128]{2,1,0:T(8,128)} %param.21) | copy-start | bytes 2752516
  7.2 89.7 %all-gather.2.cloned.1.call-start = ((), (), s32[]{:S(2)}) async-start(), calls=%async_computation.1 | async-start | bytes 15138816 | tf_op jit(solution)/shard_map/all_gather | solution.py:653
  9.4 323.6 %reduce-scatter.2.cloned.1.call-start = ((), (), s32[]{:S(2)}) async-start(), calls=%async_computation.2 | async-start | bytes 15138816 | tf_op jit(solution)/shard_map/reduce_scatter | solution.py:668
  226.5 0.7 copy-start.10
  226.6 0.7 copy-start.11
  226.6 0.8 copy-start.9
  226.6 3.7 copy-start.8
  226.6 125.8 %copy-start.2 = (f32[14,128,128]{2,1,0:T(8,128)S(1)}, f32[14,128,128]{2,1,0:T(8,128)}, u32[]{:S(2)}) copy-start(f32[14,128,128]{2,1,0:T(8,128)} %param.20) | copy-start | bytes 2752516
  227.4 1.3 collective-permute-start.5
  228.7 4.2 %collective-permute-start.6 = (f32[12,768]{1,0:T(8,128)S(1)}, f32[12,768]{1,0:T(8,128)S(1)}, u32[]{:S(2)}, u32[]{:S(2)}) collective-permute-start(f32[12,768]{1,0:T(8,128)S(1)} %fusion.24), channel_id=1, source_target_pairs={{0,2},{1,3},{2,0},{3,1},{4,6},{5,7},{6,4},{7,5},{8,10},{9,11},{10,... | collective-permute-start | bytes 110600 | tf_op jit(solution)/shard_map/ppermute | solution.py:663
  232.9 103.0 %collective-permute-start.7 = (f32[12,768]{1,0:T(8,128)S(1)}, f32[12,768]{1,0:T(8,128)S(1)}, u32[]{:S(2)}, u32[]{:S(2)}) collective-permute-start(f32[12,768]{1,0:T(8,128)S(1)} %add.96), channel_id=1, source_target_pairs={{0,4},{1,5},{2,6},{3,7},{4,0},{5,1},{6,2},{7,3},{8,12},{9,13},{10,... | collective-permute-start | bytes 110600 | tf_op jit(solution)/shard_map/ppermute | solution.py:663
  335.5 1.9 collective-permute-start
  335.9 4.2 %collective-permute-start.8 = (f32[12,768]{1,0:T(8,128)S(1)}, f32[12,768]{1,0:T(8,128)S(1)}, u32[]{:S(2)}, u32[]{:S(2)}) collective-permute-start(f32[12,768]{1,0:T(8,128)S(1)} %add.97), channel_id=1, source_target_pairs={{0,8},{1,9},{2,10},{3,11},{4,12},{5,13},{6,14},{7,15},{8,0},{9,1},... | collective-permute-start | bytes 110600 | tf_op jit(solution)/shard_map/ppermute | solution.py:663
  338.0 4.7 %collective-permute-start.1 = (f32[8,128]{1,0:T(8,128)S(1)}, f32[8,128]{1,0:T(8,128)S(1)}, u32[]{:S(2)}, u32[]{:S(2)}) collective-permute-start(f32[8,128]{1,0:T(8,128)S(1)} %broadcast_add_fusion), channel_id=1, source_target_pairs={{0,2},{1,3},{2,0},{3,1},{4,6},{5,7},{6,4},{7,5},{8,10},{9,11},{10,... | collective-permute-start | bytes 12296 | tf_op jit(solution)/shard_map/ppermute | solution.py:663
  340.1 8.5 %collective-permute-start.9 = (f32[12,768]{1,0:T(8,128)S(1)}, f32[12,768]{1,0:T(8,128)S(1)}, u32[]{:S(2)}, u32[]{:S(2)}) collective-permute-start(f32[12,768]{1,0:T(8,128)S(1)} %add.98), channel_id=1, source_target_pairs={{0,16},{1,17},{2,18},{3,19},{4,20},{5,21},{6,22},{7,23},{8,24},{9,... | collective-permute-start | bytes 110600 | tf_op jit(solution)/shard_map/ppermute | solution.py:663
  343.4 3.7 collective-permute-start.2
  347.1 3.6 collective-permute-start.3
  350.7 4.5 %collective-permute-start.4 = (f32[8,128]{1,0:T(8,128)S(1)}, f32[8,128]{1,0:T(8,128)S(1)}, u32[]{:S(2)}, u32[]{:S(2)}) collective-permute-start(f32[8,128]{1,0:T(8,128)S(1)} %add.93), channel_id=1, source_target_pairs={{0,16},{1,17},{2,18},{3,19},{4,20},{5,21},{6,22},{7,23},{8,24},{9,... | collective-permute-start | bytes 12296 | tf_op jit(solution)/shard_map/ppermute | solution.py:663
  359.8 4.8 %copy-start.3 = (f32[14,128,128]{2,1,0:T(8,128)}, f32[14,128,128]{2,1,0:T(8,128)S(1)}, u32[]{:S(2)}) copy-start(f32[14,128,128]{2,1,0:T(8,128)S(1)} %get-tuple-element.36) | copy-start | bytes 2752516
  359.8 4.8 %copy-start.4 = (f32[14,128,128]{2,1,0:T(8,128)}, f32[14,128,128]{2,1,0:T(8,128)S(1)}, u32[]{:S(2)}) copy-start(f32[14,128,128]{2,1,0:T(8,128)S(1)} %get-tuple-element.37) | copy-start | bytes 2752516
  359.8 1.8 copy-start.1
  361.7 3.0 copy-start.5
  361.7 3.0 copy-start.6
  361.7 3.0 copy-start.7
Sparse Core Ops, SparseCore 0:
  10.2 86.7 all-gather.1
  226.7 106.1 reduce-scatter.1

commit v2 on v1

--- a/solution.py
+++ b/solution.py
@@ -305,7 +305,6 @@
 
 def back_kernel(
     place,
-    whole,
     held,
     query,
     keys,
@@ -314,18 +313,12 @@
     grad_mixed,
     mixed,
     patches,
-    grad_middle,
     vectors,
-    grad_input,
-    sums,
+    grad_project,
     buffer,
-    weight,
-    grad_project,
     grad_low,
     normed,
-    grad_sum,
     stage,
-    sems,
     out_sems,
 ):
     del held
@@ -337,11 +330,6 @@
 
     @pl.when(step == 0)
     def _():
-        for part in range(3):
-            start_blocks(
-                place, whole, weight.at[part], sems.at[part], 0, 3 * side, 0, part * side, side, side
-            )
-
         def norm(t, carry):
             at = rows_of(t)
             normal, _ = normal_parts(patches[at, :].astype(wide))
@@ -381,35 +369,123 @@
                 await_bytes(stage.at[0], out_sems.at[0])
             stage[part % 2] = mm(normed[...], grad_project[part], 0, 0).astype(low)
             store_blocks(
-                place, stage.at[part % 2], buffer, out_sems.at[part % 2], 0, 3 * side, 0, part * side, side, side
+                place,
+                stage.at[part % 2],
+                buffer,
+                out_sems.at[part % 2],
+                0,
+                3 * side,
+                0,
+                part * side,
+                side,
+                side,
             )
-        for part in range(3):
-            await_bytes(weight.at[part], sems.at[part])
-        total = mm(grad_project[0], weight[0], 1, 1)
-        total = total + mm(grad_project[1], weight[1], 1, 1)
-        grad_sum[...] = total + mm(grad_project[2], weight[2], 1, 1)
-
-        def finish(t, carry):
-            at = rows_of(t)
-            grad = grad_sum[at, :]
-            normal, factor = normal_parts(patches[at, :].astype(wide))
-            back = norm_back(grad, normal, factor, vectors[0:1, :])
-            grad_input[at, :] = (grad_middle[at, :] + back).astype(low)
-            gain, shift, bias_query, bias_value = carry
-            return (
-                gain + jnp.sum(grad * normal, axis=0, keepdims=True),
-                shift + jnp.sum(grad, axis=0, keepdims=True),
-                bias_query + jnp.sum(grad_project[0, at, :].astype(wide), axis=0, keepdims=True),
-                bias_value + jnp.sum(grad_project[2, at, :].astype(wide), axis=0, keepdims=True),
-            )
-
-        empty = jnp.zeros((1, width), wide)
-        found = lax.fori_loop(0, tiles(rows), finish, (empty, empty, empty, empty))
-        for row in range(4):
-            sums[row : row + 1, :] = found[row]
-        sums[4:8, :] = jnp.zeros((4, width), wide)
         await_bytes(stage.at[1], out_sems.at[1])
         await_bytes(stage.at[0], out_sems.at[0])
+
+
+def input_kernel(
+    place, whole, grad_project, patches, grad_middle, vectors, grad_input, sums, weight, grad_sum, sems
+):
+    rows, width = patches.shape
+    side = width // 128
+    for part in range(3):
+        start_blocks(
+            place, whole, weight.at[part], sems.at[part], 0, 3 * side, 0, part * side, side, side
+        )
+    for part in range(3):
+        await_bytes(weight.at[part], sems.at[part])
+    total = mm(grad_project[0], weight[0], 1, 1)
+    total = total + mm(grad_project[1], weight[1], 1, 1)
+    grad_sum[...] = total + mm(grad_project[2], weight[2], 1, 1)
+
+    def finish(t, carry):
+        at = rows_of(t)
+        grad = grad_sum[at, :]
+        normal, factor = normal_parts(patches[at, :].astype(wide))
+        back = norm_back(grad, normal, factor, vectors[0:1, :])
+        grad_input[at, :] = (grad_middle[at, :] + back).astype(low)
+        gain, shift, bias_query, bias_value = carry
+        return (
+            gain + jnp.sum(grad * normal, axis=0, keepdims=True),
+            shift + jnp.sum(grad, axis=0, keepdims=True),
+            bias_query + jnp.sum(grad_project[0, at, :].astype(wide), axis=0, keepdims=True),
+            bias_value + jnp.sum(grad_project[2, at, :].astype(wide), axis=0, keepdims=True),
+        )
+
+    empty = jnp.zeros((1, width), wide)
+    found = lax.fori_loop(0, tiles(rows), finish, (empty, empty, empty, empty))
+    for row in range(4):
+        sums[row : row + 1, :] = found[row]
+    sums[4:8, :] = jnp.zeros((4, width), wide)
+
+
+def full_dot(a, b, ca, cb):
+    return lax.dot_general(
+        a, b, (((ca,), (cb,)), ((), ())), precision=highest, preferred_element_type=wide
+    )
+
+
+def turn_kernel(named, grads, left, right, rotated, total):
+    s = pl.program_id(0)
+    block = jnp.where(named[s] > 0, grads[0].astype(wide), 0.0)
+    rotated[0] = full_dot(full_dot(left[0], block, 0, 0), right[0], 1, 0)
+
+    @pl.when(s == 0)
+    def _():
+        total[...] = jnp.zeros_like(total)
+
+    total[...] += jnp.sum(block * block)
+
+
+def adam_parts(gradient, first, second):
+    correction = 1.0 - beta**STEP
+    new_first = beta * first + (1.0 - beta) * gradient
+    new_second = beta * second + (1.0 - beta) * gradient * gradient
+    direction = new_first / correction / (jnp.sqrt(new_second / correction) + adam_eps)
+    return new_first, new_second, direction
+
+
+def adam_kernel(
+    count,
+    total,
+    rotated,
+    master,
+    first,
+    second,
+    left,
+    right,
+    vector_sum,
+    vectors,
+    vector_first,
+    vector_second,
+    new_master,
+    new_first,
+    new_second,
+    clip,
+    new_vectors,
+    new_vector_first,
+    new_vector_second,
+    factor,
+):
+    @pl.when(pl.program_id(0) == 0)
+    def _():
+        grads = vector_sum[...]
+        norm = jnp.sqrt(total[0:1, 0:1] + jnp.sum(grads * grads))
+        clip[...] = norm
+        factor[...] = jnp.minimum(1.0, 0.5 * math.sqrt(count) / norm)
+        ahead, squares, way = adam_parts(
+            factor[...] * grads, vector_first[...], vector_second[...]
+        )
+        new_vector_first[...] = ahead
+        new_vector_second[...] = squares
+        new_vectors[...] = vectors[...] - rate_vector * way
+
+    ahead, squares, way = adam_parts(factor[...] * rotated[0], first[0], second[0])
+    new_first[0] = ahead
+    new_second[0] = squares
+    update = full_dot(full_dot(left[0], way, 1, 0), right[0], 1, 1)
+    new_master[0] = master[0] - rate_matrix * (update + decay_weight * master[0])
 
 
 VMEM_LIMIT = 60 * 1024 * 1024
@@ -429,12 +505,70 @@
     return pl.BlockSpec(shape, lambda *_: (0,) * len(shape))
 
 
-def layer(whole, place, patches, cotangent, counts, vectors, slots):
+def shards(
+    sizes,
+    patches,
+    lengths,
+    cotangent,
+    owners,
+    master,
+    first_moment,
+    second_moment,
+    left_basis,
+    right_basis,
+    vectors,
+    vector_first,
+    vector_second,
+):
+    dp, fsdp = sizes
+    devices = dp * fsdp
     rows, width = patches.shape
     hidden = 4 * width
     side = width // 128
     pairs = width // 128
+    held, size = master.shape[0], master.shape[1]
+    slots = held * devices
     shape = jax.ShapeDtypeStruct
+    me = lax.axis_index(AXES)
+    order = ring_order(dp, fsdp)
+    groups = None if order is None else [order]
+
+    def gather(value):
+        return lax.all_gather(value, AXES, axis=0, tiled=True, axis_index_groups=groups)
+
+    def scatter(value):
+        return lax.psum_scatter(
+            value, AXES, scatter_dimension=0, tiled=True, axis_index_groups=groups
+        )
+
+    def everywhere(value):
+        step = 1
+        while step < devices:
+            value = value + lax.ppermute(value, AXES, [(d, d ^ step) for d in range(devices)])
+            step *= 2
+        return value
+
+    whole = gather(master.astype(low))
+    if order is None:
+        place = owners
+    else:
+        rank = [0] * devices
+        for spot, device in enumerate(order):
+            rank[device] = spot
+        device = owners // held
+        spot = jnp.sum(
+            jnp.where(
+                device[:, None] == jnp.arange(devices, dtype=jnp.int32)[None, :],
+                jnp.array(rank, jnp.int32)[None, :],
+                0,
+            ),
+            axis=1,
+        )
+        place = spot * held + owners % held
+    mine = me * held + jnp.arange(held, dtype=jnp.int32)
+    named = jnp.any(mine[:, None] == owners[None, :], axis=1).astype(jnp.int32)
+
+    counts = lengths[0]
     ends = jnp.cumsum(counts)
     places = jnp.arange(rows, dtype=jnp.int32)[:, None]
     image = jnp.sum((places >= ends[None, :]).astype(jnp.int32), axis=1, keepdims=True)
@@ -533,7 +667,7 @@
             shape((rows, width), low),
             shape((8, width), wide),
             shape((steps, 1, CHUNK), wide),
-            shape((slots, 128, 128), low),
+            shape((slots, size, size), low),
         ],
         compiler_params=params(),
         name="feed",
@@ -548,13 +682,12 @@
         vectors[7:11].reshape(steps, 1, CHUNK),
     )
 
-    grad_input, sums_one, buffer = pl.pallas_call(
+    grad_project, buffer = pl.pallas_call(
         back_kernel,
         grid_spec=pltpu.PrefetchScalarGridSpec(
             num_scalar_prefetch=1,
             grid=(pairs,),
             in_specs=[
-                whole_spec(),
                 whole_spec(),
                 column(0),
                 column(pairs),
@@ -563,32 +696,25 @@
                 column(0),
                 column(0),
                 full((rows, width)),
-                full((rows, width)),
                 full((12, width)),
             ],
-            out_specs=[full((rows, width)), full((8, width)), whole_spec()],
+            out_specs=[full((3, rows, width)), whole_spec()],
             scratch_shapes=[
-                pltpu.VMEM((3, width, width), low),
-                pltpu.VMEM((3, rows, width), low),
                 pltpu.VMEM((2, rows, rows), low),
                 pltpu.VMEM((rows, width), low),
-                pltpu.VMEM((rows, width), wide),
                 pltpu.VMEM((2, width, width), low),
-                pltpu.SemaphoreType.DMA((3,)),
                 pltpu.SemaphoreType.DMA((2,)),
             ],
         ),
         out_shape=[
-            shape((rows, width), low),
-            shape((8, width), wide),
-            shape((slots, 128, 128), low),
+            shape((3, rows, width), low),
+            shape((slots, size, size), low),
         ],
-        input_output_aliases={2: 2},
+        input_output_aliases={1: 1},
         compiler_params=params(),
         name="back",
     )(
         place,
-        whole,
         buffer,
         project,
         project,
@@ -597,102 +723,89 @@
         grad_mixed,
         mixed,
         patches,
-        grad_middle,
         vectors,
     )
-    del side
+    owned = scatter(buffer)
+
+    grad_input, sums_one = pl.pallas_call(
+        input_kernel,
+        grid_spec=pltpu.PrefetchScalarGridSpec(
+            num_scalar_prefetch=1,
+            grid=(1,),
+            in_specs=[
+                whole_spec(),
+                full((3, rows, width)),
+                full((rows, width)),
+                full((rows, width)),
+                full((12, width)),
+            ],
+            out_specs=[full((rows, width)), full((8, width))],
+            scratch_shapes=[
+                pltpu.VMEM((3, width, width), low),
+                pltpu.VMEM((rows, width), wide),
+                pltpu.SemaphoreType.DMA((3,)),
+            ],
+        ),
+        out_shape=[shape((rows, width), low), shape((8, width), wide)],
+        compiler_params=params(),
+        name="input",
+    )(place, whole, grad_project, patches, grad_middle, vectors)
     vector_grad = jnp.concatenate(
         [sums_one[0:4], sums_two[0:3], sums_up.reshape(4, width), sums_two[3:4]], axis=0
     )
-    return result, grad_input, vector_grad, buffer
-
-
-def shards(
-    sizes,
-    patches,
-    lengths,
-    cotangent,
-    owners,
-    master,
-    first_moment,
-    second_moment,
-    left_basis,
-    right_basis,
-    vectors,
-    vector_first,
-    vector_second,
-):
-    dp, fsdp = sizes
-    devices = dp * fsdp
-    width = patches.shape[1]
-    held, size = master.shape[0], master.shape[1]
-    slots = held * devices
-    order = ring_order(dp, fsdp)
-    me = lax.axis_index(AXES)
-    if order is None:
-        groups = None
-        place = owners
-    else:
-        groups = [order]
-        rank = [0] * devices
-        for spot, device in enumerate(order):
-            rank[device] = spot
-        device = owners // held
-        spot = jnp.sum(
-            jnp.where(
-                device[:, None] == jnp.arange(devices, dtype=jnp.int32)[None, :],
-                jnp.array(rank, jnp.int32)[None, :],
-                0,
-            ),
-            axis=1,
+    vector_sum = everywhere(vector_grad)
+
+    owned, vector_sum = lax.optimization_barrier((owned, vector_sum))
+
+    def block():
+        return pl.BlockSpec((1, size, size), lambda s, *_: (s, 0, 0))
+
+    rotated, total = pl.pallas_call(
+        turn_kernel,
+        grid_spec=pltpu.PrefetchScalarGridSpec(
+            num_scalar_prefetch=1,
+            grid=(held,),
+            in_specs=[block(), block(), block()],
+            out_specs=[block(), full((8, 128))],
+        ),
+        out_shape=[shape((held, size, size), wide), shape((8, 128), wide)],
+        compiler_params=params(),
+        name="turn",
+    )(named, owned, left_basis, right_basis)
+    total = everywhere(total)
+
+    count = owners.shape[0] * size * size + vectors.shape[0] * width
+    small = full((12, width))
+    new_master, new_first, new_second, clip, new_vectors, new_vector_first, new_vector_second = (
+        pl.pallas_call(
+            functools.partial(adam_kernel, count),
+            grid=(held,),
+            in_specs=[full((8, 128))] + [block() for _ in range(6)] + [small] * 4,
+            out_specs=[block(), block(), block(), full((1, 1)), small, small, small],
+            out_shape=[shape((held, size, size), wide)] * 3
+            + [shape((1, 1), wide)]
+            + [shape((12, width), wide)] * 3,
+            scratch_shapes=[pltpu.VMEM((1, 1), wide)],
+            compiler_params=params(),
+            name="adam",
+        )(
+            total,
+            rotated,
+            master,
+            first_moment,
+            second_moment,
+            left_basis,
+            right_basis,
+            vector_sum,
+            vectors,
+            vector_first,
+            vector_second,
         )
-        place = spot * held + owners % held
-    mine = me * held + jnp.arange(held, dtype=jnp.int32)
-    named = jnp.any(mine[:, None] == owners[None, :], axis=1)
-
-    whole = lax.all_gather(
-        master.astype(low), AXES, axis=0, tiled=True, axis_index_groups=groups
-    )
-    result, grad_input, vector_grad, buffer = layer(
-        whole, place, patches, cotangent, lengths[0], vectors, slots
-    )
-
-    def everywhere(value):
-        step = 1
-        while step < devices:
-            value = value + lax.ppermute(value, AXES, [(d, d ^ step) for d in range(devices)])
-            step *= 2
-        return value
-
-    vector_sum = everywhere(vector_grad)
-    owned = lax.psum_scatter(
-        buffer, AXES, scatter_dimension=0, tiled=True, axis_index_groups=groups
-    )
-    owned = jnp.where(named[:, None, None], owned.astype(wide), 0.0)
-    total_blocks = everywhere(jnp.broadcast_to(jnp.sum(owned * owned), (8, 128)))[0, 0]
-    clip_norm = jnp.sqrt(total_blocks + jnp.sum(vector_sum * vector_sum))
-    count = owners.shape[0] * size * size + vectors.shape[0] * width
-    factor = jnp.minimum(1.0, 0.5 * math.sqrt(count) / clip_norm)
-    turned = jnp.einsum("sji,sjk->sik", left_basis, owned, precision=highest)
-    rotated = factor * jnp.einsum("sik,skl->sil", turned, right_basis, precision=highest)
-    new_first = beta * first_moment + (1.0 - beta) * rotated
-    new_second = beta * second_moment + (1.0 - beta) * rotated * rotated
-    correction = 1.0 - beta**STEP
-    direction = new_first / correction / (jnp.sqrt(new_second / correction) + adam_eps)
-    back_turn = jnp.einsum("sij,sjk->sik", left_basis, direction, precision=highest)
-    update = jnp.einsum("sik,slk->sil", back_turn, right_basis, precision=highest)
-    new_master = master - rate_matrix * (update + decay_weight * master)
-    vector_clip = factor * vector_sum
-    new_vector_first = beta * vector_first + (1.0 - beta) * vector_clip
-    new_vector_second = beta * vector_second + (1.0 - beta) * vector_clip * vector_clip
-    vector_step = (
-        new_vector_first / correction / (jnp.sqrt(new_vector_second / correction) + adam_eps)
-    )
-    new_vectors = vectors - rate_vector * vector_step
+    )
     return (
         result,
         grad_input,
-        clip_norm,
+        clip.reshape(()),
         new_master,
         new_first,
         new_second,

time: 374 us -> 379 us (1.013)
  Pallas kernels: 130 us -> 161 us
  waiting for transfers between devices: 185 us -> 170 us
  matrix products: 9.77 us -> 0 us
    pallas_call x4 -> x7, Pallas kernels: 130 us -> 161 us  [the longest x1 58.3 us: shards(): pl.pallas_call(feed_kernel, grid_spec=pltpu.PrefetchScalarGridSpec(num_sc...]
    reduce_scatter x1, waiting for transfers between devices: 98.6 us -> 71.4 us  [scatter(): lax.psum_scatter(value, AXES, scatter_dimension=0, tiled=True, axis_index...]
    ppermute x10, waiting for transfers between devices: 8.79 us -> 20.5 us  [everywhere(): lax.ppermute(value, AXES, [(d, d ^ step) for d in range(devices)])]
    dot_general x4 -> x0, matrix products: 9.77 us -> none  [the longest x1 2.96 us: shards(): jnp.einsum('sik,slk->sil', back_turn, right_basis, precision=highest)]
  transfers between devices with their start and end apart: 12 -> 12, of which waited for: 8 -> 12; matrix products, arithmetic and copies ran while one was open for 5% -> 3% of each run, Pallas kernels for 0% -> 4%
where the time goes in v2:
time: 379 us; the launch traced here: 377 us
  waiting for transfers between devices  170 us (45%)
  Pallas kernels  161 us (42%)
  starting transfers between devices  15.8 us (4%)
  between operations  14.2 us (4%)
  other arithmetic  12.1 us (3%)
    all_gather x1, waiting for transfers between devices, gather(): lax.all_gather(value, AXES, axis=0, tiled=True, axis_index_groups=groups)  78.2 us
    reduce_scatter x1, waiting for transfers between devices, scatter(): lax.psum_scatter(value, AXES, scatter_dimension=0, tiled=True, axis_index...  71.4 us
    pallas_call x1, Pallas kernels, shards(): pl.pallas_call(feed_kernel, grid_spec=pltpu.PrefetchScalarGridSpec(num_sc...  58.3 us
    pallas_call x1, Pallas kernels, shards(): pl.pallas_call(back_kernel, grid_spec=pltpu.PrefetchScalarGridSpec(num_sc...  33.7 us
    ppermute x10, waiting for transfers between devices, everywhere(): lax.ppermute(value, AXES, [(d, d ^ step) for d in range(devices)])  20.5 us
    pallas_call x1, Pallas kernels, shards(): pl.pallas_call(attend_kernel, grid=(pairs,), in_specs=[column(0), column(...  18.7 us
    ppermute x10, starting transfers between devices, everywhere(): lax.ppermute(value, AXES, [(d, d ^ step) for d in range(devices)])  15.7 us
    pallas_call x1, Pallas kernels, shards(): pl.pallas_call(functools.partial(adam_kernel, count), grid=(held,), in_sp...  13.4 us
  transfers between devices with their start and end apart: 12, of which 12 were waited for; matrix products, arithmetic and copies ran while one was open for 3% of the time, Pallas kernels for 4%

profile of v2, /device:TPU:0, one launch (start us, length us, event | category | flops | bytes accessed | tf_op | source)
XLA Modules:
  0.0 376.9 jit_solution(416145728836517667)
XLA Ops:
  7.2 2.0 convert_element_type.18
  13.7 1.4 fusion.2.inside
  15.1 1.2 fusion.4.place
  17.0 0.9 fusion.1.image_keys
  17.9 0.9 select_convert_fusion.image_query
  18.7 78.2 %all-gather.2.cloned.1.call-done.whole = bf16[448,128,128]{2,1,0:T(8,128)(2,1)} async-done(((bf16[14,128,128]{2,1,0:T(8,128)(2,1)}), bf16[448,128,128]{2,1,0:T(8,128)(2,1)}) %all-gather.2.cloned.1.call-update) | async-done | bytes 14680080 | tf_op jit(solution)/shard_map/all_gather | solution.py:537
  96.9 10.9 %qkv.1.query.keys.values = bf16[784,2304]{1,0:T(8,128)(2,1)} custom-call(s32[432]{0:T(512)} %fusion.4.place, bf16[448,128,128]{2,1,0:T(8,128)(2,1)} %all-gather.2.cloned.1.call-done.whole, bf16[784,768]{1,0:T(8,128)(2,1)} %patches.7, f32[12,768]{1,0:T(8,128)} %vectors.9), custom_call_target="tpu_custom_call" | custom-call | tf_op jit(solution)/shard_map/qkv/pallas_call | solution.py:582
  107.8 18.7 %attend.1 = (bf16[784,768]{1,0:T(8,128)(2,1)}, bf16[12,784,784]{2,1,0:T(8,128)(2,1)}) custom-call(bf16[784,2304]{1,0:T(8,128)(2,1)} %qkv.1.query.keys.values, bf16[784,2304]{1,0:T(8,128)(2,1)} %qkv.1.query.keys.values, bf16[784,2304]{1,0:T(8,128)(2,1)} %qkv.1.query.keys.values, bf16[784,128]{1,0:T(8,128)(2,1)} %select_convert_fusion.image_query, ...), custom_call_target="tpu_custom_call" | custom-call | tf_op jit(solution)/shard_map/attend/pallas_call | solution.py:603
  126.5 58.3 %feed.1 = (bf16[784,768]{1,0:T(8,128)(2,1)}, f32[784,768]{1,0:T(8,128)}, bf16[784,768]{1,0:T(8,128)(2,1)}, f32[8,768]{1,0:T(8,128)}, f32[6,1,512]{2,1,0:T(1,128)}, /*index=5*/bf16[448,128,128]{2,1,0:T(8,128)(2,1)}) custom-call(s32[432]{0:T(512)} %fusion.4.place, bf16[448,128,128]{2,1,0:T(8,128)(2,1)} %all-gather.2.cloned.1.call-done.whole, ...), custom_call_target="tpu_custom_call" | custom-call | tf_op jit(solution)/shard_map/feed/pallas_call | solution.py:621
  184.8 33.7 %back.1 = (bf16[3,784,768]{2,1,0:T(8,128)(2,1)}, bf16[448,128,128]{2,1,0:T(8,128)(2,1)}) custom-call(s32[432]{0:T(512)} %fusion.4.place, bf16[448,128,128]{2,1,0:T(8,128)(2,1)} %get-tuple-element.34.held, bf16[784,2304]{1,0:T(8,128)(2,1)} %qkv.1.query.keys.values, bf16[784,2304]{1,0:T(8,128)(2,1)} %qkv.1.query.keys.values, ...), custom_call_target="tpu_custom_call", output_to_operand_aliasing={{1}: (1, {})} | custom-call | tf_op jit(solution)/shard_map/back/pallas_call | solution.py:685
  219.3 13.2 %input.1 = (bf16[784,768]{1,0:T(8,128)(2,1)}, f32[8,768]{1,0:T(8,128)}) custom-call(s32[432]{0:T(512)} %fusion.4.place, bf16[448,128,128]{2,1,0:T(8,128)(2,1)} %all-gather.2.cloned.1.call-done.whole, bf16[3,784,768]{2,1,0:T(8,128)(2,1)} %get-tuple-element.37.grad_project, bf16[784,768]{1,0:T(8,128)(2,1)} %patches.7, ...), custom_call_target="tpu_custom_call" | custom-call | tf_op jit(solution)/shard_map/input/pallas_call | solution.py:730
  233.7 1.0 collective-permute-done
  234.7 1.5 collective-permute-start.1
  236.2 2.7 collective-permute-done.1
  238.9 2.0 collective-permute-start.2
  241.0 2.1 collective-permute-done.2
  243.1 1.5 collective-permute-start.3
  244.5 3.2 collective-permute-done.3
  247.7 2.4 collective-permute-start.4
  250.8 2.8 collective-permute-done.4
  254.3 71.4 %reduce-scatter.2.cloned.1.call-done.grads = bf16[14,128,128]{2,1,0:T(8,128)(2,1)} async-done(((bf16[448,128,128]{2,1,0:T(8,128)(2,1)}), bf16[14,128,128]{2,1,0:T(8,128)(2,1)}) %reduce-scatter.2.cloned.1.call-update) | async-done | bytes 458768 | tf_op jit(solution)/shard_map/reduce_scatter | solution.py:540
  325.7 12.9 %turn.1 = (f32[14,128,128]{2,1,0:T(8,128)}, f32[8,128]{1,0:T(8,128)}) custom-call(s32[14]{0:T(128)} %convert_element_type.23.named, bf16[14,128,128]{2,1,0:T(8,128)(2,1)} %reduce-scatter.2.cloned.1.call-done.grads, f32[14,128,128]{2,1,0:T(8,128)} %left.3, f32[14,128,128]{2,1,0:T(8,128)} %right.3), custom_call_target="tpu_custom_call" | custom-call | tf_op jit(solution)/shard_map/turn/pallas_call | solution.py:763
  338.7 1.3 collective-permute-done.5
  340.7 1.7 collective-permute-start.6
  342.4 1.9 collective-permute-done.6
  344.3 1.8 collective-permute-start.7
  346.1 1.8 collective-permute-done.7
  347.9 1.6 collective-permute-start.8
  349.5 2.0 collective-permute-done.8
  351.5 2.8 collective-permute-start.9
  354.3 1.7 collective-permute-done.9
  356.6 13.4 %adam.1 = (f32[14,128,128]{2,1,0:T(8,128)}, f32[14,128,128]{2,1,0:T(8,128)}, f32[14,128,128]{2,1,0:T(8,128)}, f32[1,1]{1,0:T(1,128)}, f32[12,768]{1,0:T(8,128)}, /*index=5*/f32[12,768]{1,0:T(8,128)}, f32[12,768]{1,0:T(8,128)}) custom-call(f32[8,128]{1,0:T(8,128)} %add.69.total, f32[14,128,128]{2,1,0:T(8,128)} %get-tuple-element.46.rotated, ...), custom_call_target="tpu_custom_call" | custom-call | tf_op jit(solution)/shard_map/adam/pallas_call | solution.py:780
  (40 shorter events, 9.7 us)
Async XLA Ops:
  7.2 89.7 %all-gather.2.cloned.1.call-start = ((), (), s32[]{:S(2)}) async-start(), calls=%async_computation.1 | async-start | bytes 15138816 | tf_op jit(solution)/shard_map/all_gather | solution.py:537
  9.3 316.4 %reduce-scatter.2.cloned.1.call-start = ((), (), s32[]{:S(2)}) async-start(), calls=%async_computation.2 | async-start | bytes 15138816 | tf_op jit(solution)/shard_map/reduce_scatter | solution.py:540
  218.5 0.7 copy-start.2
  219.3 14.0 %copy-start.1 = (f32[6,1,512]{2,1,0:T(1,128)S(1)}, f32[6,1,512]{2,1,0:T(1,128)}, u32[]{:S(2)}) copy-start(f32[6,1,512]{2,1,0:T(1,128)} %get-tuple-element.43) | copy-start | bytes 36868
  219.3 30.9 %copy-start = (s32[432]{0:T(512)S(1)}, s32[432]{0:T(512)}, u32[]{:S(2)}) copy-start(s32[432]{0:T(512)} %param.16) | copy-start | bytes 5188
  233.4 1.3 collective-permute-start
  234.7 4.2 %collective-permute-start.1 = (f32[12,768]{1,0:T(8,128)S(1)}, f32[12,768]{1,0:T(8,128)S(1)}, u32[]{:S(2)}, u32[]{:S(2)}) collective-permute-start(f32[12,768]{1,0:T(8,128)S(1)} %fusion.6), channel_id=1, source_target_pairs={{0,2},{1,3},{2,0},{3,1},{4,6},{5,7},{6,4},{7,5},{8,10},{9,11},{10,... | collective-permute-start | bytes 110600 | tf_op jit(solution)/shard_map/ppermute | solution.py:547
  238.9 4.2 %collective-permute-start.2 = (f32[12,768]{1,0:T(8,128)S(1)}, f32[12,768]{1,0:T(8,128)S(1)}, u32[]{:S(2)}, u32[]{:S(2)}) collective-permute-start(f32[12,768]{1,0:T(8,128)S(1)} %add.61), channel_id=1, source_target_pairs={{0,4},{1,5},{2,6},{3,7},{4,0},{5,1},{6,2},{7,3},{8,12},{9,13},{10,... | collective-permute-start | bytes 110600 | tf_op jit(solution)/shard_map/ppermute | solution.py:547
  243.1 4.6 %collective-permute-start.3 = (f32[12,768]{1,0:T(8,128)S(1)}, f32[12,768]{1,0:T(8,128)S(1)}, u32[]{:S(2)}, u32[]{:S(2)}) collective-permute-start(f32[12,768]{1,0:T(8,128)S(1)} %add.62), channel_id=1, source_target_pairs={{0,8},{1,9},{2,10},{3,11},{4,12},{5,13},{6,14},{7,15},{8,0},{9,1},... | collective-permute-start | bytes 110600 | tf_op jit(solution)/shard_map/ppermute | solution.py:547
  247.7 5.9 %collective-permute-start.4 = (f32[12,768]{1,0:T(8,128)S(1)}, f32[12,768]{1,0:T(8,128)S(1)}, u32[]{:S(2)}, u32[]{:S(2)}) collective-permute-start(f32[12,768]{1,0:T(8,128)S(1)} %add.63), channel_id=1, source_target_pairs={{0,16},{1,17},{2,18},{3,19},{4,20},{5,21},{6,22},{7,23},{8,24},{9,... | collective-permute-start | bytes 110600 | tf_op jit(solution)/shard_map/ppermute | solution.py:547
  338.6 1.4 collective-permute-start.5
  340.7 3.6 collective-permute-start.6
  344.3 3.6 collective-permute-start.7
  347.9 3.6 collective-permute-start.8
  351.5 4.5 %collective-permute-start.9 = (f32[8,128]{1,0:T(8,128)S(1)}, f32[8,128]{1,0:T(8,128)S(1)}, u32[]{:S(2)}, u32[]{:S(2)}) collective-permute-start(f32[8,128]{1,0:T(8,128)S(1)} %add.68), channel_id=1, source_target_pairs={{0,16},{1,17},{2,18},{3,19},{4,20},{5,21},{6,22},{7,23},{8,24},{9,... | collective-permute-start | bytes 12296 | tf_op jit(solution)/shard_map/ppermute | solution.py:547
Sparse Core Ops, SparseCore 0:
  10.2 86.7 all-gather.1
  218.7 107.0 reduce-scatter.1

commit v3 on v2

--- a/solution.py
+++ b/solution.py
@@ -155,7 +155,8 @@
     inside,
     vectors,
     bias_up,
-    result,
+    middle,
+    active,
     grad_middle,
     grad_mixed,
     sums,
@@ -164,7 +165,6 @@
     w_out,
     w_up,
     w_down,
-    middle,
     normal,
     factor,
     second,
@@ -175,7 +175,6 @@
     stage_up,
     stage_down,
     stage_out,
-    active,
     grad_pre,
     sems,
     out_sems,
@@ -236,17 +235,14 @@
     back = (grad_active * slope).astype(low)
     grad_pre[...] = back
     sums_up[0] = jnp.sum(back.astype(wide), axis=0, keepdims=True)
-    gone = mm(active[...], down, 1, 0)
     came = mm(grad_pre[...], up, 1, 1)
 
     @pl.when(step == 0)
     def _():
-        out_sum[...] = gone
         back_sum[...] = came
 
     @pl.when(step > 0)
     def _():
-        out_sum[...] += gone
         back_sum[...] += came
 
     @pl.when(step >= 2)
@@ -272,7 +268,6 @@
         def finish(t, total):
             at = rows_of(t)
             keep = inside[at, :]
-            result[at, :] = (middle[at, :] + keep * (out_sum[at, :] + vectors[11:12, :])).astype(low)
             grad = back_sum[at, :]
             scaled = normal[at, :]
             mid = cotangent[at, :].astype(wide) + norm_back(
@@ -384,6 +379,46 @@
         await_bytes(stage.at[0], out_sems.at[0])
 
 
+def result_kernel(place, whole, active, middle, inside, vectors, result, w_down, total, sems):
+    step = pl.program_id(0)
+    steps = pl.num_programs(0)
+    rows, width = middle.shape
+    side = width // 128
+    high = 4 * side
+    per = CHUNK // 128
+    first_down = 4 * side * side + side * high
+
+    def fetch(index, slot):
+        start_blocks(
+            place, whole, w_down.at[slot], sems.at[slot], first_down, side, index * per, 0, per, side
+        )
+
+    @pl.when(step == 0)
+    def _():
+        total[...] = jnp.zeros_like(total)
+        fetch(0, 0)
+        fetch(1, 1)
+
+    slot = lax.rem(step, 2)
+    await_bytes(w_down.at[slot], sems.at[slot])
+    total[...] += mm(active[...], w_down[slot], 1, 0)
+
+    @pl.when(step + 2 < steps)
+    def _():
+        fetch(step + 2, slot)
+
+    @pl.when(step == steps - 1)
+    def _():
+        def finish(t, carry):
+            at = rows_of(t)
+            result[at, :] = (
+                middle[at, :] + inside[at, :] * (total[at, :] + vectors[11:12, :])
+            ).astype(low)
+            return carry
+
+        lax.fori_loop(0, tiles(rows), finish, 0)
+
+
 def input_kernel(
     place, whole, grad_project, patches, grad_middle, vectors, grad_input, sums, weight, grad_sum, sems
 ):
@@ -418,74 +453,6 @@
     for row in range(4):
         sums[row : row + 1, :] = found[row]
     sums[4:8, :] = jnp.zeros((4, width), wide)
-
-
-def full_dot(a, b, ca, cb):
-    return lax.dot_general(
-        a, b, (((ca,), (cb,)), ((), ())), precision=highest, preferred_element_type=wide
-    )
-
-
-def turn_kernel(named, grads, left, right, rotated, total):
-    s = pl.program_id(0)
-    block = jnp.where(named[s] > 0, grads[0].astype(wide), 0.0)
-    rotated[0] = full_dot(full_dot(left[0], block, 0, 0), right[0], 1, 0)
-
-    @pl.when(s == 0)
-    def _():
-        total[...] = jnp.zeros_like(total)
-
-    total[...] += jnp.sum(block * block)
-
-
-def adam_parts(gradient, first, second):
-    correction = 1.0 - beta**STEP
-    new_first = beta * first + (1.0 - beta) * gradient
-    new_second = beta * second + (1.0 - beta) * gradient * gradient
-    direction = new_first / correction / (jnp.sqrt(new_second / correction) + adam_eps)
-    return new_first, new_second, direction
-
-
-def adam_kernel(
-    count,
-    total,
-    rotated,
-    master,
-    first,
-    second,
-    left,
-    right,
-    vector_sum,
-    vectors,
-    vector_first,
-    vector_second,
-    new_master,
-    new_first,
-    new_second,
-    clip,
-    new_vectors,
-    new_vector_first,
-    new_vector_second,
-    factor,
-):
-    @pl.when(pl.program_id(0) == 0)
-    def _():
-        grads = vector_sum[...]
-        norm = jnp.sqrt(total[0:1, 0:1] + jnp.sum(grads * grads))
-        clip[...] = norm
-        factor[...] = jnp.minimum(1.0, 0.5 * math.sqrt(count) / norm)
-        ahead, squares, way = adam_parts(
-            factor[...] * grads, vector_first[...], vector_second[...]
-        )
-        new_vector_first[...] = ahead
-        new_vector_second[...] = squares
-        new_vectors[...] = vectors[...] - rate_vector * way
-
-    ahead, squares, way = adam_parts(factor[...] * rotated[0], first[0], second[0])
-    new_first[0] = ahead
-    new_second[0] = squares
-    update = full_dot(full_dot(left[0], way, 1, 0), right[0], 1, 1)
-    new_master[0] = master[0] - rate_matrix * (update + decay_weight * master[0])
 
 
 VMEM_LIMIT = 60 * 1024 * 1024
@@ -566,7 +533,7 @@
         )
         place = spot * held + owners % held
     mine = me * held + jnp.arange(held, dtype=jnp.int32)
-    named = jnp.any(mine[:, None] == owners[None, :], axis=1).astype(jnp.int32)
+    named = jnp.any(mine[:, None] == owners[None, :], axis=1)
 
     counts = lengths[0]
     ends = jnp.cumsum(counts)
@@ -618,7 +585,7 @@
     )(project, project, project, image_query, image_keys)
 
     steps = hidden // CHUNK
-    result, grad_middle, grad_mixed, sums_two, sums_up, buffer = pl.pallas_call(
+    middle, active, grad_middle, grad_mixed, sums_two, sums_up, buffer = pl.pallas_call(
         feed_kernel,
         grid_spec=pltpu.PrefetchScalarGridSpec(
             num_scalar_prefetch=1,
@@ -634,6 +601,7 @@
             ],
             out_specs=[
                 full((rows, width)),
+                pl.BlockSpec((rows, CHUNK), lambda c, *_: (0, c)),
                 full((rows, width)),
                 full((rows, width)),
                 full((8, width)),
@@ -644,7 +612,6 @@
                 pltpu.VMEM((width, width), low),
                 pltpu.VMEM((2, width, CHUNK), low),
                 pltpu.VMEM((2, CHUNK, width), low),
-                pltpu.VMEM((rows, width), wide),
                 pltpu.VMEM((rows, width), wide),
                 pltpu.VMEM((rows, 1), wide),
                 pltpu.VMEM((rows, width), low),
@@ -656,13 +623,13 @@
                 pltpu.VMEM((2, CHUNK, width), low),
                 pltpu.VMEM((width, width), low),
                 pltpu.VMEM((rows, CHUNK), low),
-                pltpu.VMEM((rows, CHUNK), low),
                 pltpu.SemaphoreType.DMA((5,)),
                 pltpu.SemaphoreType.DMA((5,)),
             ],
         ),
         out_shape=[
-            shape((rows, width), low),
+            shape((rows, width), wide),
+            shape((rows, hidden), low),
             shape((rows, width), wide),
             shape((rows, width), low),
             shape((8, width), wide),
@@ -750,62 +717,61 @@
         compiler_params=params(),
         name="input",
     )(place, whole, grad_project, patches, grad_middle, vectors)
+    result = pl.pallas_call(
+        result_kernel,
+        grid_spec=pltpu.PrefetchScalarGridSpec(
+            num_scalar_prefetch=1,
+            grid=(steps,),
+            in_specs=[
+                whole_spec(),
+                pl.BlockSpec((rows, CHUNK), lambda c, *_: (0, c)),
+                full((rows, width)),
+                full((rows, 1)),
+                full((12, width)),
+            ],
+            out_specs=full((rows, width)),
+            scratch_shapes=[
+                pltpu.VMEM((2, CHUNK, width), low),
+                pltpu.VMEM((rows, width), wide),
+                pltpu.SemaphoreType.DMA((2,)),
+            ],
+        ),
+        out_shape=shape((rows, width), low),
+        compiler_params=params(),
+        name="result",
+    )(place, whole, active, middle, inside, vectors)
     vector_grad = jnp.concatenate(
         [sums_one[0:4], sums_two[0:3], sums_up.reshape(4, width), sums_two[3:4]], axis=0
     )
     vector_sum = everywhere(vector_grad)
 
-    owned, vector_sum = lax.optimization_barrier((owned, vector_sum))
-
-    def block():
-        return pl.BlockSpec((1, size, size), lambda s, *_: (s, 0, 0))
-
-    rotated, total = pl.pallas_call(
-        turn_kernel,
-        grid_spec=pltpu.PrefetchScalarGridSpec(
-            num_scalar_prefetch=1,
-            grid=(held,),
-            in_specs=[block(), block(), block()],
-            out_specs=[block(), full((8, 128))],
-        ),
-        out_shape=[shape((held, size, size), wide), shape((8, 128), wide)],
-        compiler_params=params(),
-        name="turn",
-    )(named, owned, left_basis, right_basis)
-    total = everywhere(total)
-
+    owned, vector_sum, result = lax.optimization_barrier((owned, vector_sum, result))
+
+    owned = jnp.where(named[:, None, None], owned.astype(wide), 0.0)
+    total_blocks = everywhere(jnp.broadcast_to(jnp.sum(owned * owned), (8, 128)))[0, 0]
+    clip_norm = jnp.sqrt(total_blocks + jnp.sum(vector_sum * vector_sum))
     count = owners.shape[0] * size * size + vectors.shape[0] * width
-    small = full((12, width))
-    new_master, new_first, new_second, clip, new_vectors, new_vector_first, new_vector_second = (
-        pl.pallas_call(
-            functools.partial(adam_kernel, count),
-            grid=(held,),
-            in_specs=[full((8, 128))] + [block() for _ in range(6)] + [small] * 4,
-            out_specs=[block(), block(), block(), full((1, 1)), small, small, small],
-            out_shape=[shape((held, size, size), wide)] * 3
-            + [shape((1, 1), wide)]
-            + [shape((12, width), wide)] * 3,
-            scratch_shapes=[pltpu.VMEM((1, 1), wide)],
-            compiler_params=params(),
-            name="adam",
-        )(
-            total,
-            rotated,
-            master,
-            first_moment,
-            second_moment,
-            left_basis,
-            right_basis,
-            vector_sum,
-            vectors,
-            vector_first,
-            vector_second,
-        )
-    )
+    factor = jnp.minimum(1.0, 0.5 * math.sqrt(count) / clip_norm)
+    turned = jnp.einsum("sji,sjk->sik", left_basis, owned, precision=highest)
+    rotated = factor * jnp.einsum("sik,skl->sil", turned, right_basis, precision=highest)
+    new_first = beta * first_moment + (1.0 - beta) * rotated
+    new_second = beta * second_moment + (1.0 - beta) * rotated * rotated
+    correction = 1.0 - beta**STEP
+    direction = new_first / correction / (jnp.sqrt(new_second / correction) + adam_eps)
+    back_turn = jnp.einsum("sij,sjk->sik", left_basis, direction, precision=highest)
+    update = jnp.einsum("sik,slk->sil", back_turn, right_basis, precision=highest)
+    new_master = master - rate_matrix * (update + decay_weight * master)
+    vector_clip = factor * vector_sum
+    new_vector_first = beta * vector_first + (1.0 - beta) * vector_clip
+    new_vector_second = beta * vector_second + (1.0 - beta) * vector_clip * vector_clip
+    vector_step = (
+        new_vector_first / correction / (jnp.sqrt(new_vector_second / correction) + adam_eps)
+    )
+    new_vectors = vectors - rate_vector * vector_step
     return (
         result,
         grad_input,
-        clip.reshape(()),
+        clip_norm,
         new_master,
         new_first,
         new_second,

time: 379 us -> 361 us (0.953)
  Pallas kernels: 161 us -> 143 us
  waiting for transfers between devices: 170 us -> 156 us
  matrix products: 0 us -> 9.78 us
    pallas_call x2 -> x1, Pallas kernels: 26.3 us -> 13.1 us  [shards(): pl.pallas_call(result_kernel, grid_spec=pltpu.PrefetchScalarGridSpec(num_...]
    dot_general x0 -> x4, matrix products: none -> 9.78 us  [the longest x1 2.96 us: shards(): jnp.einsum('sik,slk->sil', back_turn, right_basis, precision=highest)]
    reduce_scatter x1, waiting for transfers between devices: 71.4 us -> 62.3 us  [scatter(): lax.psum_scatter(value, AXES, scatter_dimension=0, tiled=True, axis_index...]
    pallas_call x1, Pallas kernels: 58.3 us -> 53.1 us  [shards(): pl.pallas_call(feed_kernel, grid_spec=pltpu.PrefetchScalarGridSpec(num_sc...]
    ppermute x10, waiting for transfers between devices: 20.5 us -> 16 us  [everywhere(): lax.ppermute(value, AXES, [(d, d ^ step) for d in range(devices)])]
  transfers between devices with their start and end apart: 12 -> 12, of which waited for: 12 -> 10; matrix products, arithmetic and copies ran while one was open for 3% -> 4% of each run, Pallas kernels for 4% -> 7%
where the time goes in v3:
time: 361 us; the launch traced here: 360 us
  waiting for transfers between devices  156 us (43%)
  Pallas kernels  143 us (40%)
  between operations  16.8 us (5%)
  starting transfers between devices  14.9 us (4%)
  other arithmetic  14.3 us (4%)
  matrix products  9.78 us (3%)
  local copies, waits for them, and re-layouts  5.05 us (1%)
    all_gather x1, waiting for transfers between devices, gather(): lax.all_gather(value, AXES, axis=0, tiled=True, axis_index_groups=groups)  78.1 us
    reduce_scatter x1, waiting for transfers between devices, scatter(): lax.psum_scatter(value, AXES, scatter_dimension=0, tiled=True, axis_index...  62.3 us
    pallas_call x1, Pallas kernels, shards(): pl.pallas_call(feed_kernel, grid_spec=pltpu.PrefetchScalarGridSpec(num_sc...  53.1 us
    pallas_call x1, Pallas kernels, shards(): pl.pallas_call(back_kernel, grid_spec=pltpu.PrefetchScalarGridSpec(num_sc...  33.7 us
    pallas_call x1, Pallas kernels, shards(): pl.pallas_call(attend_kernel, grid=(pairs,), in_specs=[column(0), column(...  18.7 us
    ppermute x10, waiting for transfers between devices, everywhere(): lax.ppermute(value, AXES, [(d, d ^ step) for d in range(devices)])  16 us
    ppermute x10, starting transfers between devices, everywhere(): lax.ppermute(value, AXES, [(d, d ^ step) for d in range(devices)])  14.8 us
    pallas_call x1, Pallas kernels, shards(): pl.pallas_call(input_kernel, grid_spec=pltpu.PrefetchScalarGridSpec(num_s...  13.2 us
  transfers between devices with their start and end apart: 12, of which 10 were waited for; matrix products, arithmetic and copies ran while one was open for 4% of the time, Pallas kernels for 7%

profile of v3, /device:TPU:0, one launch (start us, length us, event | category | flops | bytes accessed | tf_op | source)
XLA Modules:
  0.0 360.1 jit_solution(8710416853907992776)
XLA Ops:
  7.2 2.1 convert_element_type.18
  13.8 1.4 fusion.16.inside
  15.2 1.2 fusion.19.place
  18.8 78.1 %all-gather.2.cloned.1.call-done.whole = bf16[448,128,128]{2,1,0:T(8,128)(2,1)} async-done(((bf16[14,128,128]{2,1,0:T(8,128)(2,1)}), bf16[448,128,128]{2,1,0:T(8,128)(2,1)}) %all-gather.2.cloned.1.call-update) | async-done | bytes 14680080 | tf_op jit(solution)/shard_map/all_gather | solution.py:504
  96.9 11.0 %qkv.1.query.keys.values = bf16[784,2304]{1,0:T(8,128)(2,1)} custom-call(s32[432]{0:T(512)} %fusion.19.place, bf16[448,128,128]{2,1,0:T(8,128)(2,1)} %all-gather.2.cloned.1.call-done.whole, bf16[784,768]{1,0:T(8,128)(2,1)} %patches.7, f32[12,768]{1,0:T(8,128)} %vectors.9), custom_call_target="tpu_custom_call" | custom-call | tf_op jit(solution)/shard_map/qkv/pallas_call | solution.py:549
  107.9 18.7 %attend.1 = (bf16[784,768]{1,0:T(8,128)(2,1)}, bf16[12,784,784]{2,1,0:T(8,128)(2,1)}) custom-call(bf16[784,2304]{1,0:T(8,128)(2,1)} %qkv.1.query.keys.values, bf16[784,2304]{1,0:T(8,128)(2,1)} %qkv.1.query.keys.values, bf16[784,2304]{1,0:T(8,128)(2,1)} %qkv.1.query.keys.values, bf16[784,128]{1,0:T(8,128)(2,1)} %select_convert_fusion.image_query, ...), custom_call_target="tpu_custom_call" | custom-call | tf_op jit(solution)/shard_map/attend/pallas_call | solution.py:570
  126.6 53.1 %feed.1 = (f32[784,768]{1,0:T(8,128)}, bf16[784,3072]{1,0:T(8,128)(2,1)}, f32[784,768]{1,0:T(8,128)}, bf16[784,768]{1,0:T(8,128)(2,1)}, f32[8,768]{1,0:T(8,128)}...) custom-call(s32[432]{0:T(512)} %fusion.19.place, bf16[448,128,128]{2,1,0:T(8,128)(2,1)} %all-gather.2.cloned.1.call-done.whole, ...), custom_call_target="tpu_custom_call" | custom-call | tf_op jit(solution)/shard_map/feed/pallas_call | solution.py:588
  179.7 33.7 %back.1 = (bf16[3,784,768]{2,1,0:T(8,128)(2,1)}, bf16[448,128,128]{2,1,0:T(8,128)(2,1)}) custom-call(s32[432]{0:T(512)} %fusion.19.place, bf16[448,128,128]{2,1,0:T(8,128)(2,1)} %get-tuple-element.26.held, bf16[784,2304]{1,0:T(8,128)(2,1)} %qkv.1.query.keys.values, bf16[784,2304]{1,0:T(8,128)(2,1)} %qkv.1.query.keys.values, ...), custom_call_target="tpu_custom_call", output_to_operand_aliasing={{1}: (1, {})} | custom-call | tf_op jit(solution)/shard_map/back/pallas_call | solution.py:652
  214.2 13.2 %input.1 = (bf16[784,768]{1,0:T(8,128)(2,1)}, f32[8,768]{1,0:T(8,128)}) custom-call(s32[432]{0:T(512)} %fusion.19.place, bf16[448,128,128]{2,1,0:T(8,128)(2,1)} %all-gather.2.cloned.1.call-done.whole, bf16[3,784,768]{2,1,0:T(8,128)(2,1)} %get-tuple-element.30.grad_project, bf16[784,768]{1,0:T(8,128)(2,1)} %patches.7, ...), custom_call_target="tpu_custom_call" | custom-call | tf_op jit(solution)/shard_map/input/pallas_call | solution.py:697
  228.6 1.0 collective-permute-done
  229.6 1.5 collective-permute-start.1
  231.1 2.7 collective-permute-done.1
  233.8 2.0 collective-permute-start.2
  235.9 2.1 collective-permute-done.2
  238.0 1.5 collective-permute-start.3
  239.5 3.1 collective-permute-done.3
  242.6 2.4 collective-permute-start.4
  245.2 13.1 %result.1 = bf16[784,768]{1,0:T(8,128)(2,1)} custom-call(s32[432]{0:T(512)} %fusion.19.place, bf16[448,128,128]{2,1,0:T(8,128)(2,1)} %all-gather.2.cloned.1.call-done.whole, bf16[784,3072]{1,0:T(8,128)(2,1)} %get-tuple-element.35.active, f32[784,768]{1,0:T(8,128)} %get-tuple-element.36.middle, f32[784,1]{1,0:T(8,128)} %fusion.16.inside, f32[12,768]{1,0:T(8,128)} %vectors.9), custom_call_target="tpu_custom_call" | custom-call | tf_op jit(solution)/shard_map/result/pallas_call | solution.py:720
  258.4 62.3 %reduce-scatter.2.cloned.1.call-done = bf16[14,128,128]{2,1,0:T(8,128)(2,1)} async-done(((bf16[448,128,128]{2,1,0:T(8,128)(2,1)}), bf16[14,128,128]{2,1,0:T(8,128)(2,1)}) %reduce-scatter.2.cloned.1.call-update) | async-done | bytes 458768 | tf_op jit(solution)/shard_map/reduce_scatter | solution.py:507
  320.7 1.9 multiply_reduce_fusion
  323.5 1.1 collective-permute-done.5
  325.2 1.6 collective-permute-start.6
  326.8 2.1 collective-permute-done.6
  329.5 1.7 collective-permute-start.7
  331.2 2.0 collective-permute-done.7
  333.2 1.5 collective-permute-start.8
  334.7 2.7 fusion.9
  337.4 2.1 collective-permute-start.9
  340.1 1.8 collective-permute-done.9
  343.9 2.7 multiply_add_fusion
  346.6 1.5 fusion.3
  348.5 3.0 fusion.1
  (63 shorter events, 13.2 us)
Async XLA Ops:
  7.2 336.7 %copy-start = (f32[14,128,128]{2,1,0:T(8,128)S(1)}, f32[14,128,128]{2,1,0:T(8,128)}, u32[]{:S(2)}) copy-start(f32[14,128,128]{2,1,0:T(8,128)} %param.21) | copy-start | bytes 2752516
  7.2 89.7 %all-gather.2.cloned.1.call-start = ((), (), s32[]{:S(2)}) async-start(), calls=%async_computation.1 | async-start | bytes 15138816 | tf_op jit(solution)/shard_map/all_gather | solution.py:504
  9.4 311.4 %reduce-scatter.2.cloned.1.call-start = ((), (), s32[]{:S(2)}) async-start(), calls=%async_computation.2 | async-start | bytes 15138816 | tf_op jit(solution)/shard_map/reduce_scatter | solution.py:507
  213.4 0.7 copy-start.10
  214.2 14.0 %copy-start.9 = (f32[6,1,512]{2,1,0:T(1,128)S(1)}, f32[6,1,512]{2,1,0:T(1,128)}, u32[]{:S(2)}) copy-start(f32[6,1,512]{2,1,0:T(1,128)} %get-tuple-element.34) | copy-start | bytes 36868
  214.2 30.9 %copy-start.8 = (s32[432]{0:T(512)S(1)}, s32[432]{0:T(512)}, u32[]{:S(2)}) copy-start(s32[432]{0:T(512)} %param.16) | copy-start | bytes 5188
  228.3 1.3 collective-permute-start
  229.6 4.2 %collective-permute-start.1 = (f32[12,768]{1,0:T(8,128)S(1)}, f32[12,768]{1,0:T(8,128)S(1)}, u32[]{:S(2)}, u32[]{:S(2)}) collective-permute-start(f32[12,768]{1,0:T(8,128)S(1)} %fusion.24), channel_id=1, source_target_pairs={{0,2},{1,3},{2,0},{3,1},{4,6},{5,7},{6,4},{7,5},{8,10},{9,11},{10,... | collective-permute-start | bytes 110600 | tf_op jit(solution)/shard_map/ppermute | solution.py:514
  233.8 4.2 %collective-permute-start.2 = (f32[12,768]{1,0:T(8,128)S(1)}, f32[12,768]{1,0:T(8,128)S(1)}, u32[]{:S(2)}, u32[]{:S(2)}) collective-permute-start(f32[12,768]{1,0:T(8,128)S(1)} %add.88), channel_id=1, source_target_pairs={{0,4},{1,5},{2,6},{3,7},{4,0},{5,1},{6,2},{7,3},{8,12},{9,13},{10,... | collective-permute-start | bytes 110600 | tf_op jit(solution)/shard_map/ppermute | solution.py:514
  238.0 4.6 %collective-permute-start.3 = (f32[12,768]{1,0:T(8,128)S(1)}, f32[12,768]{1,0:T(8,128)S(1)}, u32[]{:S(2)}, u32[]{:S(2)}) collective-permute-start(f32[12,768]{1,0:T(8,128)S(1)} %add.89), channel_id=1, source_target_pairs={{0,8},{1,9},{2,10},{3,11},{4,12},{5,13},{6,14},{7,15},{8,0},{9,1},... | collective-permute-start | bytes 110600 | tf_op jit(solution)/shard_map/ppermute | solution.py:514
  242.6 15.8 %collective-permute-start.4 = (f32[12,768]{1,0:T(8,128)S(1)}, f32[12,768]{1,0:T(8,128)S(1)}, u32[]{:S(2)}, u32[]{:S(2)}) collective-permute-start(f32[12,768]{1,0:T(8,128)S(1)} %add.90), channel_id=1, source_target_pairs={{0,16},{1,17},{2,18},{3,19},{4,20},{5,21},{6,22},{7,23},{8,24},{9,... | collective-permute-start | bytes 110600 | tf_op jit(solution)/shard_map/ppermute | solution.py:514
  245.2 89.5 %copy-start.3 = (f32[14,128,128]{2,1,0:T(8,128)S(1)}, f32[14,128,128]{2,1,0:T(8,128)}, u32[]{:S(2)}) copy-start(f32[14,128,128]{2,1,0:T(8,128)} %param.20) | copy-start | bytes 2752516
  323.3 1.2 collective-permute-start.5
  325.2 3.7 %collective-permute-start.6 = (f32[8,128]{1,0:T(8,128)S(1)}, f32[8,128]{1,0:T(8,128)S(1)}, u32[]{:S(2)}, u32[]{:S(2)}) collective-permute-start(f32[8,128]{1,0:T(8,128)S(1)} %broadcast_add_fusion), channel_id=1, source_target_pairs={{0,2},{1,3},{2,0},{3,1},{4,6},{5,7},{6,4},{7,5},{8,10},{9,11},{10,... | collective-permute-start | bytes 12296 | tf_op jit(solution)/shard_map/ppermute | solution.py:514
  329.5 3.7 %collective-permute-start.7 = (f32[8,128]{1,0:T(8,128)S(1)}, f32[8,128]{1,0:T(8,128)S(1)}, u32[]{:S(2)}, u32[]{:S(2)}) collective-permute-start(f32[8,128]{1,0:T(8,128)S(1)} %fusion.32), channel_id=1, source_target_pairs={{0,4},{1,5},{2,6},{3,7},{4,0},{5,1},{6,2},{7,3},{8,12},{9,13},{10,... | collective-permute-start | bytes 12296 | tf_op jit(solution)/shard_map/ppermute | solution.py:514
  333.2 4.2 %collective-permute-start.8 = (f32[8,128]{1,0:T(8,128)S(1)}, f32[8,128]{1,0:T(8,128)S(1)}, u32[]{:S(2)}, u32[]{:S(2)}) collective-permute-start(f32[8,128]{1,0:T(8,128)S(1)} %add.97), channel_id=1, source_target_pairs={{0,8},{1,9},{2,10},{3,11},{4,12},{5,13},{6,14},{7,15},{8,0},{9,1},... | collective-permute-start | bytes 12296 | tf_op jit(solution)/shard_map/ppermute | solution.py:514
  337.4 4.6 %collective-permute-start.9 = (f32[8,128]{1,0:T(8,128)S(1)}, f32[8,128]{1,0:T(8,128)S(1)}, u32[]{:S(2)}, u32[]{:S(2)}) collective-permute-start(f32[8,128]{1,0:T(8,128)S(1)} %add.98), channel_id=1, source_target_pairs={{0,16},{1,17},{2,18},{3,19},{4,20},{5,21},{6,22},{7,23},{8,24},{9,... | collective-permute-start | bytes 12296 | tf_op jit(solution)/shard_map/ppermute | solution.py:514
  346.6 4.8 %copy-start.4 = (f32[14,128,128]{2,1,0:T(8,128)}, f32[14,128,128]{2,1,0:T(8,128)S(1)}, u32[]{:S(2)}) copy-start(f32[14,128,128]{2,1,0:T(8,128)S(1)} %get-tuple-element.44) | copy-start | bytes 2752516
  346.6 4.8 %copy-start.5 = (f32[14,128,128]{2,1,0:T(8,128)}, f32[14,128,128]{2,1,0:T(8,128)S(1)}, u32[]{:S(2)}) copy-start(f32[14,128,128]{2,1,0:T(8,128)S(1)} %get-tuple-element.45) | copy-start | bytes 2752516
  346.6 1.8 copy-start.1
  348.5 3.0 copy-start.2
  348.5 3.0 copy-start.6
  348.5 3.0 copy-start.7
Sparse Core Ops, SparseCore 0:
  10.2 86.7 all-gather.1
  213.6 107.1 reduce-scatter.1

commit v4 on v3

--- a/solution.py
+++ b/solution.py
@@ -57,33 +57,29 @@
 
 
 def start_blocks(place, whole, target, sem, first, across, row0, col0, height, breadth):
-    def one(index, carry):
-        r = index // breadth
-        c = index % breadth
-        slot = place[first + (row0 + r) * across + col0 + c]
-        pltpu.make_async_copy(
-            whole.at[slot],
-            target.at[pl.ds(pl.multiple_of(r * 128, 128), 128), pl.ds(pl.multiple_of(c * 128, 128), 128)],
-            sem,
-        ).start()
+    def one(r, carry):
+        at = first + (row0 + r) * across + col0
+        down = pl.ds(pl.multiple_of(r * 128, 128), 128)
+        for c in range(breadth):
+            pltpu.make_async_copy(
+                whole.at[place[at + c]], target.at[down, pl.ds(c * 128, 128)], sem
+            ).start()
         return carry
 
-    lax.fori_loop(0, height * breadth, one, 0)
+    lax.fori_loop(0, height, one, 0)
 
 
 def store_blocks(place, source, buffer, sem, first, across, row0, col0, height, breadth):
-    def one(index, carry):
-        r = index // breadth
-        c = index % breadth
-        slot = place[first + (row0 + r) * across + col0 + c]
-        pltpu.make_async_copy(
-            source.at[pl.ds(pl.multiple_of(r * 128, 128), 128), pl.ds(pl.multiple_of(c * 128, 128), 128)],
-            buffer.at[slot],
-            sem,
-        ).start()
+    def one(r, carry):
+        at = first + (row0 + r) * across + col0
+        down = pl.ds(pl.multiple_of(r * 128, 128), 128)
+        for c in range(breadth):
+            pltpu.make_async_copy(
+                source.at[down, pl.ds(c * 128, 128)], buffer.at[place[at + c]], sem
+            ).start()
         return carry
 
-    lax.fori_loop(0, height * breadth, one, 0)
+    lax.fori_loop(0, height, one, 0)
 
 
 def await_bytes(ref, sem):
@@ -221,37 +217,30 @@
 
         sums[3:4, :] = lax.fori_loop(0, tiles(rows), norm, jnp.zeros((1, width), wide))
         second_t[...] = second[...].T
+        back_sum[...] = jnp.zeros_like(back_sum)
 
     slot = lax.rem(step, 2)
     await_bytes(w_up.at[slot], sems.at[slot])
     await_bytes(w_down.at[slot], sems.at[2 + slot])
-    up = w_up[slot]
-    down = w_down[slot]
-    pre = mm(second[...], up, 1, 0) + bias_up[0]
-    grad_active = mm(grad_two[...], down, 1, 1)
-    half = 0.5 * (1.0 + lax.erf(pre * math.sqrt(0.5)))
-    active[...] = (pre * half).astype(low)
-    slope = half + pre * (jnp.exp(-0.5 * pre * pre) * (1.0 / math.sqrt(2.0 * math.pi)))
-    back = (grad_active * slope).astype(low)
-    grad_pre[...] = back
-    sums_up[0] = jnp.sum(back.astype(wide), axis=0, keepdims=True)
-    came = mm(grad_pre[...], up, 1, 1)
-
-    @pl.when(step == 0)
-    def _():
-        back_sum[...] = came
-
-    @pl.when(step > 0)
-    def _():
-        back_sum[...] += came
 
     @pl.when(step >= 2)
     def _():
         await_bytes(stage_up.at[slot], out_sems.at[slot])
         await_bytes(stage_down.at[slot], out_sems.at[2 + slot])
 
-    stage_up[slot] = mm(second_t[...], grad_pre[...], 1, 0).astype(low)
-    stage_down[slot] = mm(active[...], grad_two[...], 0, 0).astype(low)
+    parts = [slice(h * (CHUNK // 2), (h + 1) * (CHUNK // 2)) for h in range(2)]
+    pres = [mm(second[...], w_up[slot, :, p], 1, 0) + bias_up[0, :, p] for p in parts]
+    grads = [mm(grad_two[...], w_down[slot, p, :], 1, 1) for p in parts]
+    for p, pre, grad in zip(parts, pres, grads):
+        half = 0.5 * (1.0 + lax.erf(pre * math.sqrt(0.5)))
+        active[:, p] = (pre * half).astype(low)
+        slope = half + pre * (jnp.exp(-0.5 * pre * pre) * (1.0 / math.sqrt(2.0 * math.pi)))
+        back = (grad * slope).astype(low)
+        grad_pre[:, p] = back
+        sums_up[0, :, p] = jnp.sum(back.astype(wide), axis=0, keepdims=True)
+        stage_up[slot, :, p] = mm(second_t[...], grad_pre[:, p], 1, 0).astype(low)
+        stage_down[slot, p, :] = mm(active[:, p], grad_two[...], 0, 0).astype(low)
+    back_sum[...] += mm(grad_pre[...], w_up[slot], 1, 1)
     store_blocks(
         place, stage_up.at[slot], buffer, out_sems.at[slot], first_up, high, 0, step * per, side, per
     )
@@ -748,7 +737,8 @@
     owned, vector_sum, result = lax.optimization_barrier((owned, vector_sum, result))
 
     owned = jnp.where(named[:, None, None], owned.astype(wide), 0.0)
-    total_blocks = everywhere(jnp.broadcast_to(jnp.sum(owned * owned), (8, 128)))[0, 0]
+    squares = jnp.broadcast_to(jnp.sum(owned * owned), (devices, 128))
+    total_blocks = jnp.sum(lax.all_to_all(squares, AXES, 0, 0, tiled=True)[:, 0])
     clip_norm = jnp.sqrt(total_blocks + jnp.sum(vector_sum * vector_sum))
     count = owners.shape[0] * size * size + vectors.shape[0] * width
     factor = jnp.minimum(1.0, 0.5 * math.sqrt(count) / clip_norm)

time: 361 us -> 341 us (0.945)
  Pallas kernels: 143 us -> 127 us
    pallas_call x1, Pallas kernels: 53.1 us -> 41.1 us  [shards(): pl.pallas_call(feed_kernel, grid_spec=pltpu.PrefetchScalarGridSpec(num_sc...]
    ppermute x10 -> x5, starting transfers between devices: 14.8 us -> 6.39 us  [everywhere(): lax.ppermute(value, AXES, [(d, d ^ step) for d in range(devices)])]
    ppermute x10 -> x5, waiting for transfers between devices: 16 us -> 10.2 us  [everywhere(): lax.ppermute(value, AXES, [(d, d ^ step) for d in range(devices)])]
    all_to_all x0 -> x1, starting transfers between devices: none -> 5.31 us  [shards(): lax.all_to_all(squares, AXES, 0, 0, tiled=True)[:, 0]]
  transfers between devices with their start and end apart: 12 -> 8, of which waited for: 10 -> 7; matrix products, arithmetic and copies ran while one was open for 4% -> 4% of each run, Pallas kernels for 7% -> 7%
where the time goes in v4:
time: 341 us; the launch traced here: 340 us
  waiting for transfers between devices  155 us (45%)
  Pallas kernels  127 us (37%)
  between operations  16.8 us (5%)
  other arithmetic  13.6 us (4%)
  starting transfers between devices  11.8 us (3%)
  matrix products  9.78 us (3%)
  local copies, waits for them, and re-layouts  5.15 us (2%)
    all_gather x1, waiting for transfers between devices, gather(): lax.all_gather(value, AXES, axis=0, tiled=True, axis_index_groups=groups)  78.1 us
    reduce_scatter x1, waiting for transfers between devices, scatter(): lax.psum_scatter(value, AXES, scatter_dimension=0, tiled=True, axis_index...  63.4 us
    pallas_call x1, Pallas kernels, shards(): pl.pallas_call(feed_kernel, grid_spec=pltpu.PrefetchScalarGridSpec(num_sc...  41.1 us
    pallas_call x1, Pallas kernels, shards(): pl.pallas_call(back_kernel, grid_spec=pltpu.PrefetchScalarGridSpec(num_sc...  32.5 us
    pallas_call x1, Pallas kernels, shards(): pl.pallas_call(attend_kernel, grid=(pairs,), in_specs=[column(0), column(...  18.7 us
    pallas_call x1, Pallas kernels, shards(): pl.pallas_call(input_kernel, grid_spec=pltpu.PrefetchScalarGridSpec(num_s...  13 us
    pallas_call x1, Pallas kernels, shards(): pl.pallas_call(result_kernel, grid_spec=pltpu.PrefetchScalarGridSpec(num_...  12.3 us
    ppermute x5, waiting for transfers between devices, everywhere(): lax.ppermute(value, AXES, [(d, d ^ step) for d in range(devices)])  10.2 us
  transfers between devices with their start and end apart: 8, of which 7 were waited for; matrix products, arithmetic and copies ran while one was open for 4% of the time, Pallas kernels for 7%

profile of v4, /device:TPU:0, one launch (start us, length us, event | category | flops | bytes accessed | tf_op | source)
XLA Modules:
  0.0 339.7 jit_solution(12566364040590892140)
XLA Ops:
  7.2 2.1 convert_element_type.18
  9.4 0.8 reduce-window.4
  10.8 0.8 slice.20
  13.0 0.7 select_reduce_fusion
  13.8 1.4 fusion.16.inside
  15.2 1.3 fusion.19.place
  17.2 0.9 fusion.15.image_keys
  18.0 0.9 select_convert_fusion.image_query
  18.9 78.1 %all-gather.2.cloned.1.call-done.whole = bf16[448,128,128]{2,1,0:T(8,128)(2,1)} async-done(((bf16[14,128,128]{2,1,0:T(8,128)(2,1)}), bf16[448,128,128]{2,1,0:T(8,128)(2,1)}) %all-gather.2.cloned.1.call-update) | async-done | bytes 14680080 | tf_op jit(solution)/shard_map/all_gather | solution.py:493
  96.9 9.7 %qkv.1.query.keys.values = bf16[784,2304]{1,0:T(8,128)(2,1)} custom-call(s32[432]{0:T(512)} %fusion.19.place, bf16[448,128,128]{2,1,0:T(8,128)(2,1)} %all-gather.2.cloned.1.call-done.whole, bf16[784,768]{1,0:T(8,128)(2,1)} %patches.7, f32[12,768]{1,0:T(8,128)} %vectors.9), custom_call_target="tpu_custom_call" | custom-call | tf_op jit(solution)/shard_map/qkv/pallas_call | solution.py:538
  106.6 18.7 %attend.1 = (bf16[784,768]{1,0:T(8,128)(2,1)}, bf16[12,784,784]{2,1,0:T(8,128)(2,1)}) custom-call(bf16[784,2304]{1,0:T(8,128)(2,1)} %qkv.1.query.keys.values, bf16[784,2304]{1,0:T(8,128)(2,1)} %qkv.1.query.keys.values, bf16[784,2304]{1,0:T(8,128)(2,1)} %qkv.1.query.keys.values, bf16[784,128]{1,0:T(8,128)(2,1)} %select_convert_fusion.image_query, ...), custom_call_target="tpu_custom_call" | custom-call | tf_op jit(solution)/shard_map/attend/pallas_call | solution.py:559
  125.3 41.1 %feed.1 = (f32[784,768]{1,0:T(8,128)}, bf16[784,3072]{1,0:T(8,128)(2,1)}, f32[784,768]{1,0:T(8,128)}, bf16[784,768]{1,0:T(8,128)(2,1)}, f32[8,768]{1,0:T(8,128)}...) custom-call(s32[432]{0:T(512)} %fusion.19.place, bf16[448,128,128]{2,1,0:T(8,128)(2,1)} %all-gather.2.cloned.1.call-done.whole, ...), custom_call_target="tpu_custom_call" | custom-call | tf_op jit(solution)/shard_map/feed/pallas_call | solution.py:577
  166.5 32.5 %back.1 = (bf16[3,784,768]{2,1,0:T(8,128)(2,1)}, bf16[448,128,128]{2,1,0:T(8,128)(2,1)}) custom-call(s32[432]{0:T(512)} %fusion.19.place, bf16[448,128,128]{2,1,0:T(8,128)(2,1)} %get-tuple-element.26.held, bf16[784,2304]{1,0:T(8,128)(2,1)} %qkv.1.query.keys.values, bf16[784,2304]{1,0:T(8,128)(2,1)} %qkv.1.query.keys.values, ...), custom_call_target="tpu_custom_call", output_to_operand_aliasing={{1}: (1, {})} | custom-call | tf_op jit(solution)/shard_map/back/pallas_call | solution.py:641
  199.8 13.0 %input.1 = (bf16[784,768]{1,0:T(8,128)(2,1)}, f32[8,768]{1,0:T(8,128)}) custom-call(s32[432]{0:T(512)} %fusion.19.place, bf16[448,128,128]{2,1,0:T(8,128)(2,1)} %all-gather.2.cloned.1.call-done.whole, bf16[3,784,768]{2,1,0:T(8,128)(2,1)} %get-tuple-element.30.grad_project, bf16[784,768]{1,0:T(8,128)(2,1)} %patches.7, ...), custom_call_target="tpu_custom_call" | custom-call | tf_op jit(solution)/shard_map/input/pallas_call | solution.py:686
  213.9 1.0 collective-permute-done
  214.9 1.4 collective-permute-start.1
  216.3 3.1 collective-permute-done.1
  219.4 1.6 collective-permute-start.2
  221.0 2.5 collective-permute-done.2
  223.6 1.1 collective-permute-start.3
  224.7 3.5 %collective-permute-done.3 = f32[12,768]{1,0:T(8,128)S(1)} collective-permute-done((f32[12,768]{1,0:T(8,128)S(1)}, f32[12,768]{1,0:T(8,128)S(1)}, u32[]{:S(2)}, u32[]{:S(2)}) %collective-permute-start.3) | collective-permute-done | bytes 36896 | tf_op jit(solution)/shard_map/ppermute | solution.py:503
  228.2 2.0 collective-permute-start.4
  230.4 12.3 %result.1 = bf16[784,768]{1,0:T(8,128)(2,1)} custom-call(s32[432]{0:T(512)} %fusion.19.place, bf16[448,128,128]{2,1,0:T(8,128)(2,1)} %all-gather.2.cloned.1.call-done.whole, bf16[784,3072]{1,0:T(8,128)(2,1)} %get-tuple-element.35.active, f32[784,768]{1,0:T(8,128)} %get-tuple-element.36.middle, f32[784,1]{1,0:T(8,128)} %fusion.16.inside, f32[12,768]{1,0:T(8,128)} %vectors.9), custom_call_target="tpu_custom_call" | custom-call | tf_op jit(solution)/shard_map/result/pallas_call | solution.py:709
  242.8 63.4 %reduce-scatter.2.cloned.1.call-done = bf16[14,128,128]{2,1,0:T(8,128)(2,1)} async-done(((bf16[448,128,128]{2,1,0:T(8,128)(2,1)}), bf16[14,128,128]{2,1,0:T(8,128)(2,1)}) %reduce-scatter.2.cloned.1.call-update) | async-done | bytes 458768 | tf_op jit(solution)/shard_map/reduce_scatter | solution.py:496
  306.2 1.9 multiply_reduce_fusion
  308.1 1.3 broadcast_in_dim.56
  309.4 5.3 %all-to-all-start = ((f32[32,1,128]{2,1,0:T(1,128)}), f32[32,1,128]{2,1,0:T(1,128)S(1)}, u32[]{:S(2)}, u32[]{:S(2)}) async-start(f32[32,1,128]{2,1,0:T(1,128)} %broadcast_in_dim.56), calls=%async_computation.1 | async-start | bytes 32768 | tf_op jit(solution)/shard_map/all_to_all | solution.py:741
  314.7 2.7 fusion.9
  318.0 3.6 %all-to-all-done = f32[32,1,128]{2,1,0:T(1,128)S(1)} async-done(((f32[32,1,128]{2,1,0:T(1,128)}), f32[32,1,128]{2,1,0:T(1,128)S(1)}, u32[]{:S(2)}, u32[]{:S(2)}) %all-to-all-start) | async-done | bytes 16416 | tf_op jit(solution)/shard_map/all_to_all | solution.py:741
  323.5 2.7 multiply_add_fusion
  326.3 1.5 fusion.3
  328.1 3.0 fusion.1
  (50 shorter events, 7.1 us)
Async XLA Ops:
  7.2 316.3 %copy-start = (f32[14,128,128]{2,1,0:T(8,128)S(1)}, f32[14,128,128]{2,1,0:T(8,128)}, u32[]{:S(2)}) copy-start(f32[14,128,128]{2,1,0:T(8,128)} %param.21) | copy-start | bytes 2752516
  7.2 89.7 %all-gather.2.cloned.1.call-start = ((), (), s32[]{:S(2)}) async-start(), calls=%async_computation.2 | async-start | bytes 15138816 | tf_op jit(solution)/shard_map/all_gather | solution.py:493
  9.4 296.8 %reduce-scatter.2.cloned.1.call-start = ((), (), s32[]{:S(2)}) async-start(), calls=%async_computation.3 | async-start | bytes 15138816 | tf_op jit(solution)/shard_map/reduce_scatter | solution.py:496
  199.0 0.7 copy-start.10
  199.7 13.7 %copy-start.9 = (f32[6,1,512]{2,1,0:T(1,128)S(1)}, f32[6,1,512]{2,1,0:T(1,128)}, u32[]{:S(2)}) copy-start(f32[6,1,512]{2,1,0:T(1,128)} %get-tuple-element.34) | copy-start | bytes 36868
  199.7 30.4 %copy-start.8 = (s32[432]{0:T(512)S(1)}, s32[432]{0:T(512)}, u32[]{:S(2)}) copy-start(s32[432]{0:T(512)} %param.16) | copy-start | bytes 5188
  213.6 1.3 collective-permute-start
  214.9 4.5 %collective-permute-start.1 = (f32[12,768]{1,0:T(8,128)S(1)}, f32[12,768]{1,0:T(8,128)S(1)}, u32[]{:S(2)}, u32[]{:S(2)}) collective-permute-start(f32[12,768]{1,0:T(8,128)S(1)} %fusion.24), channel_id=1, source_target_pairs={{0,2},{1,3},{2,0},{3,1},{4,6},{5,7},{6,4},{7,5},{8,10},{9,11},{10,... | collective-permute-start | bytes 110600 | tf_op jit(solution)/shard_map/ppermute | solution.py:503
  219.4 4.2 %collective-permute-start.2 = (f32[12,768]{1,0:T(8,128)S(1)}, f32[12,768]{1,0:T(8,128)S(1)}, u32[]{:S(2)}, u32[]{:S(2)}) collective-permute-start(f32[12,768]{1,0:T(8,128)S(1)} %add.73), channel_id=1, source_target_pairs={{0,4},{1,5},{2,6},{3,7},{4,0},{5,1},{6,2},{7,3},{8,12},{9,13},{10,... | collective-permute-start | bytes 110600 | tf_op jit(solution)/shard_map/ppermute | solution.py:503
  223.6 4.6 %collective-permute-start.3 = (f32[12,768]{1,0:T(8,128)S(1)}, f32[12,768]{1,0:T(8,128)S(1)}, u32[]{:S(2)}, u32[]{:S(2)}) collective-permute-start(f32[12,768]{1,0:T(8,128)S(1)} %add.74), channel_id=1, source_target_pairs={{0,8},{1,9},{2,10},{3,11},{4,12},{5,13},{6,14},{7,15},{8,0},{9,1},... | collective-permute-start | bytes 110600 | tf_op jit(solution)/shard_map/ppermute | solution.py:503
  228.2 14.5 %collective-permute-start.4 = (f32[12,768]{1,0:T(8,128)S(1)}, f32[12,768]{1,0:T(8,128)S(1)}, u32[]{:S(2)}, u32[]{:S(2)}) collective-permute-start(f32[12,768]{1,0:T(8,128)S(1)} %add.75), channel_id=1, source_target_pairs={{0,16},{1,17},{2,18},{3,19},{4,20},{5,21},{6,22},{7,23},{8,24},{9,... | collective-permute-start | bytes 110600 | tf_op jit(solution)/shard_map/ppermute | solution.py:503
  230.4 84.3 %copy-start.3 = (f32[14,128,128]{2,1,0:T(8,128)S(1)}, f32[14,128,128]{2,1,0:T(8,128)}, u32[]{:S(2)}) copy-start(f32[14,128,128]{2,1,0:T(8,128)} %param.20) | copy-start | bytes 2752516
  309.4 12.2 %all-to-all-start = ((f32[32,1,128]{2,1,0:T(1,128)}), f32[32,1,128]{2,1,0:T(1,128)S(1)}, u32[]{:S(2)}, u32[]{:S(2)}) async-start(f32[32,1,128]{2,1,0:T(1,128)} %broadcast_in_dim.56), calls=%async_computation.1 | async-start | bytes 32768 | tf_op jit(solution)/shard_map/all_to_all | solution.py:741
  326.2 4.8 %copy-start.4 = (f32[14,128,128]{2,1,0:T(8,128)}, f32[14,128,128]{2,1,0:T(8,128)S(1)}, u32[]{:S(2)}) copy-start(f32[14,128,128]{2,1,0:T(8,128)S(1)} %get-tuple-element.44) | copy-start | bytes 2752516
  326.2 4.8 %copy-start.5 = (f32[14,128,128]{2,1,0:T(8,128)}, f32[14,128,128]{2,1,0:T(8,128)S(1)}, u32[]{:S(2)}) copy-start(f32[14,128,128]{2,1,0:T(8,128)S(1)} %get-tuple-element.45) | copy-start | bytes 2752516
  326.2 1.8 copy-start.1
  328.1 3.0 copy-start.2
  328.1 3.0 copy-start.6
  328.1 3.0 copy-start.7
Sparse Core Ops, SparseCore 0:
  10.2 86.7 all-gather.1
  199.1 106.9 reduce-scatter.1

commit v5 on v4

--- a/solution.py
+++ b/solution.py
@@ -97,21 +97,28 @@
     return pl.ds(pl.multiple_of(t * TILE, 16), TILE)
 
 
-def qkv_kernel(place, whole, patches, vectors, project, weight, normed, sems):
+def ready_kernel(patches, cotangent, inside, vectors, normed, normed_t, grad_two, bias_down):
     rows, width = patches.shape
+
+    def norm(t, total):
+        at = rows_of(t)
+        normal, _ = normal_parts(patches[at, :].astype(wide))
+        normed[at, :] = (normal * vectors[0:1, :] + vectors[1:2, :]).astype(low)
+        two = (inside[at, :] * cotangent[at, :].astype(wide)).astype(low)
+        grad_two[at, :] = two
+        return total + jnp.sum(two.astype(wide), axis=0, keepdims=True)
+
+    bias_down[...] = lax.fori_loop(0, tiles(rows), norm, jnp.zeros((1, width), wide))
+    normed_t[...] = normed[...].T
+
+
+def qkv_kernel(place, whole, normed, vectors, project, weight, sems):
+    rows, width = normed.shape
     side = width // 128
     for part in range(3):
         start_blocks(
             place, whole, weight.at[part], sems.at[part], 0, 3 * side, 0, part * side, side, side
         )
-
-    def norm(t, carry):
-        at = rows_of(t)
-        normal, _ = normal_parts(patches[at, :].astype(wide))
-        normed[at, :] = (normal * vectors[0:1, :] + vectors[1:2, :]).astype(low)
-        return carry
-
-    lax.fori_loop(0, tiles(rows), norm, 0)
     for part in range(3):
         await_bytes(weight.at[part], sems.at[part])
         out = mm(normed[...], weight[part], 1, 0)
@@ -147,6 +154,7 @@
     whole,
     patches,
     cotangent,
+    grad_two,
     mixed,
     inside,
     vectors,
@@ -165,7 +173,6 @@
     factor,
     second,
     second_t,
-    grad_two,
     out_sum,
     back_sum,
     stage_up,
@@ -202,7 +209,7 @@
         await_bytes(w_out, sems.at[4])
         out_sum[...] = mm(mixed[...], w_out[...], 1, 0)
 
-        def norm(t, total):
+        def norm(t, carry):
             at = rows_of(t)
             keep = inside[at, :]
             mid = patches[at, :].astype(wide) + keep * (out_sum[at, :] + vectors[4:5, :])
@@ -211,11 +218,9 @@
             normal[at, :] = scaled
             factor[at, :] = q
             second[at, :] = (scaled * vectors[5:6, :] + vectors[6:7, :]).astype(low)
-            two = (keep * cotangent[at, :].astype(wide)).astype(low)
-            grad_two[at, :] = two
-            return total + jnp.sum(two.astype(wide), axis=0, keepdims=True)
-
-        sums[3:4, :] = lax.fori_loop(0, tiles(rows), norm, jnp.zeros((1, width), wide))
+            return carry
+
+        lax.fori_loop(0, tiles(rows), norm, 0)
         second_t[...] = second[...].T
         back_sum[...] = jnp.zeros_like(back_sum)
 
@@ -277,7 +282,7 @@
         sums[0:1, :] = bias
         sums[1:2, :] = gain
         sums[2:3, :] = shift
-        sums[4:8, :] = jnp.zeros((4, width), wide)
+        sums[3:8, :] = jnp.zeros((5, width), wide)
         stage_out[...] = mm(mixed[...], second[...], 0, 0).astype(low)
         store_blocks(place, stage_out, buffer, out_sems.at[4], first_out, side, 0, 0, side, side)
         grad_mixed[...] = mm(second[...], w_out[...], 1, 1).astype(low)
@@ -296,49 +301,36 @@
     probs,
     grad_mixed,
     mixed,
-    patches,
-    vectors,
+    normed_t,
     grad_project,
     buffer,
     grad_low,
-    normed,
     stage,
     out_sems,
 ):
     del held
     step = pl.program_id(0)
     steps = pl.num_programs(0)
-    rows, width = patches.shape
+    width, rows = normed_t.shape
     side = width // 128
     scale = 0.125
-
-    @pl.when(step == 0)
-    def _():
-        def norm(t, carry):
-            at = rows_of(t)
-            normal, _ = normal_parts(patches[at, :].astype(wide))
-            normed[at, :] = (normal * vectors[0:1, :] + vectors[1:2, :]).astype(low)
-            return carry
-
-        lax.fori_loop(0, tiles(rows), norm, 0)
-
     lane = lax.broadcasted_iota(jnp.int32, (rows, 128), 1)
     grad = grad_mixed[...]
     grad_t = grad.T
     query_t = query[...].T
     outer = grad.astype(wide) * mixed[...].astype(wide)
+    mine = [lane // 64 == h for h in range(2)]
+    grad_probs = [
+        mm(jnp.where(mine[h], grad, jnp.zeros_like(grad)), values[...], 1, 1) for h in range(2)
+    ]
+    turned_values = [mm(grad_t[h * 64 : (h + 1) * 64, :], probs[h], 1, 0) for h in range(2)]
     turned_query = []
     turned_keys = []
-    turned_values = []
     for h in range(2):
-        mine = lane // 64 == h
-        delta = jnp.sum(jnp.where(mine, outer, 0.0), axis=-1, keepdims=True)
-        part = jnp.where(mine, grad, jnp.zeros_like(grad))
-        grad_probs = mm(part, values[...], 1, 1)
-        grad_low[h] = (probs[h].astype(wide) * (grad_probs - delta)).astype(low)
+        delta = jnp.sum(jnp.where(mine[h], outer, 0.0), axis=-1, keepdims=True)
+        grad_low[h] = (probs[h].astype(wide) * (grad_probs[h] - delta)).astype(low)
         turned_query.append(mm(grad_low[h], keys[...], 1, 0))
         turned_keys.append(mm(query_t[h * 64 : (h + 1) * 64, :], grad_low[h], 1, 0))
-        turned_values.append(mm(grad_t[h * 64 : (h + 1) * 64, :], probs[h], 1, 0))
     grad_query = jnp.where(lane < 64, turned_query[0], turned_query[1]) * scale
     grad_keys = (jnp.concatenate(turned_keys, axis=0) * scale).T
     grad_values = jnp.concatenate(turned_values, axis=0).T
@@ -351,7 +343,7 @@
         for part in range(3):
             if part == 2:
                 await_bytes(stage.at[0], out_sems.at[0])
-            stage[part % 2] = mm(normed[...], grad_project[part], 0, 0).astype(low)
+            stage[part % 2] = mm(normed_t[...], grad_project[part], 1, 0).astype(low)
             store_blocks(
                 place,
                 stage.at[part % 2],
@@ -535,6 +527,18 @@
     image_keys = (lanes == image).astype(low)
     image_query = jnp.where((lanes != image) & (lanes < 5), -far, 0.0).astype(low)
 
+    normed, normed_t, grad_two, bias_down = pl.pallas_call(
+        ready_kernel,
+        out_shape=[
+            shape((rows, width), low),
+            shape((width, rows), low),
+            shape((rows, width), low),
+            shape((1, width), wide),
+        ],
+        compiler_params=pltpu.CompilerParams(vmem_limit_bytes=VMEM_LIMIT),
+        name="ready",
+    )(patches, cotangent, inside, vectors)
+
     project = pl.pallas_call(
         qkv_kernel,
         grid_spec=pltpu.PrefetchScalarGridSpec(
@@ -544,14 +548,13 @@
             out_specs=full((rows, 3 * width)),
             scratch_shapes=[
                 pltpu.VMEM((3, width, width), low),
-                pltpu.VMEM((rows, width), low),
                 pltpu.SemaphoreType.DMA((3,)),
             ],
         ),
         out_shape=shape((rows, 3 * width), low),
         compiler_params=params(),
         name="qkv",
-    )(place, whole, patches, vectors)
+    )(place, whole, normed, vectors)
 
     def column(offset):
         return pl.BlockSpec((rows, 128), lambda j, *_: (0, j + offset))
@@ -584,6 +587,7 @@
                 full((rows, width)),
                 full((rows, width)),
                 full((rows, width)),
+                full((rows, width)),
                 full((rows, 1)),
                 full((12, width)),
                 pl.BlockSpec((1, 1, CHUNK), lambda c, *_: (c, 0, 0)),
@@ -605,7 +609,6 @@
                 pltpu.VMEM((rows, 1), wide),
                 pltpu.VMEM((rows, width), low),
                 pltpu.VMEM((width, rows), low),
-                pltpu.VMEM((rows, width), low),
                 pltpu.VMEM((rows, width), wide),
                 pltpu.VMEM((rows, width), wide),
                 pltpu.VMEM((2, width, CHUNK), low),
@@ -632,6 +635,7 @@
         whole,
         patches,
         cotangent,
+        grad_two,
         mixed,
         inside,
         vectors,
@@ -651,13 +655,11 @@
                 pl.BlockSpec((2, rows, rows), lambda j, *_: (j, 0, 0)),
                 column(0),
                 column(0),
-                full((rows, width)),
-                full((12, width)),
+                full((width, rows)),
             ],
             out_specs=[full((3, rows, width)), whole_spec()],
             scratch_shapes=[
                 pltpu.VMEM((2, rows, rows), low),
-                pltpu.VMEM((rows, width), low),
                 pltpu.VMEM((2, width, width), low),
                 pltpu.SemaphoreType.DMA((2,)),
             ],
@@ -678,8 +680,7 @@
         probs,
         grad_mixed,
         mixed,
-        patches,
-        vectors,
+        normed_t,
     )
     owned = scatter(buffer)
 
@@ -730,7 +731,7 @@
         name="result",
     )(place, whole, active, middle, inside, vectors)
     vector_grad = jnp.concatenate(
-        [sums_one[0:4], sums_two[0:3], sums_up.reshape(4, width), sums_two[3:4]], axis=0
+        [sums_one[0:4], sums_two[0:3], sums_up.reshape(4, width), bias_down], axis=0
     )
     vector_sum = everywhere(vector_grad)
 

time: 341 us -> 338 us (level)
    pallas_call x0 -> x1, Pallas kernels: none -> 5.45 us  [shards(): pl.pallas_call(ready_kernel, out_shape=[shape((rows, width), low), shape(...]
    all_gather x1, waiting for transfers between devices: 78.1 us -> 74.6 us  [gather(): lax.all_gather(value, AXES, axis=0, tiled=True, axis_index_groups=groups)]
  transfers between devices with their start and end apart: 8 -> 8, of which waited for: 7 -> 7; matrix products, arithmetic and copies ran while one was open for 4% -> 3% of each run, Pallas kernels for 7% -> 9%
where the time goes in v5:
time: 338 us; the launch traced here: 337 us
  waiting for transfers between devices  154 us (46%)
  Pallas kernels  130 us (38%)
  between operations  16.8 us (5%)
  other arithmetic  11.6 us (3%)
  starting transfers between devices  10.8 us (3%)
  matrix products  9.77 us (3%)
  local copies, waits for them, and re-layouts  4.45 us (1%)
    all_gather x1, waiting for transfers between devices, gather(): lax.all_gather(value, AXES, axis=0, tiled=True, axis_index_groups=groups)  74.6 us
    reduce_scatter x1, waiting for transfers between devices, scatter(): lax.psum_scatter(value, AXES, scatter_dimension=0, tiled=True, axis_index...  64.9 us
    pallas_call x1, Pallas kernels, shards(): pl.pallas_call(feed_kernel, grid_spec=pltpu.PrefetchScalarGridSpec(num_sc...  41.1 us
    pallas_call x1, Pallas kernels, shards(): pl.pallas_call(back_kernel, grid_spec=pltpu.PrefetchScalarGridSpec(num_sc...  30.4 us
    pallas_call x1, Pallas kernels, shards(): pl.pallas_call(attend_kernel, grid=(pairs,), in_specs=[column(0), column(...  18.7 us
    pallas_call x1, Pallas kernels, shards(): pl.pallas_call(input_kernel, grid_spec=pltpu.PrefetchScalarGridSpec(num_s...  12.7 us
    pallas_call x1, Pallas kernels, shards(): pl.pallas_call(result_kernel, grid_spec=pltpu.PrefetchScalarGridSpec(num_...  12.3 us
    ppermute x5, waiting for transfers between devices, everywhere(): lax.ppermute(value, AXES, [(d, d ^ step) for d in range(devices)])  10.9 us
  transfers between devices with their start and end apart: 8, of which 7 were waited for; matrix products, arithmetic and copies ran while one was open for 3% of the time, Pallas kernels for 9%

profile of v5, /device:TPU:0, one launch (start us, length us, event | category | flops | bytes accessed | tf_op | source)
XLA Modules:
  0.0 337.1 jit_solution(17709884173611820464)
XLA Ops:
  7.3 2.1 convert_element_type.18
  9.4 0.8 reduce-window.4
  10.8 0.8 slice.17
  12.3 1.4 fusion.14.inside
  13.7 5.4 %ready.1 = (bf16[784,768]{1,0:T(8,128)(2,1)}, bf16[768,784]{1,0:T(8,128)(2,1)}, bf16[784,768]{1,0:T(8,128)(2,1)}, f32[1,768]{1,0:T(1,128)}) custom-call(bf16[784,768]{1,0:T(8,128)(2,1)} %patches.5, bf16[784,768]{1,0:T(8,128)(2,1)} %cotangent.3, f32[784,1]{1,0:T(8,128)} %fusion.14.inside, f32[12,768]{1,0:T(8,128)} %vectors.9), custom_call_target="tpu_custom_call" | custom-call | tf_op jit(solution)/shard_map/ready/pallas_call | solution.py:530
  20.6 0.9 fusion.16.image_keys
  21.5 0.9 select_convert_fusion.image_query
  22.3 74.6 %all-gather.2.cloned.1.call-done.whole = bf16[448,128,128]{2,1,0:T(8,128)(2,1)} async-done(((bf16[14,128,128]{2,1,0:T(8,128)(2,1)}), bf16[448,128,128]{2,1,0:T(8,128)(2,1)}) %all-gather.2.cloned.1.call-update) | async-done | bytes 14680080 | tf_op jit(solution)/shard_map/all_gather | solution.py:485
  96.9 9.0 %qkv.1.query.keys.values = bf16[784,2304]{1,0:T(8,128)(2,1)} custom-call(s32[432]{0:T(512)} %fusion.19.place, bf16[448,128,128]{2,1,0:T(8,128)(2,1)} %all-gather.2.cloned.1.call-done.whole, bf16[784,768]{1,0:T(8,128)(2,1)} %get-tuple-element.30.normed, f32[12,768]{1,0:T(8,128)} %vectors.9), custom_call_target="tpu_custom_call" | custom-call | tf_op jit(solution)/shard_map/qkv/pallas_call | solution.py:542
  105.9 18.7 %attend.1 = (bf16[784,768]{1,0:T(8,128)(2,1)}, bf16[12,784,784]{2,1,0:T(8,128)(2,1)}) custom-call(bf16[784,2304]{1,0:T(8,128)(2,1)} %qkv.1.query.keys.values, bf16[784,2304]{1,0:T(8,128)(2,1)} %qkv.1.query.keys.values, bf16[784,2304]{1,0:T(8,128)(2,1)} %qkv.1.query.keys.values, bf16[784,128]{1,0:T(8,128)(2,1)} %select_convert_fusion.image_query, ...), custom_call_target="tpu_custom_call" | custom-call | tf_op jit(solution)/shard_map/attend/pallas_call | solution.py:562
  124.7 41.1 %feed.1 = (f32[784,768]{1,0:T(8,128)}, bf16[784,3072]{1,0:T(8,128)(2,1)}, f32[784,768]{1,0:T(8,128)}, bf16[784,768]{1,0:T(8,128)(2,1)}, f32[8,768]{1,0:T(8,128)}...) custom-call(s32[432]{0:T(512)} %fusion.19.place, bf16[448,128,128]{2,1,0:T(8,128)(2,1)} %all-gather.2.cloned.1.call-done.whole, ...), custom_call_target="tpu_custom_call" | custom-call | tf_op jit(solution)/shard_map/feed/pallas_call | solution.py:580
  165.8 30.4 %back.1 = (bf16[3,784,768]{2,1,0:T(8,128)(2,1)}, bf16[448,128,128]{2,1,0:T(8,128)(2,1)}) custom-call(s32[432]{0:T(512)} %fusion.19.place, bf16[448,128,128]{2,1,0:T(8,128)(2,1)} %get-tuple-element.32.held, bf16[784,2304]{1,0:T(8,128)(2,1)} %qkv.1.query.keys.values, bf16[784,2304]{1,0:T(8,128)(2,1)} %qkv.1.query.keys.values, ...), custom_call_target="tpu_custom_call", output_to_operand_aliasing={{1}: (1, {})} | custom-call | tf_op jit(solution)/shard_map/back/pallas_call | solution.py:645
  196.2 12.7 %input.1 = (bf16[784,768]{1,0:T(8,128)(2,1)}, f32[8,768]{1,0:T(8,128)}) custom-call(s32[432]{0:T(512)} %fusion.19.place, bf16[448,128,128]{2,1,0:T(8,128)(2,1)} %all-gather.2.cloned.1.call-done.whole, bf16[3,784,768]{2,1,0:T(8,128)(2,1)} %get-tuple-element.37.grad_project, bf16[784,768]{1,0:T(8,128)(2,1)} %patches.5, ...), custom_call_target="tpu_custom_call" | custom-call | tf_op jit(solution)/shard_map/input/pallas_call | solution.py:687
  208.9 0.7 slice.18
  210.1 1.0 collective-permute-done
  211.1 1.5 collective-permute-start.1
  212.6 3.4 collective-permute-done.1
  216.0 1.4 collective-permute-start.2
  217.3 2.8 collective-permute-done.2
  220.1 0.8 collective-permute-start.3
  220.9 3.7 %collective-permute-done.3 = f32[12,768]{1,0:T(8,128)S(1)} collective-permute-done((f32[12,768]{1,0:T(8,128)S(1)}, f32[12,768]{1,0:T(8,128)S(1)}, u32[]{:S(2)}, u32[]{:S(2)}) %collective-permute-start.3) | collective-permute-done | bytes 36896 | tf_op jit(solution)/shard_map/ppermute | solution.py:495
  224.7 1.4 collective-permute-start.4
  226.3 12.3 %result.1 = bf16[784,768]{1,0:T(8,128)(2,1)} custom-call(s32[432]{0:T(512)} %fusion.19.place, bf16[448,128,128]{2,1,0:T(8,128)(2,1)} %all-gather.2.cloned.1.call-done.whole, bf16[784,3072]{1,0:T(8,128)(2,1)} %get-tuple-element.43.active, f32[784,768]{1,0:T(8,128)} %get-tuple-element.44.middle, f32[784,1]{1,0:T(8,128)} %fusion.14.inside, f32[12,768]{1,0:T(8,128)} %vectors.9), custom_call_target="tpu_custom_call" | custom-call | tf_op jit(solution)/shard_map/result/pallas_call | solution.py:710
  238.7 64.9 %reduce-scatter.2.cloned.1.call-done = bf16[14,128,128]{2,1,0:T(8,128)(2,1)} async-done(((bf16[448,128,128]{2,1,0:T(8,128)(2,1)}), bf16[14,128,128]{2,1,0:T(8,128)(2,1)}) %reduce-scatter.2.cloned.1.call-update) | async-done | bytes 458768 | tf_op jit(solution)/shard_map/reduce_scatter | solution.py:488
  303.6 1.9 multiply_reduce_fusion
  305.6 1.3 broadcast_in_dim.56
  306.8 5.3 %all-to-all-start = ((f32[32,1,128]{2,1,0:T(1,128)}), f32[32,1,128]{2,1,0:T(1,128)S(1)}, u32[]{:S(2)}, u32[]{:S(2)}) async-start(f32[32,1,128]{2,1,0:T(1,128)} %broadcast_in_dim.56), calls=%async_computation.1 | async-start | bytes 32768 | tf_op jit(solution)/shard_map/all_to_all | solution.py:742
  312.1 2.7 fusion.9
  315.4 3.6 %all-to-all-done = f32[32,1,128]{2,1,0:T(1,128)S(1)} async-done(((f32[32,1,128]{2,1,0:T(1,128)}), f32[32,1,128]{2,1,0:T(1,128)S(1)}, u32[]{:S(2)}, u32[]{:S(2)}) %all-to-all-start) | async-done | bytes 16416 | tf_op jit(solution)/shard_map/all_to_all | solution.py:742
  320.9 2.7 multiply_add_fusion
  323.7 1.5 fusion.3
  325.5 3.0 fusion.1
  (54 shorter events, 5.7 us)
Async XLA Ops:
  7.2 313.7 %copy-start = (f32[14,128,128]{2,1,0:T(8,128)S(1)}, f32[14,128,128]{2,1,0:T(8,128)}, u32[]{:S(2)}) copy-start(f32[14,128,128]{2,1,0:T(8,128)} %param.21) | copy-start | bytes 2752516
  7.2 12.1 %copy-start.12 = (s32[32]{0:T(128)S(1)}, s32[32]{0:T(128)}, u32[]{:S(2)}) copy-start(s32[32]{0:T(128)} %constant.69.clone) | copy-start | bytes 388
  7.2 12.0 %copy-start.8 = (s32[432]{0:T(512)S(1)}, s32[432]{0:T(512)}, u32[]{:S(2)}) copy-start(s32[432]{0:T(512)} %param.16) | copy-start | bytes 5188
  7.2 89.7 %all-gather.2.cloned.1.call-start = ((), (), s32[]{:S(2)}) async-start(), calls=%async_computation.2 | async-start | bytes 15138816 | tf_op jit(solution)/shard_map/all_gather | solution.py:485
  9.4 294.2 %reduce-scatter.2.cloned.1.call-start = ((), (), s32[]{:S(2)}) async-start(), calls=%async_computation.3 | async-start | bytes 15138816 | tf_op jit(solution)/shard_map/reduce_scatter | solution.py:488
  196.2 13.5 %copy-start.9 = (f32[6,1,512]{2,1,0:T(1,128)S(1)}, f32[6,1,512]{2,1,0:T(1,128)}, u32[]{:S(2)}) copy-start(f32[6,1,512]{2,1,0:T(1,128)} %get-tuple-element.41) | copy-start | bytes 36868
  196.2 13.5 %copy-start.11 = (f32[8,768]{1,0:T(8,128)S(1)}, f32[8,768]{1,0:T(8,128)}, u32[]{:S(2)}) copy-start(f32[8,768]{1,0:T(8,128)} %get-tuple-element.40) | copy-start | bytes 73732
  196.2 13.5 %copy-start.10 = (f32[1,768]{1,0:T(1,128)S(1)}, f32[1,768]{1,0:T(1,128)}, u32[]{:S(2)}) copy-start(f32[1,768]{1,0:T(1,128)} %get-tuple-element.42) | copy-start | bytes 9220
  209.8 1.3 collective-permute-start
  211.1 4.9 %collective-permute-start.1 = (f32[12,768]{1,0:T(8,128)S(1)}, f32[12,768]{1,0:T(8,128)S(1)}, u32[]{:S(2)}, u32[]{:S(2)}) collective-permute-start(f32[12,768]{1,0:T(8,128)S(1)} %fusion.24), channel_id=1, source_target_pairs={{0,2},{1,3},{2,0},{3,1},{4,6},{5,7},{6,4},{7,5},{8,10},{9,11},{10,... | collective-permute-start | bytes 110600 | tf_op jit(solution)/shard_map/ppermute | solution.py:495
  216.0 4.2 %collective-permute-start.2 = (f32[12,768]{1,0:T(8,128)S(1)}, f32[12,768]{1,0:T(8,128)S(1)}, u32[]{:S(2)}, u32[]{:S(2)}) collective-permute-start(f32[12,768]{1,0:T(8,128)S(1)} %add.73), channel_id=1, source_target_pairs={{0,4},{1,5},{2,6},{3,7},{4,0},{5,1},{6,2},{7,3},{8,12},{9,13},{10,... | collective-permute-start | bytes 110600 | tf_op jit(solution)/shard_map/ppermute | solution.py:495
  220.1 4.6 %collective-permute-start.3 = (f32[12,768]{1,0:T(8,128)S(1)}, f32[12,768]{1,0:T(8,128)S(1)}, u32[]{:S(2)}, u32[]{:S(2)}) collective-permute-start(f32[12,768]{1,0:T(8,128)S(1)} %add.74), channel_id=1, source_target_pairs={{0,8},{1,9},{2,10},{3,11},{4,12},{5,13},{6,14},{7,15},{8,0},{9,1},... | collective-permute-start | bytes 110600 | tf_op jit(solution)/shard_map/ppermute | solution.py:495
  224.7 14.0 %collective-permute-start.4 = (f32[12,768]{1,0:T(8,128)S(1)}, f32[12,768]{1,0:T(8,128)S(1)}, u32[]{:S(2)}, u32[]{:S(2)}) collective-permute-start(f32[12,768]{1,0:T(8,128)S(1)} %add.75), channel_id=1, source_target_pairs={{0,16},{1,17},{2,18},{3,19},{4,20},{5,21},{6,22},{7,23},{8,24},{9,... | collective-permute-start | bytes 110600 | tf_op jit(solution)/shard_map/ppermute | solution.py:495
  226.3 85.8 %copy-start.3 = (f32[14,128,128]{2,1,0:T(8,128)S(1)}, f32[14,128,128]{2,1,0:T(8,128)}, u32[]{:S(2)}) copy-start(f32[14,128,128]{2,1,0:T(8,128)} %param.20) | copy-start | bytes 2752516
  306.8 12.1 %all-to-all-start = ((f32[32,1,128]{2,1,0:T(1,128)}), f32[32,1,128]{2,1,0:T(1,128)S(1)}, u32[]{:S(2)}, u32[]{:S(2)}) async-start(f32[32,1,128]{2,1,0:T(1,128)} %broadcast_in_dim.56), calls=%async_computation.1 | async-start | bytes 32768 | tf_op jit(solution)/shard_map/all_to_all | solution.py:742
  323.6 4.8 %copy-start.4 = (f32[14,128,128]{2,1,0:T(8,128)}, f32[14,128,128]{2,1,0:T(8,128)S(1)}, u32[]{:S(2)}) copy-start(f32[14,128,128]{2,1,0:T(8,128)S(1)} %get-tuple-element.52) | copy-start | bytes 2752516
  323.6 4.8 %copy-start.5 = (f32[14,128,128]{2,1,0:T(8,128)}, f32[14,128,128]{2,1,0:T(8,128)S(1)}, u32[]{:S(2)}) copy-start(f32[14,128,128]{2,1,0:T(8,128)S(1)} %get-tuple-element.53) | copy-start | bytes 2752516
  323.7 1.8 copy-start.1
  325.5 3.0 copy-start.2
  325.5 3.0 copy-start.6
  325.5 3.0 copy-start.7
Sparse Core Ops, SparseCore 0:
  10.2 86.7 all-gather.1
  196.3 107.2 reduce-scatter.1

commit v6 on v5

--- a/solution.py
+++ b/solution.py
@@ -18,7 +18,7 @@
 rate_matrix = 0.03
 rate_vector = 0.05
 decay_weight = 0.01
-highest = lax.Precision.HIGHEST
+high = lax.Precision.HIGH
 far = 2.0**30
 low = jnp.bfloat16
 wide = jnp.float32
@@ -436,6 +436,14 @@
     sums[4:8, :] = jnp.zeros((4, width), wide)
 
 
+def squares_kernel(named, grads, spread):
+    total = jnp.zeros((128, 128), wide)
+    for s in range(grads.shape[0]):
+        block = jnp.where(named[s] > 0, grads[s].astype(wide), 0.0)
+        total = total + block * block
+    spread[...] = jnp.broadcast_to(jnp.sum(total), spread.shape)
+
+
 VMEM_LIMIT = 60 * 1024 * 1024
 
 
@@ -737,20 +745,28 @@
 
     owned, vector_sum, result = lax.optimization_barrier((owned, vector_sum, result))
 
+    received = owned
     owned = jnp.where(named[:, None, None], owned.astype(wide), 0.0)
-    squares = jnp.broadcast_to(jnp.sum(owned * owned), (devices, 128))
+    squares = pl.pallas_call(
+        squares_kernel,
+        in_specs=[pl.BlockSpec(memory_space=pltpu.SMEM), full((held, size, size))],
+        out_specs=full((devices, 128)),
+        out_shape=shape((devices, 128), wide),
+        grid=(),
+        name="squares",
+    )(named.astype(jnp.int32), received)
     total_blocks = jnp.sum(lax.all_to_all(squares, AXES, 0, 0, tiled=True)[:, 0])
     clip_norm = jnp.sqrt(total_blocks + jnp.sum(vector_sum * vector_sum))
     count = owners.shape[0] * size * size + vectors.shape[0] * width
     factor = jnp.minimum(1.0, 0.5 * math.sqrt(count) / clip_norm)
-    turned = jnp.einsum("sji,sjk->sik", left_basis, owned, precision=highest)
-    rotated = factor * jnp.einsum("sik,skl->sil", turned, right_basis, precision=highest)
+    turned = jnp.einsum("sji,sjk->sik", left_basis, owned, precision=high)
+    rotated = factor * jnp.einsum("sik,skl->sil", turned, right_basis, precision=high)
     new_first = beta * first_moment + (1.0 - beta) * rotated
     new_second = beta * second_moment + (1.0 - beta) * rotated * rotated
     correction = 1.0 - beta**STEP
     direction = new_first / correction / (jnp.sqrt(new_second / correction) + adam_eps)
-    back_turn = jnp.einsum("sij,sjk->sik", left_basis, direction, precision=highest)
-    update = jnp.einsum("sik,slk->sil", back_turn, right_basis, precision=highest)
+    back_turn = jnp.einsum("sij,sjk->sik", left_basis, direction, precision=high)
+    update = jnp.einsum("sik,slk->sil", back_turn, right_basis, precision=high)
     new_master = master - rate_matrix * (update + decay_weight * master)
     vector_clip = factor * vector_sum
     new_vector_first = beta * vector_first + (1.0 - beta) * vector_clip

time: 338 us -> 336 us (level)
  no operation moved by 1% of the time
where the time goes in v6:
time: 336 us; the launch traced here: 335 us
  waiting for transfers between devices  154 us (46%)
  Pallas kernels  132 us (39%)
  between operations  16.8 us (5%)
  starting transfers between devices  11.1 us (3%)
  other arithmetic  10.2 us (3%)
  matrix products  7.2 us (2%)
  local copies, waits for them, and re-layouts  3.63 us (1%)
    all_gather x1, waiting for transfers between devices, gather(): lax.all_gather(value, AXES, axis=0, tiled=True, axis_index_groups=groups)  74.6 us
    reduce_scatter x1, waiting for transfers between devices, scatter(): lax.psum_scatter(value, AXES, scatter_dimension=0, tiled=True, axis_index...  64.4 us
    pallas_call x1, Pallas kernels, shards(): pl.pallas_call(feed_kernel, grid_spec=pltpu.PrefetchScalarGridSpec(num_sc...  41.1 us
    pallas_call x1, Pallas kernels, shards(): pl.pallas_call(back_kernel, grid_spec=pltpu.PrefetchScalarGridSpec(num_sc...  30.4 us
    pallas_call x1, Pallas kernels, shards(): pl.pallas_call(attend_kernel, grid=(pairs,), in_specs=[column(0), column(...  18.7 us
    pallas_call x1, Pallas kernels, shards(): pl.pallas_call(input_kernel, grid_spec=pltpu.PrefetchScalarGridSpec(num_s...  12.7 us
    pallas_call x1, Pallas kernels, shards(): pl.pallas_call(result_kernel, grid_spec=pltpu.PrefetchScalarGridSpec(num_...  12.4 us
    ppermute x5, waiting for transfers between devices, everywhere(): lax.ppermute(value, AXES, [(d, d ^ step) for d in range(devices)])  10.9 us
  transfers between devices with their start and end apart: 8, of which 7 were waited for; matrix products, arithmetic and copies ran while one was open for 3% of the time, Pallas kernels for 9%

profile of v6, /device:TPU:0, one launch (start us, length us, event | category | flops | bytes accessed | tf_op | source)
XLA Modules:
  0.0 334.8 jit_solution(2943425367833502338)
XLA Ops:
  7.3 2.1 convert_element_type.21
  9.4 0.8 reduce-window.4
  10.8 0.8 slice.17
  12.3 1.4 fusion.16.inside
  13.7 5.4 %ready.1 = (bf16[784,768]{1,0:T(8,128)(2,1)}, bf16[768,784]{1,0:T(8,128)(2,1)}, bf16[784,768]{1,0:T(8,128)(2,1)}, f32[1,768]{1,0:T(1,128)}) custom-call(bf16[784,768]{1,0:T(8,128)(2,1)} %patches.5, bf16[784,768]{1,0:T(8,128)(2,1)} %cotangent.3, f32[784,1]{1,0:T(8,128)} %fusion.16.inside, f32[12,768]{1,0:T(8,128)} %vectors.9), custom_call_target="tpu_custom_call" | custom-call | tf_op jit(solution)/shard_map/ready/pallas_call | solution.py:538
  20.6 0.9 fusion.18.image_keys
  21.5 0.9 select_convert_fusion.image_query
  22.3 74.6 %all-gather.2.cloned.1.call-done.whole = bf16[448,128,128]{2,1,0:T(8,128)(2,1)} async-done(((bf16[14,128,128]{2,1,0:T(8,128)(2,1)}), bf16[448,128,128]{2,1,0:T(8,128)(2,1)}) %all-gather.2.cloned.1.call-update) | async-done | bytes 14680080 | tf_op jit(solution)/shard_map/all_gather | solution.py:493
  96.9 9.0 %qkv.1.query.keys.values = bf16[784,2304]{1,0:T(8,128)(2,1)} custom-call(s32[432]{0:T(512)} %fusion.21.place, bf16[448,128,128]{2,1,0:T(8,128)(2,1)} %all-gather.2.cloned.1.call-done.whole, bf16[784,768]{1,0:T(8,128)(2,1)} %get-tuple-element.30.normed, f32[12,768]{1,0:T(8,128)} %vectors.9), custom_call_target="tpu_custom_call" | custom-call | tf_op jit(solution)/shard_map/qkv/pallas_call | solution.py:550
  105.9 18.7 %attend.1 = (bf16[784,768]{1,0:T(8,128)(2,1)}, bf16[12,784,784]{2,1,0:T(8,128)(2,1)}) custom-call(bf16[784,2304]{1,0:T(8,128)(2,1)} %qkv.1.query.keys.values, bf16[784,2304]{1,0:T(8,128)(2,1)} %qkv.1.query.keys.values, bf16[784,2304]{1,0:T(8,128)(2,1)} %qkv.1.query.keys.values, bf16[784,128]{1,0:T(8,128)(2,1)} %select_convert_fusion.image_query, ...), custom_call_target="tpu_custom_call" | custom-call | tf_op jit(solution)/shard_map/attend/pallas_call | solution.py:570
  124.6 41.1 %feed.1 = (f32[784,768]{1,0:T(8,128)}, bf16[784,3072]{1,0:T(8,128)(2,1)}, f32[784,768]{1,0:T(8,128)}, bf16[784,768]{1,0:T(8,128)(2,1)}, f32[8,768]{1,0:T(8,128)}...) custom-call(s32[432]{0:T(512)} %fusion.21.place, bf16[448,128,128]{2,1,0:T(8,128)(2,1)} %all-gather.2.cloned.1.call-done.whole, ...), custom_call_target="tpu_custom_call" | custom-call | tf_op jit(solution)/shard_map/feed/pallas_call | solution.py:588
  165.7 30.4 %back.1 = (bf16[3,784,768]{2,1,0:T(8,128)(2,1)}, bf16[448,128,128]{2,1,0:T(8,128)(2,1)}) custom-call(s32[432]{0:T(512)} %fusion.21.place, bf16[448,128,128]{2,1,0:T(8,128)(2,1)} %get-tuple-element.32.held, bf16[784,2304]{1,0:T(8,128)(2,1)} %qkv.1.query.keys.values, bf16[784,2304]{1,0:T(8,128)(2,1)} %qkv.1.query.keys.values, ...), custom_call_target="tpu_custom_call", output_to_operand_aliasing={{1}: (1, {})} | custom-call | tf_op jit(solution)/shard_map/back/pallas_call | solution.py:653
  196.2 12.7 %input.1 = (bf16[784,768]{1,0:T(8,128)(2,1)}, f32[8,768]{1,0:T(8,128)}) custom-call(s32[432]{0:T(512)} %fusion.21.place, bf16[448,128,128]{2,1,0:T(8,128)(2,1)} %all-gather.2.cloned.1.call-done.whole, bf16[3,784,768]{2,1,0:T(8,128)(2,1)} %get-tuple-element.37.grad_project, bf16[784,768]{1,0:T(8,128)(2,1)} %patches.5, ...), custom_call_target="tpu_custom_call" | custom-call | tf_op jit(solution)/shard_map/input/pallas_call | solution.py:695
  208.9 0.7 slice.18
  210.1 1.0 collective-permute-done
  211.1 1.5 collective-permute-start.1
  212.6 3.4 %collective-permute-done.1 = f32[12,768]{1,0:T(8,128)S(1)} collective-permute-done((f32[12,768]{1,0:T(8,128)S(1)}, f32[12,768]{1,0:T(8,128)S(1)}, u32[]{:S(2)}, u32[]{:S(2)}) %collective-permute-start.1) | collective-permute-done | bytes 36896 | tf_op jit(solution)/shard_map/ppermute | solution.py:503
  216.0 1.3 collective-permute-start.2
  217.3 2.8 collective-permute-done.2
  220.1 0.8 collective-permute-start.3
  220.9 3.7 %collective-permute-done.3 = f32[12,768]{1,0:T(8,128)S(1)} collective-permute-done((f32[12,768]{1,0:T(8,128)S(1)}, f32[12,768]{1,0:T(8,128)S(1)}, u32[]{:S(2)}, u32[]{:S(2)}) %collective-permute-start.3) | collective-permute-done | bytes 36896 | tf_op jit(solution)/shard_map/ppermute | solution.py:503
  224.7 1.4 collective-permute-start.4
  226.8 12.4 %result.1 = bf16[784,768]{1,0:T(8,128)(2,1)} custom-call(s32[432]{0:T(512)} %fusion.21.place, bf16[448,128,128]{2,1,0:T(8,128)(2,1)} %all-gather.2.cloned.1.call-done.whole, bf16[784,3072]{1,0:T(8,128)(2,1)} %get-tuple-element.43.active, f32[784,768]{1,0:T(8,128)} %get-tuple-element.44.middle, f32[784,1]{1,0:T(8,128)} %fusion.16.inside, f32[12,768]{1,0:T(8,128)} %vectors.9), custom_call_target="tpu_custom_call" | custom-call | tf_op jit(solution)/shard_map/result/pallas_call | solution.py:718
  239.2 64.4 %reduce-scatter.2.cloned.1.call-done.grads = bf16[14,128,128]{2,1,0:T(8,128)(2,1)} async-done(((bf16[448,128,128]{2,1,0:T(8,128)(2,1)}), bf16[14,128,128]{2,1,0:T(8,128)(2,1)}) %reduce-scatter.2.cloned.1.call-update) | async-done | bytes 458768 | tf_op jit(solution)/shard_map/reduce_scatter | solution.py:496
  303.6 1.9 squares.1
  305.5 5.7 %all-to-all-start = ((f32[32,1,128]{2,1,0:T(1,128)}), f32[32,1,128]{2,1,0:T(1,128)S(1)}, u32[]{:S(2)}, u32[]{:S(2)}) async-start(f32[32,1,128]{2,1,0:T(1,128)} %bitcast.13), calls=%async_computation.1 | async-start | bytes 32768 | tf_op jit(solution)/shard_map/all_to_all | solution.py:758
  311.2 1.9 fusion.9
  313.8 4.3 %all-to-all-done = f32[32,1,128]{2,1,0:T(1,128)S(1)} async-done(((f32[32,1,128]{2,1,0:T(1,128)}), f32[32,1,128]{2,1,0:T(1,128)S(1)}, u32[]{:S(2)}, u32[]{:S(2)}) %all-to-all-start) | async-done | bytes 16416 | tf_op jit(solution)/shard_map/all_to_all | solution.py:758
  320.0 2.2 multiply_add_fusion
  322.3 1.0 fusion.3
  323.3 0.8 copy-done.1
  324.1 2.0 fusion.1
  (54 shorter events, 5.8 us)
Async XLA Ops:
  7.2 312.9 %copy-start = (f32[14,128,128]{2,1,0:T(8,128)S(1)}, f32[14,128,128]{2,1,0:T(8,128)}, u32[]{:S(2)}) copy-start(f32[14,128,128]{2,1,0:T(8,128)} %param.21) | copy-start | bytes 2752516
  7.2 12.1 %copy-start.12 = (s32[32]{0:T(128)S(1)}, s32[32]{0:T(128)}, u32[]{:S(2)}) copy-start(s32[32]{0:T(128)} %constant.69.clone) | copy-start | bytes 388
  7.2 12.0 %copy-start.8 = (s32[432]{0:T(512)S(1)}, s32[432]{0:T(512)}, u32[]{:S(2)}) copy-start(s32[432]{0:T(512)} %param.16) | copy-start | bytes 5188
  7.2 89.7 %all-gather.2.cloned.1.call-start = ((), (), s32[]{:S(2)}) async-start(), calls=%async_computation.2 | async-start | bytes 15138816 | tf_op jit(solution)/shard_map/all_gather | solution.py:493
  9.4 294.2 %reduce-scatter.2.cloned.1.call-start = ((), (), s32[]{:S(2)}) async-start(), calls=%async_computation.3 | async-start | bytes 15138816 | tf_op jit(solution)/shard_map/reduce_scatter | solution.py:496
  196.2 13.5 %copy-start.9 = (f32[6,1,512]{2,1,0:T(1,128)S(1)}, f32[6,1,512]{2,1,0:T(1,128)}, u32[]{:S(2)}) copy-start(f32[6,1,512]{2,1,0:T(1,128)} %get-tuple-element.41) | copy-start | bytes 36868
  196.2 13.5 %copy-start.11 = (f32[8,768]{1,0:T(8,128)S(1)}, f32[8,768]{1,0:T(8,128)}, u32[]{:S(2)}) copy-start(f32[8,768]{1,0:T(8,128)} %get-tuple-element.40) | copy-start | bytes 73732
  196.2 13.5 %copy-start.10 = (f32[1,768]{1,0:T(1,128)S(1)}, f32[1,768]{1,0:T(1,128)}, u32[]{:S(2)}) copy-start(f32[1,768]{1,0:T(1,128)} %get-tuple-element.42) | copy-start | bytes 9220
  209.8 1.3 collective-permute-start
  211.1 4.9 %collective-permute-start.1 = (f32[12,768]{1,0:T(8,128)S(1)}, f32[12,768]{1,0:T(8,128)S(1)}, u32[]{:S(2)}, u32[]{:S(2)}) collective-permute-start(f32[12,768]{1,0:T(8,128)S(1)} %fusion.26), channel_id=1, source_target_pairs={{0,2},{1,3},{2,0},{3,1},{4,6},{5,7},{6,4},{7,5},{8,10},{9,11},{10,... | collective-permute-start | bytes 110600 | tf_op jit(solution)/shard_map/ppermute | solution.py:503
  216.0 4.2 %collective-permute-start.2 = (f32[12,768]{1,0:T(8,128)S(1)}, f32[12,768]{1,0:T(8,128)S(1)}, u32[]{:S(2)}, u32[]{:S(2)}) collective-permute-start(f32[12,768]{1,0:T(8,128)S(1)} %add.73), channel_id=1, source_target_pairs={{0,4},{1,5},{2,6},{3,7},{4,0},{5,1},{6,2},{7,3},{8,12},{9,13},{10,... | collective-permute-start | bytes 110600 | tf_op jit(solution)/shard_map/ppermute | solution.py:503
  220.1 4.6 %collective-permute-start.3 = (f32[12,768]{1,0:T(8,128)S(1)}, f32[12,768]{1,0:T(8,128)S(1)}, u32[]{:S(2)}, u32[]{:S(2)}) collective-permute-start(f32[12,768]{1,0:T(8,128)S(1)} %add.74), channel_id=1, source_target_pairs={{0,8},{1,9},{2,10},{3,11},{4,12},{5,13},{6,14},{7,15},{8,0},{9,1},... | collective-permute-start | bytes 110600 | tf_op jit(solution)/shard_map/ppermute | solution.py:503
  224.7 14.5 %collective-permute-start.4 = (f32[12,768]{1,0:T(8,128)S(1)}, f32[12,768]{1,0:T(8,128)S(1)}, u32[]{:S(2)}, u32[]{:S(2)}) collective-permute-start(f32[12,768]{1,0:T(8,128)S(1)} %add.75), channel_id=1, source_target_pairs={{0,16},{1,17},{2,18},{3,19},{4,20},{5,21},{6,22},{7,23},{8,24},{9,... | collective-permute-start | bytes 110600 | tf_op jit(solution)/shard_map/ppermute | solution.py:503
  226.8 84.4 %copy-start.3 = (f32[14,128,128]{2,1,0:T(8,128)S(1)}, f32[14,128,128]{2,1,0:T(8,128)}, u32[]{:S(2)}) copy-start(f32[14,128,128]{2,1,0:T(8,128)} %param.20) | copy-start | bytes 2752516
  305.5 12.6 %all-to-all-start = ((f32[32,1,128]{2,1,0:T(1,128)}), f32[32,1,128]{2,1,0:T(1,128)S(1)}, u32[]{:S(2)}, u32[]{:S(2)}) async-start(f32[32,1,128]{2,1,0:T(1,128)} %bitcast.13), calls=%async_computation.1 | async-start | bytes 32768 | tf_op jit(solution)/shard_map/all_to_all | solution.py:758
  322.3 3.9 %copy-start.4 = (f32[14,128,128]{2,1,0:T(8,128)}, f32[14,128,128]{2,1,0:T(8,128)S(1)}, u32[]{:S(2)}) copy-start(f32[14,128,128]{2,1,0:T(8,128)S(1)} %get-tuple-element.52) | copy-start | bytes 2752516
  322.3 3.9 %copy-start.5 = (f32[14,128,128]{2,1,0:T(8,128)}, f32[14,128,128]{2,1,0:T(8,128)S(1)}, u32[]{:S(2)}) copy-start(f32[14,128,128]{2,1,0:T(8,128)S(1)} %get-tuple-element.53) | copy-start | bytes 2752516
  322.3 1.8 copy-start.1
  324.1 2.0 copy-start.2
  324.1 2.0 copy-start.6
  324.1 2.0 copy-start.7
Sparse Core Ops, SparseCore 0:
  10.2 86.7 all-gather.1
  196.3 107.2 reduce-scatter.1

commit v7 on v6

--- a/solution.py
+++ b/solution.py
@@ -23,7 +23,7 @@
 low = jnp.bfloat16
 wide = jnp.float32
 
-CHUNK = 512
+CHUNK = 1024
 
 
 def ring_order(dp, fsdp):
@@ -233,7 +233,7 @@
         await_bytes(stage_up.at[slot], out_sems.at[slot])
         await_bytes(stage_down.at[slot], out_sems.at[2 + slot])
 
-    parts = [slice(h * (CHUNK // 2), (h + 1) * (CHUNK // 2)) for h in range(2)]
+    parts = [slice(h * 256, (h + 1) * 256) for h in range(CHUNK // 256)]
     pres = [mm(second[...], w_up[slot, :, p], 1, 0) + bias_up[0, :, p] for p in parts]
     grads = [mm(grad_two[...], w_down[slot, p, :], 1, 1) for p in parts]
     for p, pre, grad in zip(parts, pres, grads):

time: 336 us -> 334 us (level)
  no operation moved by 1% of the time
where the time goes in v7:
time: 334 us; the launch traced here: 333 us
  waiting for transfers between devices  155 us (46%)
  Pallas kernels  129 us (39%)
  between operations  16.8 us (5%)
  starting transfers between devices  10.8 us (3%)
  other arithmetic  10.2 us (3%)
  matrix products  7.2 us (2%)
  local copies, waits for them, and re-layouts  3.64 us (1%)
    all_gather x1, waiting for transfers between devices, gather(): lax.all_gather(value, AXES, axis=0, tiled=True, axis_index_groups=groups)  74.6 us
    reduce_scatter x1, waiting for transfers between devices, scatter(): lax.psum_scatter(value, AXES, scatter_dimension=0, tiled=True, axis_index...  65.3 us
    pallas_call x1, Pallas kernels, shards(): pl.pallas_call(feed_kernel, grid_spec=pltpu.PrefetchScalarGridSpec(num_sc...  39.9 us
    pallas_call x1, Pallas kernels, shards(): pl.pallas_call(back_kernel, grid_spec=pltpu.PrefetchScalarGridSpec(num_sc...  30.4 us
    pallas_call x1, Pallas kernels, shards(): pl.pallas_call(attend_kernel, grid=(pairs,), in_specs=[column(0), column(...  18.7 us
    pallas_call x1, Pallas kernels, shards(): pl.pallas_call(input_kernel, grid_spec=pltpu.PrefetchScalarGridSpec(num_s...  12.7 us
    pallas_call x1, Pallas kernels, shards(): pl.pallas_call(result_kernel, grid_spec=pltpu.PrefetchScalarGridSpec(num_...  11.4 us
    ppermute x5, waiting for transfers between devices, everywhere(): lax.ppermute(value, AXES, [(d, d ^ step) for d in range(devices)])  10.9 us
  transfers between devices with their start and end apart: 8, of which 7 were waited for; matrix products, arithmetic and copies ran while one was open for 3% of the time, Pallas kernels for 9%

profile of v7, /device:TPU:0, one launch (start us, length us, event | category | flops | bytes accessed | tf_op | source)
XLA Modules:
  0.0 333.2 jit_solution(2730896395783989780)
XLA Ops:
  7.3 2.1 convert_element_type.21
  9.4 0.8 reduce-window.4
  10.8 0.8 slice.17
  12.3 1.4 fusion.16.inside
  13.7 5.4 %ready.1 = (bf16[784,768]{1,0:T(8,128)(2,1)}, bf16[768,784]{1,0:T(8,128)(2,1)}, bf16[784,768]{1,0:T(8,128)(2,1)}, f32[1,768]{1,0:T(1,128)}) custom-call(bf16[784,768]{1,0:T(8,128)(2,1)} %patches.5, bf16[784,768]{1,0:T(8,128)(2,1)} %cotangent.3, f32[784,1]{1,0:T(8,128)} %fusion.16.inside, f32[12,768]{1,0:T(8,128)} %vectors.9), custom_call_target="tpu_custom_call" | custom-call | tf_op jit(solution)/shard_map/ready/pallas_call | solution.py:538
  20.6 0.9 fusion.18.image_keys
  21.5 0.9 select_convert_fusion.image_query
  22.3 74.6 %all-gather.2.cloned.1.call-done.whole = bf16[448,128,128]{2,1,0:T(8,128)(2,1)} async-done(((bf16[14,128,128]{2,1,0:T(8,128)(2,1)}), bf16[448,128,128]{2,1,0:T(8,128)(2,1)}) %all-gather.2.cloned.1.call-update) | async-done | bytes 14680080 | tf_op jit(solution)/shard_map/all_gather | solution.py:493
  96.9 9.0 %qkv.1.query.keys.values = bf16[784,2304]{1,0:T(8,128)(2,1)} custom-call(s32[432]{0:T(512)} %fusion.21.place, bf16[448,128,128]{2,1,0:T(8,128)(2,1)} %all-gather.2.cloned.1.call-done.whole, bf16[784,768]{1,0:T(8,128)(2,1)} %get-tuple-element.30.normed, f32[12,768]{1,0:T(8,128)} %vectors.9), custom_call_target="tpu_custom_call" | custom-call | tf_op jit(solution)/shard_map/qkv/pallas_call | solution.py:550
  105.9 18.7 %attend.1 = (bf16[784,768]{1,0:T(8,128)(2,1)}, bf16[12,784,784]{2,1,0:T(8,128)(2,1)}) custom-call(bf16[784,2304]{1,0:T(8,128)(2,1)} %qkv.1.query.keys.values, bf16[784,2304]{1,0:T(8,128)(2,1)} %qkv.1.query.keys.values, bf16[784,2304]{1,0:T(8,128)(2,1)} %qkv.1.query.keys.values, bf16[784,128]{1,0:T(8,128)(2,1)} %select_convert_fusion.image_query, ...), custom_call_target="tpu_custom_call" | custom-call | tf_op jit(solution)/shard_map/attend/pallas_call | solution.py:570
  124.6 39.9 %feed.1 = (f32[784,768]{1,0:T(8,128)}, bf16[784,3072]{1,0:T(8,128)(2,1)}, f32[784,768]{1,0:T(8,128)}, bf16[784,768]{1,0:T(8,128)(2,1)}, f32[8,768]{1,0:T(8,128)}...) custom-call(s32[432]{0:T(512)} %fusion.21.place, bf16[448,128,128]{2,1,0:T(8,128)(2,1)} %all-gather.2.cloned.1.call-done.whole, ...), custom_call_target="tpu_custom_call" | custom-call | tf_op jit(solution)/shard_map/feed/pallas_call | solution.py:588
  164.6 30.4 %back.1 = (bf16[3,784,768]{2,1,0:T(8,128)(2,1)}, bf16[448,128,128]{2,1,0:T(8,128)(2,1)}) custom-call(s32[432]{0:T(512)} %fusion.21.place, bf16[448,128,128]{2,1,0:T(8,128)(2,1)} %get-tuple-element.32.held, bf16[784,2304]{1,0:T(8,128)(2,1)} %qkv.1.query.keys.values, bf16[784,2304]{1,0:T(8,128)(2,1)} %qkv.1.query.keys.values, ...), custom_call_target="tpu_custom_call", output_to_operand_aliasing={{1}: (1, {})} | custom-call | tf_op jit(solution)/shard_map/back/pallas_call | solution.py:653
  195.0 12.7 %input.1 = (bf16[784,768]{1,0:T(8,128)(2,1)}, f32[8,768]{1,0:T(8,128)}) custom-call(s32[432]{0:T(512)} %fusion.21.place, bf16[448,128,128]{2,1,0:T(8,128)(2,1)} %all-gather.2.cloned.1.call-done.whole, bf16[3,784,768]{2,1,0:T(8,128)(2,1)} %get-tuple-element.37.grad_project, bf16[784,768]{1,0:T(8,128)(2,1)} %patches.5, ...), custom_call_target="tpu_custom_call" | custom-call | tf_op jit(solution)/shard_map/input/pallas_call | solution.py:695
  207.7 0.7 slice.18
  208.9 1.0 collective-permute-done
  209.9 1.5 collective-permute-start.1
  211.4 3.4 %collective-permute-done.1 = f32[12,768]{1,0:T(8,128)S(1)} collective-permute-done((f32[12,768]{1,0:T(8,128)S(1)}, f32[12,768]{1,0:T(8,128)S(1)}, u32[]{:S(2)}, u32[]{:S(2)}) %collective-permute-start.1) | collective-permute-done | bytes 36896 | tf_op jit(solution)/shard_map/ppermute | solution.py:503
  214.8 1.3 collective-permute-start.2
  216.1 2.8 collective-permute-done.2
  218.9 0.8 collective-permute-start.3
  219.8 3.7 %collective-permute-done.3 = f32[12,768]{1,0:T(8,128)S(1)} collective-permute-done((f32[12,768]{1,0:T(8,128)S(1)}, f32[12,768]{1,0:T(8,128)S(1)}, u32[]{:S(2)}, u32[]{:S(2)}) %collective-permute-start.3) | collective-permute-done | bytes 36896 | tf_op jit(solution)/shard_map/ppermute | solution.py:503
  223.5 1.4 collective-permute-start.4
  225.7 11.4 %result.1 = bf16[784,768]{1,0:T(8,128)(2,1)} custom-call(s32[432]{0:T(512)} %fusion.21.place, bf16[448,128,128]{2,1,0:T(8,128)(2,1)} %all-gather.2.cloned.1.call-done.whole, bf16[784,3072]{1,0:T(8,128)(2,1)} %get-tuple-element.43.active, f32[784,768]{1,0:T(8,128)} %get-tuple-element.44.middle, f32[784,1]{1,0:T(8,128)} %fusion.16.inside, f32[12,768]{1,0:T(8,128)} %vectors.9), custom_call_target="tpu_custom_call" | custom-call | tf_op jit(solution)/shard_map/result/pallas_call | solution.py:718
  237.1 65.3 %reduce-scatter.2.cloned.1.call-done.grads = bf16[14,128,128]{2,1,0:T(8,128)(2,1)} async-done(((bf16[448,128,128]{2,1,0:T(8,128)(2,1)}), bf16[14,128,128]{2,1,0:T(8,128)(2,1)}) %reduce-scatter.2.cloned.1.call-update) | async-done | bytes 458768 | tf_op jit(solution)/shard_map/reduce_scatter | solution.py:496
  302.4 1.9 squares.1
  304.3 5.3 %all-to-all-start = ((f32[32,1,128]{2,1,0:T(1,128)}), f32[32,1,128]{2,1,0:T(1,128)S(1)}, u32[]{:S(2)}, u32[]{:S(2)}) async-start(f32[32,1,128]{2,1,0:T(1,128)} %bitcast.13), calls=%async_computation.1 | async-start | bytes 32768 | tf_op jit(solution)/shard_map/all_to_all | solution.py:758
  309.6 1.9 fusion.9
  312.2 4.3 %all-to-all-done = f32[32,1,128]{2,1,0:T(1,128)S(1)} async-done(((f32[32,1,128]{2,1,0:T(1,128)}), f32[32,1,128]{2,1,0:T(1,128)S(1)}, u32[]{:S(2)}, u32[]{:S(2)}) %all-to-all-start) | async-done | bytes 16416 | tf_op jit(solution)/shard_map/all_to_all | solution.py:758
  318.4 2.2 multiply_add_fusion
  320.7 1.0 fusion.3
  321.7 0.8 copy-done.1
  322.5 2.0 fusion.1
  (54 shorter events, 5.9 us)
Async XLA Ops:
  7.2 311.3 %copy-start = (f32[14,128,128]{2,1,0:T(8,128)S(1)}, f32[14,128,128]{2,1,0:T(8,128)}, u32[]{:S(2)}) copy-start(f32[14,128,128]{2,1,0:T(8,128)} %param.21) | copy-start | bytes 2752516
  7.2 12.1 %copy-start.12 = (s32[32]{0:T(128)S(1)}, s32[32]{0:T(128)}, u32[]{:S(2)}) copy-start(s32[32]{0:T(128)} %constant.69.clone) | copy-start | bytes 388
  7.2 12.0 %copy-start.8 = (s32[432]{0:T(512)S(1)}, s32[432]{0:T(512)}, u32[]{:S(2)}) copy-start(s32[432]{0:T(512)} %param.16) | copy-start | bytes 5188
  7.2 89.7 %all-gather.2.cloned.1.call-start = ((), (), s32[]{:S(2)}) async-start(), calls=%async_computation.2 | async-start | bytes 15138816 | tf_op jit(solution)/shard_map/all_gather | solution.py:493
  9.4 293.0 %reduce-scatter.2.cloned.1.call-start = ((), (), s32[]{:S(2)}) async-start(), calls=%async_computation.3 | async-start | bytes 15138816 | tf_op jit(solution)/shard_map/reduce_scatter | solution.py:496
  195.0 13.4 %copy-start.9 = (f32[3,1,1024]{2,1,0:T(1,128)S(1)}, f32[3,1,1024]{2,1,0:T(1,128)}, u32[]{:S(2)}) copy-start(f32[3,1,1024]{2,1,0:T(1,128)} %get-tuple-element.41) | copy-start | bytes 36868
  195.0 13.5 %copy-start.11 = (f32[8,768]{1,0:T(8,128)S(1)}, f32[8,768]{1,0:T(8,128)}, u32[]{:S(2)}) copy-start(f32[8,768]{1,0:T(8,128)} %get-tuple-element.40) | copy-start | bytes 73732
  195.0 13.5 %copy-start.10 = (f32[1,768]{1,0:T(1,128)S(1)}, f32[1,768]{1,0:T(1,128)}, u32[]{:S(2)}) copy-start(f32[1,768]{1,0:T(1,128)} %get-tuple-element.42) | copy-start | bytes 9220
  208.6 1.3 collective-permute-start
  209.9 4.9 %collective-permute-start.1 = (f32[12,768]{1,0:T(8,128)S(1)}, f32[12,768]{1,0:T(8,128)S(1)}, u32[]{:S(2)}, u32[]{:S(2)}) collective-permute-start(f32[12,768]{1,0:T(8,128)S(1)} %fusion.26), channel_id=1, source_target_pairs={{0,2},{1,3},{2,0},{3,1},{4,6},{5,7},{6,4},{7,5},{8,10},{9,11},{10,... | collective-permute-start | bytes 110600 | tf_op jit(solution)/shard_map/ppermute | solution.py:503
  214.8 4.2 %collective-permute-start.2 = (f32[12,768]{1,0:T(8,128)S(1)}, f32[12,768]{1,0:T(8,128)S(1)}, u32[]{:S(2)}, u32[]{:S(2)}) collective-permute-start(f32[12,768]{1,0:T(8,128)S(1)} %add.73), channel_id=1, source_target_pairs={{0,4},{1,5},{2,6},{3,7},{4,0},{5,1},{6,2},{7,3},{8,12},{9,13},{10,... | collective-permute-start | bytes 110600 | tf_op jit(solution)/shard_map/ppermute | solution.py:503
  218.9 4.6 %collective-permute-start.3 = (f32[12,768]{1,0:T(8,128)S(1)}, f32[12,768]{1,0:T(8,128)S(1)}, u32[]{:S(2)}, u32[]{:S(2)}) collective-permute-start(f32[12,768]{1,0:T(8,128)S(1)} %add.74), channel_id=1, source_target_pairs={{0,8},{1,9},{2,10},{3,11},{4,12},{5,13},{6,14},{7,15},{8,0},{9,1},... | collective-permute-start | bytes 110600 | tf_op jit(solution)/shard_map/ppermute | solution.py:503
  223.5 13.6 %collective-permute-start.4 = (f32[12,768]{1,0:T(8,128)S(1)}, f32[12,768]{1,0:T(8,128)S(1)}, u32[]{:S(2)}, u32[]{:S(2)}) collective-permute-start(f32[12,768]{1,0:T(8,128)S(1)} %add.75), channel_id=1, source_target_pairs={{0,16},{1,17},{2,18},{3,19},{4,20},{5,21},{6,22},{7,23},{8,24},{9,... | collective-permute-start | bytes 110600 | tf_op jit(solution)/shard_map/ppermute | solution.py:503
  225.7 83.9 %copy-start.3 = (f32[14,128,128]{2,1,0:T(8,128)S(1)}, f32[14,128,128]{2,1,0:T(8,128)}, u32[]{:S(2)}) copy-start(f32[14,128,128]{2,1,0:T(8,128)} %param.20) | copy-start | bytes 2752516
  304.3 12.2 %all-to-all-start = ((f32[32,1,128]{2,1,0:T(1,128)}), f32[32,1,128]{2,1,0:T(1,128)S(1)}, u32[]{:S(2)}, u32[]{:S(2)}) async-start(f32[32,1,128]{2,1,0:T(1,128)} %bitcast.13), calls=%async_computation.1 | async-start | bytes 32768 | tf_op jit(solution)/shard_map/all_to_all | solution.py:758
  320.7 3.9 %copy-start.4 = (f32[14,128,128]{2,1,0:T(8,128)}, f32[14,128,128]{2,1,0:T(8,128)S(1)}, u32[]{:S(2)}) copy-start(f32[14,128,128]{2,1,0:T(8,128)S(1)} %get-tuple-element.52) | copy-start | bytes 2752516
  320.7 3.9 %copy-start.5 = (f32[14,128,128]{2,1,0:T(8,128)}, f32[14,128,128]{2,1,0:T(8,128)S(1)}, u32[]{:S(2)}) copy-start(f32[14,128,128]{2,1,0:T(8,128)S(1)} %get-tuple-element.53) | copy-start | bytes 2752516
  320.7 1.8 copy-start.1
  322.5 2.0 copy-start.2
  322.5 2.0 copy-start.6
  322.5 2.0 copy-start.7
Sparse Core Ops, SparseCore 0:
  10.2 86.7 all-gather.1
  195.1 107.2 reduce-scatter.1

commit v8 on v7

--- a/solution.py
+++ b/solution.py
@@ -24,6 +24,7 @@
 wide = jnp.float32
 
 CHUNK = 1024
+PIECE = 256
 
 
 def ring_order(dp, fsdp):
@@ -366,7 +367,7 @@
     rows, width = middle.shape
     side = width // 128
     high = 4 * side
-    per = CHUNK // 128
+    per = PIECE // 128
     first_down = 4 * side * side + side * high
 
     def fetch(index, slot):
@@ -409,11 +410,14 @@
         start_blocks(
             place, whole, weight.at[part], sems.at[part], 0, 3 * side, 0, part * side, side, side
         )
-    for part in range(3):
+    grad_sum[...] = jnp.zeros_like(grad_sum)
+
+    def product(part, carry):
         await_bytes(weight.at[part], sems.at[part])
-    total = mm(grad_project[0], weight[0], 1, 1)
-    total = total + mm(grad_project[1], weight[1], 1, 1)
-    grad_sum[...] = total + mm(grad_project[2], weight[2], 1, 1)
+        grad_sum[...] += mm(grad_project[part], weight[part], 1, 1)
+        return carry
+
+    lax.fori_loop(0, 3, product, 0)
 
     def finish(t, carry):
         at = rows_of(t)
@@ -719,17 +723,17 @@
         result_kernel,
         grid_spec=pltpu.PrefetchScalarGridSpec(
             num_scalar_prefetch=1,
-            grid=(steps,),
+            grid=(hidden // PIECE,),
             in_specs=[
                 whole_spec(),
-                pl.BlockSpec((rows, CHUNK), lambda c, *_: (0, c)),
+                pl.BlockSpec((rows, PIECE), lambda c, *_: (0, c)),
                 full((rows, width)),
                 full((rows, 1)),
                 full((12, width)),
             ],
             out_specs=full((rows, width)),
             scratch_shapes=[
-                pltpu.VMEM((2, CHUNK, width), low),
+                pltpu.VMEM((2, PIECE, width), low),
                 pltpu.VMEM((rows, width), wide),
                 pltpu.SemaphoreType.DMA((2,)),
             ],

time: 334 us -> 334 us (level)
  Pallas kernels: 129 us -> 133 us
  waiting for transfers between devices: 155 us -> 151 us
    pallas_call x1, Pallas kernels: 11.4 us -> 15.5 us  [shards(): pl.pallas_call(result_kernel, grid_spec=pltpu.PrefetchScalarGridSpec(num_...]
    reduce_scatter x1, waiting for transfers between devices: 65.3 us -> 61.4 us  [scatter(): lax.psum_scatter(value, AXES, scatter_dimension=0, tiled=True, axis_index...]
  transfers between devices with their start and end apart: 8 -> 8, of which waited for: 7 -> 7; matrix products, arithmetic and copies ran while one was open for 3% -> 3% of each run, Pallas kernels for 9% -> 10%
where the time goes in v8:
time: 334 us; the launch traced here: 333 us
  waiting for transfers between devices  151 us (45%)
  Pallas kernels  133 us (40%)
  between operations  16.8 us (5%)
  starting transfers between devices  11 us (3%)
  other arithmetic  10.2 us (3%)
  matrix products  7.2 us (2%)
  local copies, waits for them, and re-layouts  3.65 us (1%)
    all_gather x1, waiting for transfers between devices, gather(): lax.all_gather(value, AXES, axis=0, tiled=True, axis_index_groups=groups)  74.6 us
    reduce_scatter x1, waiting for transfers between devices, scatter(): lax.psum_scatter(value, AXES, scatter_dimension=0, tiled=True, axis_index...  61.4 us
    pallas_call x1, Pallas kernels, shards(): pl.pallas_call(feed_kernel, grid_spec=pltpu.PrefetchScalarGridSpec(num_sc...  39.9 us
    pallas_call x1, Pallas kernels, shards(): pl.pallas_call(back_kernel, grid_spec=pltpu.PrefetchScalarGridSpec(num_sc...  30.5 us
    pallas_call x1, Pallas kernels, shards(): pl.pallas_call(attend_kernel, grid=(pairs,), in_specs=[column(0), column(...  18.7 us
    pallas_call x1, Pallas kernels, shards(): pl.pallas_call(result_kernel, grid_spec=pltpu.PrefetchScalarGridSpec(num_...  15.5 us
    pallas_call x1, Pallas kernels, shards(): pl.pallas_call(input_kernel, grid_spec=pltpu.PrefetchScalarGridSpec(num_s...  12.4 us
    ppermute x5, waiting for transfers between devices, everywhere(): lax.ppermute(value, AXES, [(d, d ^ step) for d in range(devices)])  10.7 us
  transfers between devices with their start and end apart: 8, of which 7 were waited for; matrix products, arithmetic and copies ran while one was open for 3% of the time, Pallas kernels for 10%

profile of v8, /device:TPU:0, one launch (start us, length us, event | category | flops | bytes accessed | tf_op | source)
XLA Modules:
  0.0 333.2 jit_solution(15003225440932974671)
XLA Ops:
  7.3 2.1 convert_element_type.21
  9.4 0.8 reduce-window.4
  10.8 0.8 slice.17
  12.3 1.4 fusion.16.inside
  13.7 5.4 %ready.1 = (bf16[784,768]{1,0:T(8,128)(2,1)}, bf16[768,784]{1,0:T(8,128)(2,1)}, bf16[784,768]{1,0:T(8,128)(2,1)}, f32[1,768]{1,0:T(1,128)}) custom-call(bf16[784,768]{1,0:T(8,128)(2,1)} %patches.5, bf16[784,768]{1,0:T(8,128)(2,1)} %cotangent.3, f32[784,1]{1,0:T(8,128)} %fusion.16.inside, f32[12,768]{1,0:T(8,128)} %vectors.9), custom_call_target="tpu_custom_call" | custom-call | tf_op jit(solution)/shard_map/ready/pallas_call | solution.py:542
  20.6 0.9 fusion.18.image_keys
  21.5 0.9 select_convert_fusion.image_query
  22.3 74.6 %all-gather.2.cloned.1.call-done.whole = bf16[448,128,128]{2,1,0:T(8,128)(2,1)} async-done(((bf16[14,128,128]{2,1,0:T(8,128)(2,1)}), bf16[448,128,128]{2,1,0:T(8,128)(2,1)}) %all-gather.2.cloned.1.call-update) | async-done | bytes 14680080 | tf_op jit(solution)/shard_map/all_gather | solution.py:497
  96.9 9.0 %qkv.1.query.keys.values = bf16[784,2304]{1,0:T(8,128)(2,1)} custom-call(s32[432]{0:T(512)} %fusion.21.place, bf16[448,128,128]{2,1,0:T(8,128)(2,1)} %all-gather.2.cloned.1.call-done.whole, bf16[784,768]{1,0:T(8,128)(2,1)} %get-tuple-element.30.normed, f32[12,768]{1,0:T(8,128)} %vectors.9), custom_call_target="tpu_custom_call" | custom-call | tf_op jit(solution)/shard_map/qkv/pallas_call | solution.py:554
  105.9 18.7 %attend.1 = (bf16[784,768]{1,0:T(8,128)(2,1)}, bf16[12,784,784]{2,1,0:T(8,128)(2,1)}) custom-call(bf16[784,2304]{1,0:T(8,128)(2,1)} %qkv.1.query.keys.values, bf16[784,2304]{1,0:T(8,128)(2,1)} %qkv.1.query.keys.values, bf16[784,2304]{1,0:T(8,128)(2,1)} %qkv.1.query.keys.values, bf16[784,128]{1,0:T(8,128)(2,1)} %select_convert_fusion.image_query, ...), custom_call_target="tpu_custom_call" | custom-call | tf_op jit(solution)/shard_map/attend/pallas_call | solution.py:574
  124.6 39.9 %feed.1 = (f32[784,768]{1,0:T(8,128)}, bf16[784,3072]{1,0:T(8,128)(2,1)}, f32[784,768]{1,0:T(8,128)}, bf16[784,768]{1,0:T(8,128)(2,1)}, f32[8,768]{1,0:T(8,128)}...) custom-call(s32[432]{0:T(512)} %fusion.21.place, bf16[448,128,128]{2,1,0:T(8,128)(2,1)} %all-gather.2.cloned.1.call-done.whole, ...), custom_call_target="tpu_custom_call" | custom-call | tf_op jit(solution)/shard_map/feed/pallas_call | solution.py:592
  164.6 30.5 %back.1 = (bf16[3,784,768]{2,1,0:T(8,128)(2,1)}, bf16[448,128,128]{2,1,0:T(8,128)(2,1)}) custom-call(s32[432]{0:T(512)} %fusion.21.place, bf16[448,128,128]{2,1,0:T(8,128)(2,1)} %get-tuple-element.32.held, bf16[784,2304]{1,0:T(8,128)(2,1)} %qkv.1.query.keys.values, bf16[784,2304]{1,0:T(8,128)(2,1)} %qkv.1.query.keys.values, ...), custom_call_target="tpu_custom_call", output_to_operand_aliasing={{1}: (1, {})} | custom-call | tf_op jit(solution)/shard_map/back/pallas_call | solution.py:657
  195.1 12.4 %input.1 = (bf16[784,768]{1,0:T(8,128)(2,1)}, f32[8,768]{1,0:T(8,128)}) custom-call(s32[432]{0:T(512)} %fusion.21.place, bf16[448,128,128]{2,1,0:T(8,128)(2,1)} %all-gather.2.cloned.1.call-done.whole, bf16[3,784,768]{2,1,0:T(8,128)(2,1)} %get-tuple-element.37.grad_project, bf16[784,768]{1,0:T(8,128)(2,1)} %patches.5, ...), custom_call_target="tpu_custom_call" | custom-call | tf_op jit(solution)/shard_map/input/pallas_call | solution.py:699
  207.5 0.7 slice.18
  208.7 1.0 collective-permute-done
  209.6 1.6 collective-permute-start.1
  211.2 3.3 collective-permute-done.1
  214.5 1.4 collective-permute-start.2
  215.9 2.7 collective-permute-done.2
  218.7 0.8 collective-permute-start.3
  219.5 3.7 %collective-permute-done.3 = f32[12,768]{1,0:T(8,128)S(1)} collective-permute-done((f32[12,768]{1,0:T(8,128)S(1)}, f32[12,768]{1,0:T(8,128)S(1)}, u32[]{:S(2)}, u32[]{:S(2)}) %collective-permute-start.3) | collective-permute-done | bytes 36896 | tf_op jit(solution)/shard_map/ppermute | solution.py:507
  223.2 1.5 collective-permute-start.4
  225.5 15.5 %result.1 = bf16[784,768]{1,0:T(8,128)(2,1)} custom-call(s32[432]{0:T(512)} %fusion.21.place, bf16[448,128,128]{2,1,0:T(8,128)(2,1)} %all-gather.2.cloned.1.call-done.whole, bf16[784,3072]{1,0:T(8,128)(2,1)} %get-tuple-element.43.active, f32[784,768]{1,0:T(8,128)} %get-tuple-element.44.middle, f32[784,1]{1,0:T(8,128)} %fusion.16.inside, f32[12,768]{1,0:T(8,128)} %vectors.9), custom_call_target="tpu_custom_call" | custom-call | tf_op jit(solution)/shard_map/result/pallas_call | solution.py:722
  241.0 61.4 %reduce-scatter.2.cloned.1.call-done.grads = bf16[14,128,128]{2,1,0:T(8,128)(2,1)} async-done(((bf16[448,128,128]{2,1,0:T(8,128)(2,1)}), bf16[14,128,128]{2,1,0:T(8,128)(2,1)}) %reduce-scatter.2.cloned.1.call-update) | async-done | bytes 458768 | tf_op jit(solution)/shard_map/reduce_scatter | solution.py:500
  302.5 1.9 squares.1
  304.3 5.3 %all-to-all-start = ((f32[32,1,128]{2,1,0:T(1,128)}), f32[32,1,128]{2,1,0:T(1,128)S(1)}, u32[]{:S(2)}, u32[]{:S(2)}) async-start(f32[32,1,128]{2,1,0:T(1,128)} %bitcast.13), calls=%async_computation.1 | async-start | bytes 32768 | tf_op jit(solution)/shard_map/all_to_all | solution.py:762
  309.6 1.9 fusion.9
  312.2 4.3 %all-to-all-done = f32[32,1,128]{2,1,0:T(1,128)S(1)} async-done(((f32[32,1,128]{2,1,0:T(1,128)}), f32[32,1,128]{2,1,0:T(1,128)S(1)}, u32[]{:S(2)}, u32[]{:S(2)}) %all-to-all-start) | async-done | bytes 16416 | tf_op jit(solution)/shard_map/all_to_all | solution.py:762
  318.4 2.2 multiply_add_fusion
  320.7 1.0 fusion.3
  321.7 0.8 copy-done.1
  322.5 2.0 fusion.1
  (54 shorter events, 5.9 us)
Async XLA Ops:
  7.2 311.2 %copy-start = (f32[14,128,128]{2,1,0:T(8,128)S(1)}, f32[14,128,128]{2,1,0:T(8,128)}, u32[]{:S(2)}) copy-start(f32[14,128,128]{2,1,0:T(8,128)} %param.21) | copy-start | bytes 2752516
  7.2 12.1 %copy-start.12 = (s32[32]{0:T(128)S(1)}, s32[32]{0:T(128)}, u32[]{:S(2)}) copy-start(s32[32]{0:T(128)} %constant.69.clone) | copy-start | bytes 388
  7.2 12.0 %copy-start.8 = (s32[432]{0:T(512)S(1)}, s32[432]{0:T(512)}, u32[]{:S(2)}) copy-start(s32[432]{0:T(512)} %param.16) | copy-start | bytes 5188
  7.2 89.7 %all-gather.2.cloned.1.call-start = ((), (), s32[]{:S(2)}) async-start(), calls=%async_computation.2 | async-start | bytes 15138816 | tf_op jit(solution)/shard_map/all_gather | solution.py:497
  9.4 293.1 %reduce-scatter.2.cloned.1.call-start = ((), (), s32[]{:S(2)}) async-start(), calls=%async_computation.3 | async-start | bytes 15138816 | tf_op jit(solution)/shard_map/reduce_scatter | solution.py:500
  195.1 13.2 %copy-start.9 = (f32[3,1,1024]{2,1,0:T(1,128)S(1)}, f32[3,1,1024]{2,1,0:T(1,128)}, u32[]{:S(2)}) copy-start(f32[3,1,1024]{2,1,0:T(1,128)} %get-tuple-element.41) | copy-start | bytes 36868
  195.1 13.2 %copy-start.11 = (f32[8,768]{1,0:T(8,128)S(1)}, f32[8,768]{1,0:T(8,128)}, u32[]{:S(2)}) copy-start(f32[8,768]{1,0:T(8,128)} %get-tuple-element.40) | copy-start | bytes 73732
  195.1 13.2 %copy-start.10 = (f32[1,768]{1,0:T(1,128)S(1)}, f32[1,768]{1,0:T(1,128)}, u32[]{:S(2)}) copy-start(f32[1,768]{1,0:T(1,128)} %get-tuple-element.42) | copy-start | bytes 9220
  208.3 1.3 collective-permute-start
  209.6 4.9 %collective-permute-start.1 = (f32[12,768]{1,0:T(8,128)S(1)}, f32[12,768]{1,0:T(8,128)S(1)}, u32[]{:S(2)}, u32[]{:S(2)}) collective-permute-start(f32[12,768]{1,0:T(8,128)S(1)} %fusion.26), channel_id=1, source_target_pairs={{0,2},{1,3},{2,0},{3,1},{4,6},{5,7},{6,4},{7,5},{8,10},{9,11},{10,... | collective-permute-start | bytes 110600 | tf_op jit(solution)/shard_map/ppermute | solution.py:507
  214.5 4.2 %collective-permute-start.2 = (f32[12,768]{1,0:T(8,128)S(1)}, f32[12,768]{1,0:T(8,128)S(1)}, u32[]{:S(2)}, u32[]{:S(2)}) collective-permute-start(f32[12,768]{1,0:T(8,128)S(1)} %add.73), channel_id=1, source_target_pairs={{0,4},{1,5},{2,6},{3,7},{4,0},{5,1},{6,2},{7,3},{8,12},{9,13},{10,... | collective-permute-start | bytes 110600 | tf_op jit(solution)/shard_map/ppermute | solution.py:507
  218.7 4.5 %collective-permute-start.3 = (f32[12,768]{1,0:T(8,128)S(1)}, f32[12,768]{1,0:T(8,128)S(1)}, u32[]{:S(2)}, u32[]{:S(2)}) collective-permute-start(f32[12,768]{1,0:T(8,128)S(1)} %add.74), channel_id=1, source_target_pairs={{0,8},{1,9},{2,10},{3,11},{4,12},{5,13},{6,14},{7,15},{8,0},{9,1},... | collective-permute-start | bytes 110600 | tf_op jit(solution)/shard_map/ppermute | solution.py:507
  223.2 17.8 %collective-permute-start.4 = (f32[12,768]{1,0:T(8,128)S(1)}, f32[12,768]{1,0:T(8,128)S(1)}, u32[]{:S(2)}, u32[]{:S(2)}) collective-permute-start(f32[12,768]{1,0:T(8,128)S(1)} %add.75), channel_id=1, source_target_pairs={{0,16},{1,17},{2,18},{3,19},{4,20},{5,21},{6,22},{7,23},{8,24},{9,... | collective-permute-start | bytes 110600 | tf_op jit(solution)/shard_map/ppermute | solution.py:507
  225.5 84.1 %copy-start.3 = (f32[14,128,128]{2,1,0:T(8,128)S(1)}, f32[14,128,128]{2,1,0:T(8,128)}, u32[]{:S(2)}) copy-start(f32[14,128,128]{2,1,0:T(8,128)} %param.20) | copy-start | bytes 2752516
  304.3 12.1 %all-to-all-start = ((f32[32,1,128]{2,1,0:T(1,128)}), f32[32,1,128]{2,1,0:T(1,128)S(1)}, u32[]{:S(2)}, u32[]{:S(2)}) async-start(f32[32,1,128]{2,1,0:T(1,128)} %bitcast.13), calls=%async_computation.1 | async-start | bytes 32768 | tf_op jit(solution)/shard_map/all_to_all | solution.py:762
  320.7 3.9 %copy-start.4 = (f32[14,128,128]{2,1,0:T(8,128)}, f32[14,128,128]{2,1,0:T(8,128)S(1)}, u32[]{:S(2)}) copy-start(f32[14,128,128]{2,1,0:T(8,128)S(1)} %get-tuple-element.52) | copy-start | bytes 2752516
  320.7 3.9 %copy-start.5 = (f32[14,128,128]{2,1,0:T(8,128)}, f32[14,128,128]{2,1,0:T(8,128)S(1)}, u32[]{:S(2)}) copy-start(f32[14,128,128]{2,1,0:T(8,128)S(1)} %get-tuple-element.53) | copy-start | bytes 2752516
  320.7 1.8 copy-start.1
  322.5 2.0 copy-start.2
  322.5 2.0 copy-start.6
  322.5 2.0 copy-start.7
Sparse Core Ops, SparseCore 0:
  10.2 86.7 all-gather.1
  195.2 107.2 reduce-scatter.1

commit v9 on v8

--- a/solution.py
+++ b/solution.py
@@ -206,7 +206,6 @@
     def _():
         start_blocks(place, whole, w_out, sems.at[4], first_out, side, 0, 0, side, side)
         fetch(0, 0)
-        fetch(1, 1)
         await_bytes(w_out, sems.at[4])
         out_sum[...] = mm(mixed[...], w_out[...], 1, 0)
 
@@ -224,6 +223,7 @@
         lax.fori_loop(0, tiles(rows), norm, 0)
         second_t[...] = second[...].T
         back_sum[...] = jnp.zeros_like(back_sum)
+        fetch(1, 1)
 
     slot = lax.rem(step, 2)
     await_bytes(w_up.at[slot], sems.at[slot])

time: 334 us -> 335 us (level)
  no operation moved by 1% of the time
where the time goes in v9:
time: 335 us; the launch traced here: 333 us
  waiting for transfers between devices  151 us (45%)
  Pallas kernels  134 us (40%)
  between operations  16.8 us (5%)
  starting transfers between devices  11 us (3%)
  other arithmetic  10.2 us (3%)
  matrix products  7.2 us (2%)
  local copies, waits for them, and re-layouts  3.64 us (1%)
    all_gather x1, waiting for transfers between devices, gather(): lax.all_gather(value, AXES, axis=0, tiled=True, axis_index_groups=groups)  74.6 us
    reduce_scatter x1, waiting for transfers between devices, scatter(): lax.psum_scatter(value, AXES, scatter_dimension=0, tiled=True, axis_index...  61.4 us
    pallas_call x1, Pallas kernels, shards(): pl.pallas_call(feed_kernel, grid_spec=pltpu.PrefetchScalarGridSpec(num_sc...  40.2 us
    pallas_call x1, Pallas kernels, shards(): pl.pallas_call(back_kernel, grid_spec=pltpu.PrefetchScalarGridSpec(num_sc...  30.4 us
    pallas_call x1, Pallas kernels, shards(): pl.pallas_call(attend_kernel, grid=(pairs,), in_specs=[column(0), column(...  18.7 us
    pallas_call x1, Pallas kernels, shards(): pl.pallas_call(result_kernel, grid_spec=pltpu.PrefetchScalarGridSpec(num_...  15.5 us
    pallas_call x1, Pallas kernels, shards(): pl.pallas_call(input_kernel, grid_spec=pltpu.PrefetchScalarGridSpec(num_s...  12.4 us
    ppermute x5, waiting for transfers between devices, everywhere(): lax.ppermute(value, AXES, [(d, d ^ step) for d in range(devices)])  10.7 us
  transfers between devices with their start and end apart: 8, of which 7 were waited for; matrix products, arithmetic and copies ran while one was open for 3% of the time, Pallas kernels for 10%

profile of v9, /device:TPU:0, one launch (start us, length us, event | category | flops | bytes accessed | tf_op | source)
XLA Modules:
  0.0 333.5 jit_solution(3638367016661536031)
XLA Ops:
  7.3 2.1 convert_element_type.21
  9.4 0.8 reduce-window.4
  10.8 0.8 slice.17
  12.3 1.4 fusion.16.inside
  13.7 5.4 %ready.1 = (bf16[784,768]{1,0:T(8,128)(2,1)}, bf16[768,784]{1,0:T(8,128)(2,1)}, bf16[784,768]{1,0:T(8,128)(2,1)}, f32[1,768]{1,0:T(1,128)}) custom-call(bf16[784,768]{1,0:T(8,128)(2,1)} %patches.5, bf16[784,768]{1,0:T(8,128)(2,1)} %cotangent.3, f32[784,1]{1,0:T(8,128)} %fusion.16.inside, f32[12,768]{1,0:T(8,128)} %vectors.9), custom_call_target="tpu_custom_call" | custom-call | tf_op jit(solution)/shard_map/ready/pallas_call | solution.py:542
  20.6 0.9 fusion.18.image_keys
  21.5 0.9 select_convert_fusion.image_query
  22.3 74.6 %all-gather.2.cloned.1.call-done.whole = bf16[448,128,128]{2,1,0:T(8,128)(2,1)} async-done(((bf16[14,128,128]{2,1,0:T(8,128)(2,1)}), bf16[448,128,128]{2,1,0:T(8,128)(2,1)}) %all-gather.2.cloned.1.call-update) | async-done | bytes 14680080 | tf_op jit(solution)/shard_map/all_gather | solution.py:497
  96.9 9.0 %qkv.1.query.keys.values = bf16[784,2304]{1,0:T(8,128)(2,1)} custom-call(s32[432]{0:T(512)} %fusion.21.place, bf16[448,128,128]{2,1,0:T(8,128)(2,1)} %all-gather.2.cloned.1.call-done.whole, bf16[784,768]{1,0:T(8,128)(2,1)} %get-tuple-element.30.normed, f32[12,768]{1,0:T(8,128)} %vectors.9), custom_call_target="tpu_custom_call" | custom-call | tf_op jit(solution)/shard_map/qkv/pallas_call | solution.py:554
  105.9 18.7 %attend.1 = (bf16[784,768]{1,0:T(8,128)(2,1)}, bf16[12,784,784]{2,1,0:T(8,128)(2,1)}) custom-call(bf16[784,2304]{1,0:T(8,128)(2,1)} %qkv.1.query.keys.values, bf16[784,2304]{1,0:T(8,128)(2,1)} %qkv.1.query.keys.values, bf16[784,2304]{1,0:T(8,128)(2,1)} %qkv.1.query.keys.values, bf16[784,128]{1,0:T(8,128)(2,1)} %select_convert_fusion.image_query, ...), custom_call_target="tpu_custom_call" | custom-call | tf_op jit(solution)/shard_map/attend/pallas_call | solution.py:574
  124.6 40.2 %feed.1 = (f32[784,768]{1,0:T(8,128)}, bf16[784,3072]{1,0:T(8,128)(2,1)}, f32[784,768]{1,0:T(8,128)}, bf16[784,768]{1,0:T(8,128)(2,1)}, f32[8,768]{1,0:T(8,128)}...) custom-call(s32[432]{0:T(512)} %fusion.21.place, bf16[448,128,128]{2,1,0:T(8,128)(2,1)} %all-gather.2.cloned.1.call-done.whole, ...), custom_call_target="tpu_custom_call" | custom-call | tf_op jit(solution)/shard_map/feed/pallas_call | solution.py:592
  164.8 30.4 %back.1 = (bf16[3,784,768]{2,1,0:T(8,128)(2,1)}, bf16[448,128,128]{2,1,0:T(8,128)(2,1)}) custom-call(s32[432]{0:T(512)} %fusion.21.place, bf16[448,128,128]{2,1,0:T(8,128)(2,1)} %get-tuple-element.32.held, bf16[784,2304]{1,0:T(8,128)(2,1)} %qkv.1.query.keys.values, bf16[784,2304]{1,0:T(8,128)(2,1)} %qkv.1.query.keys.values, ...), custom_call_target="tpu_custom_call", output_to_operand_aliasing={{1}: (1, {})} | custom-call | tf_op jit(solution)/shard_map/back/pallas_call | solution.py:657
  195.3 12.4 %input.1 = (bf16[784,768]{1,0:T(8,128)(2,1)}, f32[8,768]{1,0:T(8,128)}) custom-call(s32[432]{0:T(512)} %fusion.21.place, bf16[448,128,128]{2,1,0:T(8,128)(2,1)} %all-gather.2.cloned.1.call-done.whole, bf16[3,784,768]{2,1,0:T(8,128)(2,1)} %get-tuple-element.37.grad_project, bf16[784,768]{1,0:T(8,128)(2,1)} %patches.5, ...), custom_call_target="tpu_custom_call" | custom-call | tf_op jit(solution)/shard_map/input/pallas_call | solution.py:699
  207.7 0.7 slice.18
  208.9 1.0 collective-permute-done
  209.9 1.6 collective-permute-start.1
  211.5 3.3 collective-permute-done.1
  214.8 1.4 collective-permute-start.2
  216.2 2.7 collective-permute-done.2
  219.0 0.8 collective-permute-start.3
  219.8 3.7 %collective-permute-done.3 = f32[12,768]{1,0:T(8,128)S(1)} collective-permute-done((f32[12,768]{1,0:T(8,128)S(1)}, f32[12,768]{1,0:T(8,128)S(1)}, u32[]{:S(2)}, u32[]{:S(2)}) %collective-permute-start.3) | collective-permute-done | bytes 36896 | tf_op jit(solution)/shard_map/ppermute | solution.py:507
  223.5 1.5 collective-permute-start.4
  225.7 15.5 %result.1 = bf16[784,768]{1,0:T(8,128)(2,1)} custom-call(s32[432]{0:T(512)} %fusion.21.place, bf16[448,128,128]{2,1,0:T(8,128)(2,1)} %all-gather.2.cloned.1.call-done.whole, bf16[784,3072]{1,0:T(8,128)(2,1)} %get-tuple-element.43.active, f32[784,768]{1,0:T(8,128)} %get-tuple-element.44.middle, f32[784,1]{1,0:T(8,128)} %fusion.16.inside, f32[12,768]{1,0:T(8,128)} %vectors.9), custom_call_target="tpu_custom_call" | custom-call | tf_op jit(solution)/shard_map/result/pallas_call | solution.py:722
  241.3 61.4 %reduce-scatter.2.cloned.1.call-done.grads = bf16[14,128,128]{2,1,0:T(8,128)(2,1)} async-done(((bf16[448,128,128]{2,1,0:T(8,128)(2,1)}), bf16[14,128,128]{2,1,0:T(8,128)(2,1)}) %reduce-scatter.2.cloned.1.call-update) | async-done | bytes 458768 | tf_op jit(solution)/shard_map/reduce_scatter | solution.py:500
  302.7 1.9 squares.1
  304.6 5.3 %all-to-all-start = ((f32[32,1,128]{2,1,0:T(1,128)}), f32[32,1,128]{2,1,0:T(1,128)S(1)}, u32[]{:S(2)}, u32[]{:S(2)}) async-start(f32[32,1,128]{2,1,0:T(1,128)} %bitcast.13), calls=%async_computation.1 | async-start | bytes 32768 | tf_op jit(solution)/shard_map/all_to_all | solution.py:762
  309.9 1.9 fusion.9
  312.4 4.3 %all-to-all-done = f32[32,1,128]{2,1,0:T(1,128)S(1)} async-done(((f32[32,1,128]{2,1,0:T(1,128)}), f32[32,1,128]{2,1,0:T(1,128)S(1)}, u32[]{:S(2)}, u32[]{:S(2)}) %all-to-all-start) | async-done | bytes 16416 | tf_op jit(solution)/shard_map/all_to_all | solution.py:762
  318.7 2.2 multiply_add_fusion
  321.0 1.0 fusion.3
  322.0 0.8 copy-done.1
  322.8 2.0 fusion.1
  (54 shorter events, 5.9 us)
Async XLA Ops:
  7.2 311.5 %copy-start = (f32[14,128,128]{2,1,0:T(8,128)S(1)}, f32[14,128,128]{2,1,0:T(8,128)}, u32[]{:S(2)}) copy-start(f32[14,128,128]{2,1,0:T(8,128)} %param.21) | copy-start | bytes 2752516
  7.2 12.1 %copy-start.12 = (s32[32]{0:T(128)S(1)}, s32[32]{0:T(128)}, u32[]{:S(2)}) copy-start(s32[32]{0:T(128)} %constant.69.clone) | copy-start | bytes 388
  7.2 12.0 %copy-start.8 = (s32[432]{0:T(512)S(1)}, s32[432]{0:T(512)}, u32[]{:S(2)}) copy-start(s32[432]{0:T(512)} %param.16) | copy-start | bytes 5188
  7.2 89.7 %all-gather.2.cloned.1.call-start = ((), (), s32[]{:S(2)}) async-start(), calls=%async_computation.2 | async-start | bytes 15138816 | tf_op jit(solution)/shard_map/all_gather | solution.py:497
  9.4 293.3 %reduce-scatter.2.cloned.1.call-start = ((), (), s32[]{:S(2)}) async-start(), calls=%async_computation.3 | async-start | bytes 15138816 | tf_op jit(solution)/shard_map/reduce_scatter | solution.py:500
  195.3 13.2 %copy-start.9 = (f32[3,1,1024]{2,1,0:T(1,128)S(1)}, f32[3,1,1024]{2,1,0:T(1,128)}, u32[]{:S(2)}) copy-start(f32[3,1,1024]{2,1,0:T(1,128)} %get-tuple-element.41) | copy-start | bytes 36868
  195.3 13.2 %copy-start.11 = (f32[8,768]{1,0:T(8,128)S(1)}, f32[8,768]{1,0:T(8,128)}, u32[]{:S(2)}) copy-start(f32[8,768]{1,0:T(8,128)} %get-tuple-element.40) | copy-start | bytes 73732
  195.3 13.2 %copy-start.10 = (f32[1,768]{1,0:T(1,128)S(1)}, f32[1,768]{1,0:T(1,128)}, u32[]{:S(2)}) copy-start(f32[1,768]{1,0:T(1,128)} %get-tuple-element.42) | copy-start | bytes 9220
  208.6 1.3 collective-permute-start
  209.9 4.9 %collective-permute-start.1 = (f32[12,768]{1,0:T(8,128)S(1)}, f32[12,768]{1,0:T(8,128)S(1)}, u32[]{:S(2)}, u32[]{:S(2)}) collective-permute-start(f32[12,768]{1,0:T(8,128)S(1)} %fusion.26), channel_id=1, source_target_pairs={{0,2},{1,3},{2,0},{3,1},{4,6},{5,7},{6,4},{7,5},{8,10},{9,11},{10,... | collective-permute-start | bytes 110600 | tf_op jit(solution)/shard_map/ppermute | solution.py:507
  214.8 4.2 %collective-permute-start.2 = (f32[12,768]{1,0:T(8,128)S(1)}, f32[12,768]{1,0:T(8,128)S(1)}, u32[]{:S(2)}, u32[]{:S(2)}) collective-permute-start(f32[12,768]{1,0:T(8,128)S(1)} %add.73), channel_id=1, source_target_pairs={{0,4},{1,5},{2,6},{3,7},{4,0},{5,1},{6,2},{7,3},{8,12},{9,13},{10,... | collective-permute-start | bytes 110600 | tf_op jit(solution)/shard_map/ppermute | solution.py:507
  219.0 4.5 %collective-permute-start.3 = (f32[12,768]{1,0:T(8,128)S(1)}, f32[12,768]{1,0:T(8,128)S(1)}, u32[]{:S(2)}, u32[]{:S(2)}) collective-permute-start(f32[12,768]{1,0:T(8,128)S(1)} %add.74), channel_id=1, source_target_pairs={{0,8},{1,9},{2,10},{3,11},{4,12},{5,13},{6,14},{7,15},{8,0},{9,1},... | collective-permute-start | bytes 110600 | tf_op jit(solution)/shard_map/ppermute | solution.py:507
  223.5 17.8 %collective-permute-start.4 = (f32[12,768]{1,0:T(8,128)S(1)}, f32[12,768]{1,0:T(8,128)S(1)}, u32[]{:S(2)}, u32[]{:S(2)}) collective-permute-start(f32[12,768]{1,0:T(8,128)S(1)} %add.75), channel_id=1, source_target_pairs={{0,16},{1,17},{2,18},{3,19},{4,20},{5,21},{6,22},{7,23},{8,24},{9,... | collective-permute-start | bytes 110600 | tf_op jit(solution)/shard_map/ppermute | solution.py:507
  225.7 84.1 %copy-start.3 = (f32[14,128,128]{2,1,0:T(8,128)S(1)}, f32[14,128,128]{2,1,0:T(8,128)}, u32[]{:S(2)}) copy-start(f32[14,128,128]{2,1,0:T(8,128)} %param.20) | copy-start | bytes 2752516
  304.6 12.1 %all-to-all-start = ((f32[32,1,128]{2,1,0:T(1,128)}), f32[32,1,128]{2,1,0:T(1,128)S(1)}, u32[]{:S(2)}, u32[]{:S(2)}) async-start(f32[32,1,128]{2,1,0:T(1,128)} %bitcast.13), calls=%async_computation.1 | async-start | bytes 32768 | tf_op jit(solution)/shard_map/all_to_all | solution.py:762
  320.9 3.9 %copy-start.4 = (f32[14,128,128]{2,1,0:T(8,128)}, f32[14,128,128]{2,1,0:T(8,128)S(1)}, u32[]{:S(2)}) copy-start(f32[14,128,128]{2,1,0:T(8,128)S(1)} %get-tuple-element.52) | copy-start | bytes 2752516
  320.9 3.9 %copy-start.5 = (f32[14,128,128]{2,1,0:T(8,128)}, f32[14,128,128]{2,1,0:T(8,128)S(1)}, u32[]{:S(2)}) copy-start(f32[14,128,128]{2,1,0:T(8,128)S(1)} %get-tuple-element.53) | copy-start | bytes 2752516
  320.9 1.8 copy-start.1
  322.8 2.0 copy-start.2
  322.8 2.0 copy-start.6
  322.8 2.0 copy-start.7
Sparse Core Ops, SparseCore 0:
  10.2 86.7 all-gather.1
  195.4 107.2 reduce-scatter.1
